TPU v7x, 32 devices: a whole 2x2x4 slice. The times are simulated.
32 devices in a mesh: fsdp: 4 (over y, x), context: 4 (over z), tensor: 2 (over core).
Axes of the slice: x: 2, y: 2, z: 4, core: 2. Of those that a mesh axis runs over, the one named last changes fastest.
Arguments:
- tokens: bfloat16 [8192, 1536], P(('fsdp', 'context')), may hold values from -6 to 6
- block_order: int32 [4, 4], P('fsdp'), may hold values from 0 to 3, as said below
- norm_one: bfloat16 [1536], P(('fsdp', 'context')), may hold values from 0.5 to 1.5
- w_query: bfloat16 [1536, 1536], P(('fsdp', 'context'), 'tensor'), may hold values from -0.15625 to 0.15625
- b_query: bfloat16 [2, 768], P('tensor', ('fsdp', 'context')), may hold values from -3 to 3
- w_key: bfloat16 [1536, 256], P(('fsdp', 'context'), 'tensor'), may hold values from -0.15625 to 0.15625
- b_key: bfloat16 [2, 128], P('tensor', ('fsdp', 'context')), may hold values from -3 to 3
- w_value: bfloat16 [1536, 256], P(('fsdp', 'context'), 'tensor'), may hold values from -0.15625 to 0.15625
- b_value: bfloat16 [2, 128], P('tensor', ('fsdp', 'context')), may hold values from -3 to 3
- w_out: bfloat16 [1536, 1536], P('tensor', ('fsdp', 'context')), may hold values from -3 to 3
- norm_two: bfloat16 [1536], P(('fsdp', 'context')), may hold values from 0.099609375 to 1.8984375
- w_gate: bfloat16 [1536, 8960], P(('fsdp', 'context'), 'tensor'), may hold values from -0.15625 to 0.15625
- w_up: bfloat16 [1536, 8960], P(('fsdp', 'context'), 'tensor'), may hold values from -0.15625 to 0.15625
- w_down: bfloat16 [8960, 1536], P('tensor', ('fsdp', 'context')), may hold values from -0.25 to 0.25
- cotangent: bfloat16 [8192, 1536], P(('fsdp', 'context')), may hold values from -6 to 6
Outputs:
- result: bfloat16 [8192, 1536], P(('fsdp', 'context'))
- grad_tokens: bfloat16 [8192, 1536], P(('fsdp', 'context'))
- grad_norm_one: float32 [1536], P(('fsdp', 'context'))
- grad_w_query: float32 [1536, 1536], P(('fsdp', 'context'), 'tensor')
- grad_b_query: float32 [2, 768], P('tensor', ('fsdp', 'context'))
- grad_w_key: float32 [1536, 256], P(('fsdp', 'context'), 'tensor')
- grad_b_key: float32 [2, 128], P('tensor', ('fsdp', 'context'))
- grad_w_value: float32 [1536, 256], P(('fsdp', 'context'), 'tensor')
- grad_b_value: float32 [2, 128], P('tensor', ('fsdp', 'context'))
- grad_w_out: float32 [1536, 1536], P('tensor', ('fsdp', 'context'))
- grad_norm_two: float32 [1536], P(('fsdp', 'context'))
- grad_w_gate: float32 [1536, 8960], P(('fsdp', 'context'), 'tensor')
- grad_w_up: float32 [1536, 8960], P(('fsdp', 'context'), 'tensor')
- grad_w_down: float32 [8960, 1536], P('tensor', ('fsdp', 'context'))
Inputs may be any that keep to these rules, and one draw needn't show every extreme that they name: Each row of block_order is an ordering of the 4 token blocks 0 to 3 of a group, each once.
All inputs are finite; a program needn't handle non-finite values.
Results may differ from a plain program's by a relative error of at most 0.039.
Values may be sent and summed in bfloat16 or wider, within the bound.
No kernel may reach another device: no remote copies, remote signals or barrier semaphores. Data moves between devices by JAX's collectives and lax.ppermute only.
A program may use at most 256 MiB of HBM per device.

v0:
```python
import jax
import jax.numpy as jnp
from jax import lax
from jax.sharding import PartitionSpec as P

EPSILON = 1e-06
ROPE_BASE = 1000000.0
MASKED = -1e30


def tables(positions, head_width):
    ladder = jnp.arange(head_width // 2, dtype=jnp.float32)
    inverse = jnp.exp(-jnp.log(ROPE_BASE) * 2.0 * ladder / head_width)
    angles = positions.astype(jnp.float32)[:, None] * inverse[None, :]
    return (jnp.cos(angles), jnp.sin(angles))


def rotate(field, cosine, sine):
    middle = field.shape[-1] // 2
    first_half = field[..., :middle]
    second_half = field[..., middle:]
    cos_rows = cosine[:, None, :]
    sin_rows = sine[:, None, :]
    return jnp.concatenate(
        [
            first_half * cos_rows - second_half * sin_rows,
            second_half * cos_rows + first_half * sin_rows,
        ],
        axis=-1,
    )


def unrotate(gradient, cosine, sine):
    middle = gradient.shape[-1] // 2
    first_half = gradient[..., :middle]
    second_half = gradient[..., middle:]
    cos_rows = cosine[:, None, :]
    sin_rows = sine[:, None, :]
    return jnp.concatenate(
        [
            first_half * cos_rows + second_half * sin_rows,
            second_half * cos_rows - first_half * sin_rows,
        ],
        axis=-1,
    )


def locate(blocks, prompt_slots, block_rows):
    segment = jnp.where(blocks < prompt_slots, 0, blocks - prompt_slots + 1)
    anchor = jnp.where(blocks < prompt_slots, blocks * block_rows, prompt_slots * block_rows)
    return (segment, anchor)


def block_split(piece_rows):
    return (512, piece_rows // 512)


def back_dot(left_side, right_side):
    return lax.dot_general(
        left_side, right_side, (((0,), (0,)), ((), ())), preferred_element_type=jnp.float32
    )


def dot_tail(left_side, right_side):
    return lax.dot_general(
        left_side, right_side, (((1,), (1,)), ((), ())), preferred_element_type=jnp.float32
    )


def norm_back(grad_normed, rows_normed, inv_rms, gain):
    grad_rows = grad_normed * gain.astype(jnp.float32)
    return inv_rms * (
        grad_rows - rows_normed * jnp.mean(grad_rows * rows_normed, axis=-1, keepdims=True)
    )


def on_device(
    tokens,
    block_order,
    norm_one,
    w_query,
    b_query,
    w_key,
    b_key,
    w_value,
    b_value,
    w_out,
    norm_two,
    w_gate,
    w_up,
    w_down,
    cotangent,
):
    block_rows = tokens.shape[0]
    slot_count = lax.axis_size("context")
    prompt_slots = slot_count // 2
    my_slot = lax.axis_index("context")
    owners = block_order[0]
    my_block = jnp.sum(jnp.where(jnp.arange(slot_count) == my_slot, owners, 0))
    query_seg, query_anchor = locate(my_block, prompt_slots, block_rows)
    query_pos = query_anchor + jnp.arange(block_rows)
    attn_set = (
        lax.all_gather(norm_one, ("fsdp", "context"), axis=0, tiled=True),
        lax.all_gather(w_query, ("fsdp", "context"), axis=0, tiled=True),
        lax.all_gather(b_query, ("fsdp", "context"), axis=1, tiled=True),
        lax.all_gather(w_key, ("fsdp", "context"), axis=0, tiled=True),
        lax.all_gather(b_key, ("fsdp", "context"), axis=1, tiled=True),
        lax.all_gather(w_value, ("fsdp", "context"), axis=0, tiled=True),
        lax.all_gather(b_value, ("fsdp", "context"), axis=1, tiled=True),
        lax.all_gather(w_out, ("fsdp", "context"), axis=1, tiled=True),
    )
    mlp_set = (
        lax.all_gather(norm_two, ("fsdp", "context"), axis=0, tiled=True),
        lax.all_gather(w_gate, ("fsdp", "context"), axis=0, tiled=True),
        lax.all_gather(w_up, ("fsdp", "context"), axis=0, tiled=True),
        lax.all_gather(w_down, ("fsdp", "context"), axis=1, tiled=True),
    )
    gain_one, query_full, bias_query, key_full, bias_key, value_full, bias_value, out_full = (
        attn_set
    )
    gain_two, gate_full, up_full, down_full = mlp_set
    head_width = key_full.shape[1]
    head_group = query_full.shape[1] // head_width
    score_scale = head_width ** (-0.5)
    inputs = tokens.astype(jnp.float32)
    inv_one = lax.rsqrt(jnp.mean(inputs * inputs, axis=-1, keepdims=True) + EPSILON)
    rows_one = inputs * inv_one
    normed_one = (rows_one * gain_one.astype(jnp.float32)).astype(jnp.bfloat16)
    cosine, sine = tables(query_pos, head_width)
    query_lin = jnp.dot(
        normed_one, query_full, preferred_element_type=jnp.float32
    ) + bias_query.reshape(-1).astype(jnp.float32)
    key_lin = jnp.dot(normed_one, key_full, preferred_element_type=jnp.float32) + bias_key.reshape(
        -1
    ).astype(jnp.float32)
    value_lin = jnp.dot(
        normed_one, value_full, preferred_element_type=jnp.float32
    ) + bias_value.reshape(-1).astype(jnp.float32)
    queries = rotate(query_lin.reshape(block_rows, head_group, head_width), cosine, sine).astype(
        jnp.bfloat16
    )
    keys = (
        rotate(key_lin.reshape(block_rows, 1, head_width), cosine, sine)
        .reshape(block_rows, head_width)
        .astype(jnp.bfloat16)
    )
    values = value_lin.astype(jnp.bfloat16)

    def key_meta(piece_rows):
        key_index = jnp.arange(piece_rows)
        key_slot = key_index // block_rows
        key_block = jnp.sum(
            jnp.where(key_slot[:, None] == jnp.arange(slot_count)[None, :], owners[None, :], 0),
            axis=1,
        )
        key_seg, key_anchor = locate(key_block, prompt_slots, block_rows)
        return (key_anchor + key_index % block_rows, key_seg)

    def visible(key_pos, key_seg):
        return (key_pos[None, :] <= query_pos[:, None]) & (
            (key_seg[None, :] == 0) | (key_seg[None, :] == query_seg)
        )

    def keep_state(running):
        return running

    start_state = (
        jnp.full((head_group, block_rows), MASKED, jnp.float32),
        jnp.zeros((head_group, block_rows), jnp.float32),
        jnp.zeros((head_group, block_rows, head_width), jnp.float32),
    )
    running = start_state
    key_piece = lax.all_gather(keys, "context", axis=0, tiled=True)
    value_piece = lax.all_gather(values, "context", axis=0, tiled=True)
    piece_rows = key_piece.shape[0]
    block_size, block_count = block_split(piece_rows)
    key_pos, key_seg = key_meta(piece_rows)
    stacked = (
        key_piece.reshape(block_count, block_size, head_width),
        value_piece.reshape(block_count, block_size, head_width),
        key_pos.reshape(block_count, block_size),
        key_seg.reshape(block_count, block_size),
    )

    def per_block(state, current):
        key_blk, value_blk, pos_blk, seg_blk = current
        allowed = visible(pos_blk, seg_blk)

        def update_block(inner):
            run_peak, run_total, run_sum = inner
            scores = (
                jnp.einsum("qhd,kd->hqk", queries, key_blk, preferred_element_type=jnp.float32)
                * score_scale
            )
            scores = jnp.where(allowed[None], scores, MASKED)
            new_peak = jnp.maximum(run_peak, jnp.max(scores, axis=-1))
            shrink = jnp.exp(run_peak - new_peak)
            attn_probs = jnp.where(allowed[None], jnp.exp(scores - new_peak[..., None]), 0.0)
            new_total = run_total * shrink + jnp.sum(attn_probs, axis=-1)
            new_sum = run_sum * shrink[..., None] + jnp.einsum(
                "hqk,kd->hqd",
                attn_probs.astype(jnp.bfloat16),
                value_blk,
                preferred_element_type=jnp.float32,
            )
            return (new_peak, new_total, new_sum)

        return (lax.cond(jnp.any(allowed), update_block, keep_state, state), None)

    running, unused = lax.scan(per_block, running, stacked)
    run_peak, run_total, run_sum = running
    log_total = run_peak + jnp.log(run_total)
    attn_heads = run_sum / run_total[..., None]
    out_low = (
        attn_heads.transpose(1, 0, 2)
        .reshape(block_rows, head_group * head_width)
        .astype(jnp.bfloat16)
    )
    attn_total = lax.psum(
        jnp.dot(out_low, out_full, preferred_element_type=jnp.float32).astype(jnp.bfloat16),
        "tensor",
    ).astype(jnp.float32)
    hidden_one = inputs + attn_total
    inv_two = lax.rsqrt(jnp.mean(hidden_one * hidden_one, axis=-1, keepdims=True) + EPSILON)
    rows_two = hidden_one * inv_two
    normed_two = (rows_two * gain_two.astype(jnp.float32)).astype(jnp.bfloat16)
    gate_lin = jnp.dot(normed_two, gate_full, preferred_element_type=jnp.float32)
    up_lin = jnp.dot(normed_two, up_full, preferred_element_type=jnp.float32)
    sigmoid_gate = jax.nn.sigmoid(gate_lin)
    silu_gate = gate_lin * sigmoid_gate
    hidden_low = (silu_gate * up_lin).astype(jnp.bfloat16)
    mlp_total = lax.psum(
        jnp.dot(hidden_low, down_full, preferred_element_type=jnp.float32).astype(jnp.bfloat16),
        "tensor",
    ).astype(jnp.float32)
    result = (hidden_one + mlp_total).astype(jnp.bfloat16)
    gain_two, gate_full, up_full, down_full = (
        lax.all_gather(norm_two, ("fsdp", "context"), axis=0, tiled=True),
        lax.all_gather(w_gate, ("fsdp", "context"), axis=0, tiled=True),
        lax.all_gather(w_up, ("fsdp", "context"), axis=0, tiled=True),
        lax.all_gather(w_down, ("fsdp", "context"), axis=1, tiled=True),
    )
    gain_one, query_full, bias_query, key_full, bias_key, value_full, bias_value, out_full = (
        lax.all_gather(norm_one, ("fsdp", "context"), axis=0, tiled=True),
        lax.all_gather(w_query, ("fsdp", "context"), axis=0, tiled=True),
        lax.all_gather(b_query, ("fsdp", "context"), axis=1, tiled=True),
        lax.all_gather(w_key, ("fsdp", "context"), axis=0, tiled=True),
        lax.all_gather(b_key, ("fsdp", "context"), axis=1, tiled=True),
        lax.all_gather(w_value, ("fsdp", "context"), axis=0, tiled=True),
        lax.all_gather(b_value, ("fsdp", "context"), axis=1, tiled=True),
        lax.all_gather(w_out, ("fsdp", "context"), axis=1, tiled=True),
    )
    grad_down = back_dot(hidden_low, cotangent)
    grad_hidden = dot_tail(cotangent, down_full)
    grad_gate = (
        grad_hidden * up_lin * sigmoid_gate * (1.0 + gate_lin * (1.0 - sigmoid_gate))
    ).astype(jnp.bfloat16)
    grad_up = (grad_hidden * silu_gate).astype(jnp.bfloat16)
    grad_wgate = back_dot(normed_two, grad_gate)
    grad_wup = back_dot(normed_two, grad_up)
    grad_normed_two = lax.psum(
        (dot_tail(grad_gate, gate_full) + dot_tail(grad_up, up_full)).astype(jnp.bfloat16), "tensor"
    ).astype(jnp.float32)
    grad_gain_two = jnp.sum(grad_normed_two * rows_two, axis=0)
    grad_hidden_one = cotangent.astype(jnp.float32) + norm_back(
        grad_normed_two, rows_two, inv_two, gain_two
    )
    mlp_grads = (
        lax.psum_scatter(grad_gain_two, ("fsdp", "context"), scatter_dimension=0, tiled=True),
        lax.psum_scatter(grad_wgate, ("fsdp", "context"), scatter_dimension=0, tiled=True),
        lax.psum_scatter(grad_wup, ("fsdp", "context"), scatter_dimension=0, tiled=True),
        lax.psum_scatter(grad_down, ("fsdp", "context"), scatter_dimension=1, tiled=True),
    )
    grad_low = grad_hidden_one.astype(jnp.bfloat16)
    grad_wout = back_dot(out_low, grad_low)
    grad_heads = (
        dot_tail(grad_low, out_full)
        .astype(jnp.bfloat16)
        .reshape(block_rows, head_group, head_width)
    )
    delta_rows = jnp.einsum("qhd,hqd->hq", grad_heads.astype(jnp.float32), attn_heads)
    grad_query = jnp.zeros((block_rows, head_group, head_width), jnp.float32)
    key_piece = lax.all_gather(keys, "context", axis=0, tiled=True)
    value_piece = lax.all_gather(values, "context", axis=0, tiled=True)
    piece_rows = key_piece.shape[0]
    block_size, block_count = block_split(piece_rows)
    key_pos, key_seg = key_meta(piece_rows)
    stacked = (
        key_piece.reshape(block_count, block_size, head_width),
        value_piece.reshape(block_count, block_size, head_width),
        key_pos.reshape(block_count, block_size),
        key_seg.reshape(block_count, block_size),
    )

    def per_block(grad_in, current):
        key_blk, value_blk, pos_blk, seg_blk = current
        allowed = visible(pos_blk, seg_blk)

        def update_block(grad_now):
            scores = (
                jnp.einsum("qhd,kd->hqk", queries, key_blk, preferred_element_type=jnp.float32)
                * score_scale
            )
            attn_probs = jnp.where(allowed[None], jnp.exp(scores - log_total[..., None]), 0.0)
            grad_value_blk = jnp.einsum(
                "hqk,qhd->kd",
                attn_probs.astype(jnp.bfloat16),
                grad_heads,
                preferred_element_type=jnp.float32,
            )
            grad_probs = jnp.einsum(
                "qhd,kd->hqk", grad_heads, value_blk, preferred_element_type=jnp.float32
            )
            grad_scores = (attn_probs * (grad_probs - delta_rows[..., None])).astype(jnp.bfloat16)
            grad_next = grad_now + score_scale * jnp.einsum(
                "hqk,kd->qhd", grad_scores, key_blk, preferred_element_type=jnp.float32
            )
            grad_key_blk = score_scale * jnp.einsum(
                "hqk,qhd->kd", grad_scores, queries, preferred_element_type=jnp.float32
            )
            return (grad_next, grad_key_blk, grad_value_blk)

        def skip_block(grad_now):
            empty = jnp.zeros((block_size, head_width), jnp.float32)
            return (grad_now, empty, empty)

        grad_out, grad_key_blk, grad_value_blk = lax.cond(
            jnp.any(allowed), update_block, skip_block, grad_in
        )
        return (grad_out, (grad_key_blk, grad_value_blk))

    grad_query, (key_blocks, value_blocks) = lax.scan(per_block, grad_query, stacked)
    grad_keys = key_blocks.reshape(piece_rows, head_width)
    grad_values = value_blocks.reshape(piece_rows, head_width)
    grad_query, grad_keys, grad_values = (grad_query, grad_keys, grad_values)
    grad_key_own, grad_value_own = (
        lax.psum_scatter(
            grad_keys.astype(jnp.bfloat16), "context", scatter_dimension=0, tiled=True
        ).astype(jnp.float32),
        lax.psum_scatter(
            grad_values.astype(jnp.bfloat16), "context", scatter_dimension=0, tiled=True
        ).astype(jnp.float32),
    )
    grad_query_lin = (
        unrotate(grad_query, cosine, sine)
        .reshape(block_rows, head_group * head_width)
        .astype(jnp.bfloat16)
    )
    grad_key_lin = (
        unrotate(grad_key_own.reshape(block_rows, 1, head_width), cosine, sine)
        .reshape(block_rows, head_width)
        .astype(jnp.bfloat16)
    )
    grad_value_lin = grad_value_own.astype(jnp.bfloat16)
    grad_wquery = back_dot(normed_one, grad_query_lin)
    grad_bquery = jnp.sum(grad_query_lin.astype(jnp.float32), axis=0)[None, :]
    grad_wkey = back_dot(normed_one, grad_key_lin)
    grad_bkey = jnp.sum(grad_key_lin.astype(jnp.float32), axis=0)[None, :]
    grad_wvalue = back_dot(normed_one, grad_value_lin)
    grad_bvalue = jnp.sum(grad_value_lin.astype(jnp.float32), axis=0)[None, :]
    grad_normed_one = lax.psum(
        (
            dot_tail(grad_query_lin, query_full)
            + dot_tail(grad_key_lin, key_full)
            + dot_tail(grad_value_lin, value_full)
        ).astype(jnp.bfloat16),
        "tensor",
    ).astype(jnp.float32)
    grad_gain_one = jnp.sum(grad_normed_one * rows_one, axis=0)
    grad_inputs = grad_hidden_one + norm_back(grad_normed_one, rows_one, inv_one, gain_one)
    attn_grads = (
        lax.psum_scatter(grad_gain_one, ("fsdp", "context"), scatter_dimension=0, tiled=True),
        lax.psum_scatter(grad_wquery, ("fsdp", "context"), scatter_dimension=0, tiled=True),
        lax.psum_scatter(grad_bquery, ("fsdp", "context"), scatter_dimension=1, tiled=True),
        lax.psum_scatter(grad_wkey, ("fsdp", "context"), scatter_dimension=0, tiled=True),
        lax.psum_scatter(grad_bkey, ("fsdp", "context"), scatter_dimension=1, tiled=True),
        lax.psum_scatter(grad_wvalue, ("fsdp", "context"), scatter_dimension=0, tiled=True),
        lax.psum_scatter(grad_bvalue, ("fsdp", "context"), scatter_dimension=1, tiled=True),
        lax.psum_scatter(grad_wout, ("fsdp", "context"), scatter_dimension=1, tiled=True),
    )
    return (
        result,
        grad_inputs.astype(jnp.bfloat16),
        attn_grads[0],
        attn_grads[1],
        attn_grads[2],
        attn_grads[3],
        attn_grads[4],
        attn_grads[5],
        attn_grads[6],
        attn_grads[7],
        mlp_grads[0],
        mlp_grads[1],
        mlp_grads[2],
        mlp_grads[3],
    )


def solution(mesh):
    return jax.shard_map(
        on_device,
        mesh=mesh,
        in_specs=(
            P(("fsdp", "context"), None),
            P("fsdp", None),
            P(("fsdp", "context")),
            P(("fsdp", "context"), "tensor"),
            P("tensor", ("fsdp", "context")),
            P(("fsdp", "context"), "tensor"),
            P("tensor", ("fsdp", "context")),
            P(("fsdp", "context"), "tensor"),
            P("tensor", ("fsdp", "context")),
            P("tensor", ("fsdp", "context")),
            P(("fsdp", "context")),
            P(("fsdp", "context"), "tensor"),
            P(("fsdp", "context"), "tensor"),
            P("tensor", ("fsdp", "context")),
            P(("fsdp", "context"), None),
        ),
        out_specs=(
            P(("fsdp", "context"), None),
            P(("fsdp", "context"), None),
            P(("fsdp", "context")),
            P(("fsdp", "context"), "tensor"),
            P("tensor", ("fsdp", "context")),
            P(("fsdp", "context"), "tensor"),
            P("tensor", ("fsdp", "context")),
            P(("fsdp", "context"), "tensor"),
            P("tensor", ("fsdp", "context")),
            P("tensor", ("fsdp", "context")),
            P(("fsdp", "context")),
            P(("fsdp", "context"), "tensor"),
            P(("fsdp", "context"), "tensor"),
            P("tensor", ("fsdp", "context")),
        ),
        check_vma=False,
    )
```

profile of v0, /device:TPU:0, one launch (start us, length us, event | category | flops | bytes accessed | tf_op | source)
XLA Modules:
  0.0 2837.1 jit_solution(9027108855186490542)
XLA Ops:
  16.7 79.6 %all-reduce.10 = (bf16[1536]{0:T(1024)(128)(2,1)S(1)}, bf16[128]{0:T(256)(128)(2,1)S(1)}, bf16[768]{0:T(1024)(128)(2,1)}, bf16[128]{0:T(256)(128)(2,1)}, bf16[1536]{0:T(1024)(128)(2,1)}) all-reduce(bf16[1536]{0:T(1024)(128)(2,1)S(1)} %dynamic-update-slice, ...), channel_id=1, replica_groups=mesh['fsdp'=4,'context'=4,'tensor'=2] {'fsdp','context'}, use_global_device_ids=true, to_apply=%add | all-reduce | flops 4096 | bytes 16384
  98.2 42.3 %all_gather.54 = bf16[1536,128]{1,0:T(8,128)(2,1)S(1)} all-gather(bf16[96,128]{1,0:T(8,128)(2,1)} %param.28), channel_id=1, replica_groups=mesh['fsdp'=4,'context'=4,'tensor'=2] {'fsdp','context'}, dimensions={0}, use_global_device_ids=true | all-gather | bytes 417792 | tf_op jit(solution)/shard_map/all_gather | solution.py:106
  169.8 43.9 %all_gather.59 = bf16[1536,128]{1,0:T(8,128)(2,1)S(1)} all-gather(bf16[96,128]{1,0:T(8,128)(2,1)} %param.30), channel_id=1, replica_groups=mesh['fsdp'=4,'context'=4,'tensor'=2] {'fsdp','context'}, dimensions={0}, use_global_device_ids=true | all-gather | bytes 417792 | tf_op jit(solution)/shard_map/all_gather | solution.py:108
  215.0 15.8 all_gather.61
  244.7 21.1 while.33
  277.6 23.2 all-reduce.16.cloned.1.call-done
  304.7 163.5 %all-gather.11.cloned.1.call-done = bf16[1536,4480]{1,0:T(8,128)(2,1)} async-done(((bf16[96,4480]{1,0:T(8,128)(2,1)}), bf16[1536,4480]{1,0:T(8,128)(2,1)}) %all-gather.11.cloned.1.call-update) | async-done | bytes 13762576 | tf_op jit(solution)/shard_map/all_gather | solution.py:114
  481.8 150.7 %all-gather.13.cloned.1.call-done = bf16[1536,4480]{1,0:T(8,128)(2,1)} async-done(((bf16[96,4480]{1,0:T(8,128)(2,1)}), bf16[1536,4480]{1,0:T(8,128)(2,1)}) %all-gather.13.cloned.1.call-update) | async-done | bytes 13762576 | tf_op jit(solution)/shard_map/all_gather | solution.py:115
  645.8 151.2 %all-gather.15.cloned.1.call-done = bf16[4480,1536]{0,1:T(8,128)(2,1)} async-done(((bf16[4480,96]{0,1:T(8,128)(2,1)}), bf16[4480,1536]{0,1:T(8,128)(2,1)}) %all-gather.15.cloned.1.call-update) | async-done | bytes 13762576 | tf_op jit(solution)/shard_map/all_gather | solution.py:116
  796.9 21.8 multiply_convert_fusion
  842.3 18.7 all-reduce.18.cloned.1.call-done
  875.9 25.0 while.34
  939.4 16.5 reduce-scatter.17.cloned.1.call-done
  974.7 15.6 fusion.112
  1023.2 57.0 %reduce-scatter.33.cloned.1.call-done = f32[48,1]{1,0:T(8,128)} async-done(((f32[768,1]{1,0:T(8,128)}), f32[48,1]{1,0:T(8,128)}) %reduce-scatter.33.cloned.1.call-update) | async-done | bytes 208
  1081.7 24.0 all-reduce.20.cloned.1.call-done
  1108.1 77.5 %all-reduce.9 = (f32[1536]{0:T(1024)S(1)}, f32[1,128]{1,0:T(1,128)S(1)}, f32[1,128]{1,0:T(1,128)S(1)}, f32[1536]{0:T(1024)S(1)}) all-reduce(f32[1536]{0:T(1024)S(1)} %get-tuple-element.473, f32[1,128]{1,0:T(1,128)S(1)} %bitcast.183, ...), channel_id=5, replica_groups=mesh['fsdp'=4,'context'=4,'tensor'=2] {'fsdp','context'}, use_global_device_ids=true, to_apply=%region_25.26.clone | all-reduce | flops 3328 | bytes 26624
  1193.1 41.2 %reduce-scatter.21.cloned.1.call-done = f32[96,128]{1,0:T(8,128)} async-done(((f32[1536,128]{1,0:T(8,128)}), f32[96,128]{1,0:T(8,128)}) %reduce-scatter.21.cloned.1.call-update) | async-done | bytes 49168 | tf_op jit(solution)/shard_map/reduce_scatter | solution.py:375
  1234.3 126.6 %reduce-scatter.23.cloned.1.call-done = f32[96,128]{1,0:T(8,128)} async-done(((f32[1536,128]{1,0:T(8,128)}), f32[96,128]{1,0:T(8,128)}) %reduce-scatter.23.cloned.1.call-update) | async-done | bytes 49168 | tf_op jit(solution)/shard_map/reduce_scatter | solution.py:377
  1360.8 141.1 %reduce-scatter.19.cloned.1.call-done = f32[96,768]{1,0:T(8,128)} async-done(((f32[1536,768]{1,0:T(8,128)}), f32[96,768]{1,0:T(8,128)}) %reduce-scatter.19.cloned.1.call-update) | async-done | bytes 294928 | tf_op jit(solution)/shard_map/reduce_scatter | solution.py:373
  1501.9 142.2 %reduce-scatter.25.cloned.1.call-done = f32[768,96]{0,1:T(8,128)} async-done(((f32[768,1536]{0,1:T(8,128)}), f32[768,96]{0,1:T(8,128)}) %reduce-scatter.25.cloned.1.call-update) | async-done | bytes 294928 | tf_op jit(solution)/shard_map/reduce_scatter | solution.py:379
  1644.2 394.9 %reduce-scatter.27.cloned.1.call-done = f32[96,4480]{1,0:T(8,128)} async-done(((f32[1536,4480]{1,0:T(8,128)}), f32[96,4480]{1,0:T(8,128)}) %reduce-scatter.27.cloned.1.call-update) | async-done | bytes 1720336 | tf_op jit(solution)/shard_map/reduce_scatter | solution.py:270
  2039.1 396.0 %reduce-scatter.29.cloned.1.call-done = f32[96,4480]{1,0:T(8,128)} async-done(((f32[1536,4480]{1,0:T(8,128)}), f32[96,4480]{1,0:T(8,128)}) %reduce-scatter.29.cloned.1.call-update) | async-done | bytes 1720336 | tf_op jit(solution)/shard_map/reduce_scatter | solution.py:271
  2435.2 394.9 %reduce-scatter.31.cloned.1.call-done = f32[4480,96]{0,1:T(8,128)} async-done(((f32[4480,1536]{0,1:T(8,128)}), f32[4480,96]{0,1:T(8,128)}) %reduce-scatter.31.cloned.1.call-update) | async-done | bytes 1720336 | tf_op jit(solution)/shard_map/reduce_scatter | solution.py:272
  (276 shorter events, 303.3 us)
Async XLA Ops:
  7.2 137.2 %copy-start = (bf16[512,1536]{1,0:T(8,128)(2,1)S(1)}, bf16[512,1536]{1,0:T(8,128)(2,1)}, u32[]{:S(2)}) copy-start(bf16[512,1536]{1,0:T(8,128)(2,1)} %param.23) | copy-start | bytes 4718596
  7.2 224.8 %all-gather.7.cloned.1.call-start = ((), (), s32[]{:S(2)}) async-start(), calls=%async_computation.10 | async-start | bytes 2506752 | tf_op jit(solution)/shard_map/all_gather | solution.py:104
  7.9 263.4 %all-gather.9.cloned.1.call-start = ((), (), s32[]{:S(2)}) async-start(), calls=%async_computation.11 | async-start | bytes 2506752 | tf_op jit(solution)/shard_map/all_gather | solution.py:110
  8.7 292.2 %all-reduce.16.cloned.1.call-start = ((), (), s32[]{:S(2)}) async-start(), calls=%async_computation.12 | async-start | bytes 3145728 | tf_op jit(solution)/shard_map/psum | solution.py:219
  143.7 87.2 %copy-start.25 = (f32[512]{0:T(512)}, f32[512]{0:T(512)S(1)}, u32[]{:S(2)}) copy-start(f32[512]{0:T(512)S(1)} %add_convert_fusion.2) | copy-start | bytes 6148
  144.9 94.4 %copy-start.2 = (bf16[512,1536]{1,0:T(8,128)(2,1)}, bf16[512,1536]{1,0:T(8,128)(2,1)S(1)}, u32[]{:S(2)}) copy-start(bf16[512,1536]{1,0:T(8,128)(2,1)S(1)} %fusion.64) | copy-start | bytes 4718596
  275.8 192.4 %all-gather.11.cloned.1.call-start = ((), (), s32[]{:S(2)}) async-start(), calls=%async_computation.13 | async-start | bytes 14622720 | tf_op jit(solution)/shard_map/all_gather | solution.py:114
  276.4 356.2 %all-gather.13.cloned.1.call-start = ((), (), s32[]{:S(2)}) async-start(), calls=%async_computation.14 | async-start | bytes 14622720 | tf_op jit(solution)/shard_map/all_gather | solution.py:115
  277.0 520.0 %all-gather.15.cloned.1.call-start = ((), (), s32[]{:S(2)}) async-start(), calls=%async_computation.15 | async-start | bytes 14622720 | tf_op jit(solution)/shard_map/all_gather | solution.py:116
  277.6 583.5 %all-reduce.18.cloned.1.call-start = ((), (), s32[]{:S(2)}) async-start(), calls=%async_computation.16 | async-start | bytes 3145728 | tf_op jit(solution)/shard_map/psum | solution.py:261
  842.3 91.4 %reduce-scatter.15.cloned.1.call-start = ((), (), s32[]{:S(2)}) async-start(), calls=%async_computation.17 | async-start | bytes 655360 | tf_op jit(solution)/shard_map/reduce_scatter | solution.py:337
  903.0 52.9 %reduce-scatter.17.cloned.1.call-start = ((), (), s32[]{:S(2)}) async-start(), calls=%async_computation.18 | async-start | bytes 655360 | tf_op jit(solution)/shard_map/reduce_scatter | solution.py:340
  903.7 176.5 %reduce-scatter.33.cloned.1.call-start = ((), (), s32[]{:S(2)}) async-start(), calls=%async_computation.26 | async-start | bytes 417792
  919.0 186.6 %all-reduce.20.cloned.1.call-start = ((), (), s32[]{:S(2)}) async-start(), calls=%async_computation.27 | async-start | bytes 6291456 | tf_op jit(solution)/shard_map/psum | solution.py:232
  959.6 274.7 %reduce-scatter.21.cloned.1.call-start = ((), (), s32[]{:S(2)}) async-start(), calls=%async_computation.20 | async-start | bytes 835584 | tf_op jit(solution)/shard_map/reduce_scatter | solution.py:375
  961.2 399.7 %reduce-scatter.23.cloned.1.call-start = ((), (), s32[]{:S(2)}) async-start(), calls=%async_computation.21 | async-start | bytes 835584 | tf_op jit(solution)/shard_map/reduce_scatter | solution.py:377
  962.7 539.2 %reduce-scatter.19.cloned.1.call-start = ((), (), s32[]{:S(2)}) async-start(), calls=%async_computation.19 | async-start | bytes 5013504 | tf_op jit(solution)/shard_map/reduce_scatter | solution.py:373
  966.4 677.8 %reduce-scatter.25.cloned.1.call-start = ((), (), s32[]{:S(2)}) async-start(), calls=%async_computation.22 | async-start | bytes 5013504 | tf_op jit(solution)/shard_map/reduce_scatter | solution.py:379
  974.7 1064.4 %reduce-scatter.27.cloned.1.call-start = ((), (), s32[]{:S(2)}) async-start(), calls=%async_computation.23 | async-start | bytes 29245440 | tf_op jit(solution)/shard_map/reduce_scatter | solution.py:270
  990.4 1444.8 %reduce-scatter.29.cloned.1.call-start = ((), (), s32[]{:S(2)}) async-start(), calls=%async_computation.24 | async-start | bytes 29245440 | tf_op jit(solution)/shard_map/reduce_scatter | solution.py:271
  1006.2 1823.9 %reduce-scatter.31.cloned.1.call-start = ((), (), s32[]{:S(2)}) async-start(), calls=%async_computation.25 | async-start | bytes 29245440 | tf_op jit(solution)/shard_map/reduce_scatter | solution.py:272
  1021.9 83.8 %copy-start.24 = (f32[1536]{0:T(1024)S(1)}, f32[1536]{0:T(1024)}, u32[]{:S(2)}) copy-start(f32[1536]{0:T(1024)} %copy-done.23) | copy-start | bytes 18436
  1021.9 83.8 %copy-start.30 = (f32[512]{0:T(512)S(1)}, f32[512]{0:T(512)}, u32[]{:S(2)}) copy-start(f32[512]{0:T(512)} %copy-done.29) | copy-start | bytes 6148
  1021.9 86.3 %copy-start.27 = (f32[1536]{0:T(1024)S(1)}, f32[1536]{0:T(1024)}, u32[]{:S(2)}) copy-start(f32[1536]{0:T(1024)} %get-tuple-element.471) | copy-start | bytes 18436
  (32 other events, 343.8 us)
Sparse Core Ops, SparseCore 0:
  10.8 65.4 all-gather.6
  79.0 64.6 all-gather.8
  275.9 24.8 all-reduce.15
  303.8 164.3 all-gather.10
  471.2 161.3 all-gather.12
  635.6 161.3 all-gather.14
  842.4 18.5 all-reduce.17
  903.1 30.4 reduce-scatter.14
  935.9 19.9 reduce-scatter.16
  960.4 119.7 reduce-scatter.32
  1083.3 22.3 all-reduce.19
  1110.8 123.4 reduce-scatter.20
  1239.5 121.2 reduce-scatter.22
  1366.4 135.4 reduce-scatter.18
  1508.3 135.7 reduce-scatter.24
  1650.6 388.4 reduce-scatter.26
  2046.6 388.5 reduce-scatter.28
  2441.6 388.4 reduce-scatter.30
where the time goes:
time: 2840 us
  waiting for transfers between devices  2250 us (79%)
  blocking collectives  275 us (10%)
  matrix products  196 us (7%)
  other arithmetic  46.3 us (2%)
  local copies, waits for them, and re-layouts  37.9 us (1%)
    reduce_scatter x1, waiting for transfers between devices, on_device(): lax.psum_scatter(grad_wup, ('fsdp', 'context'), scatter_dimension=0, tile...  396 us
    reduce_scatter x1, waiting for transfers between devices, on_device(): lax.psum_scatter(grad_wgate, ('fsdp', 'context'), scatter_dimension=0, ti...  395 us
    reduce_scatter x1, waiting for transfers between devices, on_device(): lax.psum_scatter(grad_down, ('fsdp', 'context'), scatter_dimension=1, til...  395 us
    all_gather x1, waiting for transfers between devices, on_device(): lax.all_gather(w_gate, ('fsdp', 'context'), axis=0, tiled=True)  163 us
    unnamed x2, blocking collectives  157 us
    all_gather x1, waiting for transfers between devices, on_device(): lax.all_gather(w_down, ('fsdp', 'context'), axis=1, tiled=True)  151 us
    all_gather x1, waiting for transfers between devices, on_device(): lax.all_gather(w_up, ('fsdp', 'context'), axis=0, tiled=True)  151 us
    reduce_scatter x1, waiting for transfers between devices, on_device(): lax.psum_scatter(grad_wout, ('fsdp', 'context'), scatter_dimension=1, til...  142 us
  transfers between devices with their start and end apart: 18, of which 16 were waited for; matrix products, arithmetic and copies ran while one was open for 7% of the time, Pallas kernels for 0%

commit v1 on v0

v1 whole, which is shorter than its diff:
```python
import jax
import jax.numpy as jnp
from jax import lax
from jax.sharding import PartitionSpec as P

EPSILON = 1e-06
ROPE_BASE = 1000000.0
MASKED = -1e30
LANES = 128
BOTH = ("fsdp", "context")
BF = jnp.bfloat16
F32 = jnp.float32


def tables(positions, head_width):
    ladder = jnp.arange(head_width // 2, dtype=F32)
    inverse = jnp.exp(-jnp.log(ROPE_BASE) * 2.0 * ladder / head_width)
    angles = positions.astype(F32)[:, None] * inverse[None, :]
    return (jnp.cos(angles), jnp.sin(angles))


def rotate(field, cosine, sine):
    middle = field.shape[-1] // 2
    first_half = field[..., :middle]
    second_half = field[..., middle:]
    cos_rows = cosine[:, None, :]
    sin_rows = sine[:, None, :]
    return jnp.concatenate(
        [
            first_half * cos_rows - second_half * sin_rows,
            second_half * cos_rows + first_half * sin_rows,
        ],
        axis=-1,
    )


def unrotate(gradient, cosine, sine):
    return rotate(gradient, cosine, -sine)


def locate(blocks, prompt_slots, block_rows):
    segment = jnp.where(blocks < prompt_slots, 0, blocks - prompt_slots + 1)
    anchor = jnp.where(blocks < prompt_slots, blocks * block_rows, prompt_slots * block_rows)
    return (segment, anchor)


def dot_nn(left, right):
    return lax.dot_general(left, right, (((1,), (0,)), ((), ())), preferred_element_type=F32)


def dot_tn(left, right):
    return lax.dot_general(left, right, (((0,), (0,)), ((), ())), preferred_element_type=F32)


def dot_nt(left, right):
    return lax.dot_general(left, right, (((1,), (1,)), ((), ())), preferred_element_type=F32)


def norm_back(grad_normed, rows_normed, inv_rms, gain):
    grad_rows = grad_normed * gain.astype(F32)
    return inv_rms * (
        grad_rows - rows_normed * jnp.mean(grad_rows * rows_normed, axis=-1, keepdims=True)
    )


class Grid:
    def __init__(self):
        self.nf = lax.axis_size("fsdp")
        self.nc = lax.axis_size("context")
        self.n = self.nf * self.nc
        self.cbits = self.nc.bit_length() - 1
        self.fbits = self.nf.bit_length() - 1
        self.me = lax.axis_index("fsdp") * self.nc + lax.axis_index("context")
        self.my_slot = lax.axis_index("context")
        self.core = lax.axis_index("tensor")

    def bit(self, b):
        return (self.me >> b) & 1

    def xor(self, x, mask):
        return lax.ppermute(x, BOTH, [(i, i ^ mask) for i in range(self.n)])

    def swap(self, x):
        return lax.ppermute(x, "tensor", [(0, 1), (1, 0)])

    def pair(self, b, mine, theirs, axis):
        low = self.bit(b) == 0
        return jnp.stack([jnp.where(low, mine, theirs), jnp.where(low, theirs, mine)], axis)

    def ordered(self, pieces, bits):
        if len(bits) == 0:
            return pieces[0]
        half = len(pieces) // 2
        low = self.ordered(pieces[:half], bits[:-1])
        high = self.ordered(pieces[half:], bits[:-1])
        return self.pair(bits[-1], low, high, 0)

    def gather_all(self, x):
        rows, columns = x.shape
        pieces = [x] + [self.xor(x, r) for r in range(1, self.nc)]
        x = self.ordered(pieces, list(range(self.cbits))).reshape(self.nc * rows, columns)
        rows = self.nc * rows
        if self.fbits == 2:
            xm, ym = self.nc, 2 * self.nc
            gx, gy = self.xor(x, xm), self.xor(x, ym)
            cut = rows // 2
            diagonal = jnp.concatenate([self.xor(gx[:cut], ym), self.xor(gy[cut:], xm)], 0)
            pieces = [x, gx, gy, diagonal]
            x = self.ordered(pieces, [self.cbits, self.cbits + 1])
        else:
            pieces = [x] + [self.xor(x, r * self.nc) for r in range(1, self.nf)]
            x = self.ordered(pieces, [self.cbits + k for k in range(self.fbits)])
        return x.reshape(self.nf * rows, columns)

    def scatter_all(self, x):
        columns = x.shape[1]
        x = x.reshape(self.nf, -1, columns)
        rows = x.shape[1]
        mine = lax.axis_index("fsdp")
        take = lambda r: lax.dynamic_index_in_dim(x, mine ^ r, 0, keepdims=False)
        if self.fbits == 2:
            xm, ym = self.nc, 2 * self.nc
            cut = rows // 2
            far = take(3)
            by_y = self.xor(far[:cut].astype(BF), ym)
            by_x = self.xor(far[cut:].astype(BF), xm)
            px, py = take(1), take(2)
            px = jnp.concatenate([px[:cut].astype(F32) + by_y.astype(F32), px[cut:].astype(F32)], 0)
            py = jnp.concatenate([py[:cut].astype(F32), py[cut:].astype(F32) + by_x.astype(F32)], 0)
            rx = self.xor(px.astype(BF), xm)
            ry = self.xor(py.astype(BF), ym)
            x = take(0).astype(F32) + rx.astype(F32) + ry.astype(F32)
        else:
            parts = [self.xor(take(r).astype(BF), r * self.nc) for r in range(1, self.nf)]
            x = take(0).astype(F32)
            for part in parts:
                x = x + part.astype(F32)
        x = x.astype(BF).reshape(self.nc, -1, columns)
        pick = lambda r: lax.dynamic_index_in_dim(x, self.my_slot ^ r, 0, keepdims=False)
        parts = [self.xor(pick(r), r) for r in range(1, self.nc)]
        total = pick(0).astype(F32)
        for part in parts:
            total = total + part.astype(F32)
        return total

    def scatter_small(self, x):
        columns = x.shape[1]
        x = x.reshape(self.nf, self.nc, columns)
        mine = lax.axis_index("fsdp")
        take = lambda r: lax.dynamic_index_in_dim(x, mine ^ r, 0, keepdims=False)
        total = take(0)
        for part in [self.xor(take(r), r * self.nc) for r in range(1, self.nf)]:
            total = total + part
        pick = lambda r: lax.dynamic_index_in_dim(total, self.my_slot ^ r, 0, keepdims=True)
        final = pick(0)
        for part in [self.xor(pick(r), r) for r in range(1, self.nc)]:
            final = final + part
        return final

    def tokens_in(self, x):
        zm, xm = 1, self.nc
        cut = x.shape[0] // 2
        px, pz = self.xor(x, xm), self.xor(x, zm)
        far = jnp.concatenate([self.xor(px[:cut], zm), self.xor(pz[cut:], xm)], 0)
        pieces = []
        for piece in (x, px, pz, far):
            pieces += [piece, self.swap(piece)]
        return jnp.concatenate(pieces, 0)

    def tokens_out(self, part):
        zm, xm = 1, self.nc
        part = part.reshape(4, 2, part.shape[0] // 8, part.shape[1])
        cut = part.shape[2] // 2

        def joined(k):
            return part[k, 0].astype(F32) + self.swap(part[k, 1]).astype(F32)

        far, px, pz, own = joined(3), joined(1), joined(2), joined(0)
        by_z = self.xor(far[:cut].astype(BF), zm).astype(F32)
        by_x = self.xor(far[cut:].astype(BF), xm).astype(F32)
        px = jnp.concatenate([px[:cut] + by_z, px[cut:]], 0).astype(BF)
        pz = jnp.concatenate([pz[:cut], pz[cut:] + by_x], 0).astype(BF)
        return own + self.xor(px, xm).astype(F32) + self.xor(pz, zm).astype(F32)

    def quarter_masks(self):
        return (0, 1, self.nc, self.nc + 1)

    def my_quarter(self):
        return 2 * self.bit(self.cbits) + self.bit(0)

    def weights_in(self, stack):
        count, rows, width = stack.shape
        width = width // 4
        q = self.my_quarter()
        pieces = []
        for r, mask in enumerate(self.quarter_masks()):
            block = lax.dynamic_slice(stack, (0, 0, (q ^ r) * width), (count, rows, width))
            pieces.append(block if r == 0 else self.xor(block, mask))
        near = self.ordered(pieces, [0, self.cbits])
        near = near.reshape((2, 2) + near.shape[1:]) if near.ndim == 4 else near
        outs = []
        for k in range(count):
            w = near[:, :, k]
            held = [0, self.cbits]
            for b in list(range(1, self.cbits)) + list(range(self.cbits + 1, self.cbits + self.fbits)):
                axis = sum(1 for h in held if h > b)
                w = self.pair(b, w, self.xor(w, 1 << b), axis)
                held.append(b)
            outs.append(w.reshape(self.n * rows, width))
        return outs

    def weights_out(self, grad):
        width = grad.shape[1]
        held = sorted(range(self.cbits + self.fbits), reverse=True)
        g = grad.reshape((2,) * len(held) + (-1, width))
        for b in list(range(self.cbits + self.fbits - 1, self.cbits, -1)) + list(range(self.cbits - 1, 0, -1)):
            axis = held.index(b)
            give = lax.dynamic_index_in_dim(g, 1 - self.bit(b), axis, keepdims=False)
            keep = lax.dynamic_index_in_dim(g, self.bit(b), axis, keepdims=False)
            g = (keep.astype(F32) + self.xor(give, 1 << b).astype(F32)).astype(BF)
            held.remove(b)
        q = self.my_quarter()
        g = g.reshape(4, -1, width)
        pieces = []
        for r, mask in enumerate(self.quarter_masks()):
            block = lax.dynamic_index_in_dim(g, q ^ r, 0, keepdims=False)
            pieces.append(block if r == 0 else self.xor(block, mask))
        full = self.ordered(pieces, [0, self.cbits]).reshape(4, -1, width)
        return full.transpose(1, 0, 2).reshape(-1, 4 * width).astype(F32)


def on_device(
    tokens,
    block_order,
    norm_one,
    w_query,
    b_query,
    w_key,
    b_key,
    w_value,
    b_value,
    w_out,
    norm_two,
    w_gate,
    w_up,
    w_down,
    cotangent,
):
    grid = Grid()
    block_rows, width = tokens.shape
    shard = norm_one.shape[0]
    slot_count = grid.nc
    prompt_slots = slot_count // 2
    head_width = w_key.shape[1]
    query_width = w_query.shape[1]
    head_group = query_width // head_width
    score_scale = head_width ** (-0.5)
    cores = lax.axis_size("tensor")
    own_rows = block_rows // cores
    owners = block_order[0]
    my_block = lax.dynamic_index_in_dim(owners, grid.my_slot, 0, keepdims=False)
    query_anchor = locate(my_block, prompt_slots, block_rows)[1]
    query_pos = query_anchor + jnp.arange(block_rows)

    def own(x):
        return lax.dynamic_slice(x, (grid.core * own_rows, 0), (own_rows, x.shape[1]))

    def both(x):
        other = grid.swap(x)
        first = grid.core == 0
        return jnp.concatenate([jnp.where(first, x, other), jnp.where(first, other, x)], 0)

    def summed(part):
        give = lax.dynamic_slice(part, ((1 - grid.core) * own_rows, 0), (own_rows, width))
        return own(part) + grid.swap(give.astype(BF)).astype(F32)

    bias_shard = b_query.shape[1]
    small_bias = b_key.shape[1]
    vector = jnp.concatenate(
        [norm_one[None], norm_two[None], b_query, b_key, b_value], axis=1
    )
    vectors = grid.gather_all(vector) if False else gather_small(grid, vector)
    gain_one = vectors[:, :shard].reshape(-1)
    gain_two = vectors[:, shard : 2 * shard].reshape(-1)
    start = 2 * shard
    bias = jnp.concatenate(
        [
            vectors[:, start : start + bias_shard].reshape(-1),
            vectors[:, start + bias_shard : start + bias_shard + small_bias].reshape(-1),
            vectors[:, start + bias_shard + small_bias :].reshape(-1),
        ]
    ).astype(F32)

    w_qkv = grid.gather_all(jnp.concatenate([w_query, w_key, w_value], axis=1))
    w_out_t = grid.gather_all(w_out.T)
    hidden = w_gate.shape[1]
    quarter = -(-hidden // (4 * LANES)) * LANES
    pad = ((0, 0), (0, 4 * quarter - hidden))
    stack = jnp.stack([jnp.pad(w_gate, pad), jnp.pad(w_up, pad), jnp.pad(w_down.T, pad)])
    gate_full, up_full, down_full = grid.weights_in(stack)
    grads_in = grid.tokens_in(own(cotangent))

    inputs = tokens.astype(F32)
    inv_one = lax.rsqrt(jnp.mean(inputs * inputs, axis=-1, keepdims=True) + EPSILON)
    rows_one = inputs * inv_one
    normed_one = (rows_one * gain_one.astype(F32)).astype(BF)
    cosine, sine = tables(query_pos, head_width)
    qkv = dot_nn(normed_one, w_qkv) + bias
    queries = rotate(
        qkv[:, :query_width].reshape(block_rows, head_group, head_width), cosine, sine
    ).astype(BF)
    keys = (
        rotate(
            qkv[:, query_width : query_width + head_width].reshape(block_rows, 1, head_width),
            cosine,
            sine,
        )
        .reshape(block_rows, head_width)
        .astype(BF)
    )
    values = qkv[:, query_width + head_width :].astype(BF)
    pair = jnp.concatenate([keys, values], axis=1)
    pairs = [pair] + [grid.xor(pair, r) for r in range(1, slot_count)]
    stacked = jnp.stack(pairs)
    piece_block = owners[grid.my_slot ^ jnp.arange(slot_count)]
    seen = (piece_block < prompt_slots) & (piece_block < my_block)
    causal = jnp.arange(block_rows)[None, :] <= jnp.arange(block_rows)[:, None]

    def keep_state(running):
        return running

    def attend(state, current):
        piece, first, visible = current
        key_blk, value_blk = piece[:, :head_width], piece[:, head_width:]
        allowed = causal | jnp.logical_not(first)

        def update_block(inner):
            run_peak, run_total, run_sum = inner
            scores = (
                jnp.einsum("qhd,kd->hqk", queries, key_blk, preferred_element_type=F32)
                * score_scale
            )
            scores = jnp.where(allowed[None], scores, MASKED)
            new_peak = jnp.maximum(run_peak, jnp.max(scores, axis=-1))
            shrink = jnp.exp(run_peak - new_peak)
            attn_probs = jnp.exp(scores - new_peak[..., None])
            new_total = run_total * shrink + jnp.sum(attn_probs, axis=-1)
            new_sum = run_sum * shrink[..., None] + jnp.einsum(
                "hqk,kd->hqd", attn_probs.astype(BF), value_blk, preferred_element_type=F32
            )
            return (new_peak, new_total, new_sum)

        return (lax.cond(visible, update_block, keep_state, state), None)

    start_state = (
        jnp.full((head_group, block_rows), MASKED, F32),
        jnp.zeros((head_group, block_rows), F32),
        jnp.zeros((head_group, block_rows, head_width), F32),
    )
    is_first = jnp.arange(slot_count) == 0
    meta = (is_first, is_first | seen)
    running, unused = lax.scan(attend, start_state, (stacked,) + meta)
    run_peak, run_total, run_sum = running
    log_total = run_peak + jnp.log(run_total)
    attn_heads = run_sum / run_total[..., None]
    out_low = attn_heads.transpose(1, 0, 2).reshape(block_rows, query_width).astype(BF)
    hidden_one = own(tokens).astype(F32) + summed(dot_nt(out_low, w_out_t))

    inv_two = lax.rsqrt(jnp.mean(hidden_one * hidden_one, axis=-1, keepdims=True) + EPSILON)
    rows_two = hidden_one * inv_two
    normed_two = (rows_two * gain_two.astype(F32)).astype(BF)
    normed_in = grid.tokens_in(normed_two)
    gate_lin = dot_nn(normed_in, gate_full)
    up_lin = dot_nn(normed_in, up_full)
    sigmoid_gate = jax.nn.sigmoid(gate_lin)
    silu_gate = gate_lin * sigmoid_gate
    act = (silu_gate * up_lin).astype(BF)
    grad_act = dot_nn(grads_in, down_full)
    grad_gate = (
        grad_act * up_lin * sigmoid_gate * (1.0 + gate_lin * (1.0 - sigmoid_gate))
    ).astype(BF)
    grad_up = (grad_act * silu_gate).astype(BF)
    grad_normed_two = grid.tokens_out(
        (dot_nt(grad_gate, gate_full) + dot_nt(grad_up, up_full)).astype(BF)
    )
    grad_wdown = grid.weights_out(dot_tn(grads_in, act).astype(BF))
    grad_wgate = grid.weights_out(dot_tn(normed_in, grad_gate).astype(BF))
    grad_wup = grid.weights_out(dot_tn(normed_in, grad_up).astype(BF))
    mlp_total = grid.tokens_out(dot_nt(act, down_full).astype(BF))
    result = both((hidden_one + mlp_total).astype(BF))

    grad_gain_two = jnp.sum(grad_normed_two * rows_two, axis=0)
    grad_hidden_one = own(cotangent).astype(F32) + norm_back(
        grad_normed_two, rows_two, inv_two, gain_two
    )

    grad_low = both(grad_hidden_one.astype(BF))
    grad_wout = grid.scatter_all(dot_tn(grad_low, out_low).astype(BF))
    grad_heads = (
        dot_nn(grad_low, w_out_t).astype(BF).reshape(block_rows, head_group, head_width)
    )
    delta_rows = jnp.einsum("qhd,hqd->hq", grad_heads.astype(F32), attn_heads)

    def attend_back(grad_in, current):
        piece, first, visible = current
        key_blk, value_blk = piece[:, :head_width], piece[:, head_width:]
        allowed = causal | jnp.logical_not(first)

        def update_block(grad_now):
            scores = (
                jnp.einsum("qhd,kd->hqk", queries, key_blk, preferred_element_type=F32)
                * score_scale
            )
            attn_probs = jnp.where(allowed[None], jnp.exp(scores - log_total[..., None]), 0.0)
            grad_value_blk = jnp.einsum(
                "hqk,qhd->kd", attn_probs.astype(BF), grad_heads, preferred_element_type=F32
            )
            grad_probs = jnp.einsum(
                "qhd,kd->hqk", grad_heads, value_blk, preferred_element_type=F32
            )
            grad_scores = (attn_probs * (grad_probs - delta_rows[..., None])).astype(BF)
            grad_next = grad_now + score_scale * jnp.einsum(
                "hqk,kd->qhd", grad_scores, key_blk, preferred_element_type=F32
            )
            grad_key_blk = score_scale * jnp.einsum(
                "hqk,qhd->kd", grad_scores, queries, preferred_element_type=F32
            )
            return (grad_next, jnp.concatenate([grad_key_blk, grad_value_blk], axis=1).astype(BF))

        def skip_block(grad_now):
            return (grad_now, jnp.zeros((block_rows, 2 * head_width), BF))

        return lax.cond(visible, update_block, skip_block, grad_in)

    grad_query = jnp.zeros((block_rows, head_group, head_width), F32)
    grad_query, grad_pairs = lax.scan(attend_back, grad_query, (stacked,) + meta)
    grad_pair = grad_pairs[0].astype(F32)
    for r in range(1, slot_count):
        grad_pair = grad_pair + grid.xor(grad_pairs[r], r).astype(F32)
    grad_query_lin = unrotate(grad_query, cosine, sine).reshape(block_rows, query_width)
    grad_key_lin = unrotate(
        grad_pair[:, :head_width].reshape(block_rows, 1, head_width), cosine, sine
    ).reshape(block_rows, head_width)
    grad_qkv = jnp.concatenate(
        [grad_query_lin, grad_key_lin, grad_pair[:, head_width:]], axis=1
    ).astype(BF)
    grad_wqkv = grid.scatter_all(dot_tn(normed_one, grad_qkv).astype(BF))
    grad_bias = jnp.sum(grad_qkv.astype(F32), axis=0)
    grad_normed_one = summed(dot_nt(grad_qkv, w_qkv))
    rows_own = own(rows_one)
    inv_own = own(inv_one)
    grad_gain_one = jnp.sum(grad_normed_one * rows_own, axis=0)
    grad_inputs = grad_hidden_one + norm_back(grad_normed_one, rows_own, inv_own, gain_one)
    grad_tokens = both(grad_inputs.astype(BF))

    gains = jnp.concatenate(
        [grad_gain_one.reshape(-1, shard), grad_gain_two.reshape(-1, shard)], axis=1
    )
    gains = gains + grid.swap(gains)
    small = jnp.concatenate(
        [
            gains,
            grad_bias[:query_width].reshape(-1, bias_shard),
            grad_bias[query_width : query_width + head_width].reshape(-1, small_bias),
            grad_bias[query_width + head_width :].reshape(-1, small_bias),
        ],
        axis=1,
    )
    small = grid.scatter_small(small)
    return (
        result,
        grad_tokens,
        small[0, :shard],
        grad_wqkv[:, :query_width],
        small[:, start : start + bias_shard],
        grad_wqkv[:, query_width : query_width + head_width],
        small[:, start + bias_shard : start + bias_shard + small_bias],
        grad_wqkv[:, query_width + head_width :],
        small[:, start + bias_shard + small_bias :],
        grad_wout.T,
        small[0, shard : 2 * shard],
        grad_wgate[:, :hidden],
        grad_wup[:, :hidden],
        grad_wdown[:, :hidden].T,
    )


def gather_small(grid, x):
    pieces = [x] + [grid.xor(x, r) for r in range(1, grid.nc)]
    x = grid.ordered(pieces, list(range(grid.cbits))).reshape(grid.nc, -1)
    pieces = [x] + [grid.xor(x, r * grid.nc) for r in range(1, grid.nf)]
    x = grid.ordered(pieces, [grid.cbits + k for k in range(grid.fbits)])
    return x.reshape(grid.n, -1)


def solution(mesh):
    rows = P(("fsdp", "context"), None)
    split = P(("fsdp", "context"))
    into = P(("fsdp", "context"), "tensor")
    back = P("tensor", ("fsdp", "context"))
    return jax.shard_map(
        on_device,
        mesh=mesh,
        in_specs=(
            rows,
            P("fsdp", None),
            split,
            into,
            back,
            into,
            back,
            into,
            back,
            back,
            split,
            into,
            into,
            back,
            rows,
        ),
        out_specs=(
            rows,
            rows,
            split,
            into,
            back,
            into,
            back,
            into,
            back,
            back,
            split,
            into,
            into,
            back,
        ),
        check_vma=False,
    )
```

time: 2840 us -> 955 us (0.34)
  waiting for transfers between devices: 2250 us -> 480 us
  blocking collectives: 275 us -> 0 us
  starting transfers between devices: 1.3 us -> 129 us
  local copies, waits for them, and re-layouts: 37.9 us -> 87.9 us
  matrix products: 196 us -> 149 us
  other arithmetic: 46.3 us -> 86.4 us
    reduce_scatter x9 -> x0, waiting for transfers between devices: 1660 us -> none  [the longest x1 396 us: on_device(): lax.psum_scatter(grad_wup, ('fsdp', 'context'), scatter_dimension=0, tile...]
    ppermute x0 -> x108, waiting for transfers between devices: none -> 480 us  [the longest x86 480 us: xor(): return lax.ppermute(x, BOTH, [(i, i ^ mask) for i in range(self.n)])]
    all_gather x5 -> x0, waiting for transfers between devices: 465 us -> none  [the longest x1 163 us: on_device(): lax.all_gather(w_gate, ('fsdp', 'context'), axis=0, tiled=True)]
    unnamed x2 -> x0, blocking collectives: 157 us -> none
    ppermute x0 -> x108, starting transfers between devices: none -> 129 us  [the longest x86 126 us: xor(): return lax.ppermute(x, BOTH, [(i, i ^ mask) for i in range(self.n)])]
    all_gather x4 -> x0, blocking collectives: 118 us -> none  [the longest x1 43.9 us: on_device(): lax.all_gather(w_value, ('fsdp', 'context'), axis=0, tiled=True)]
    psum x3 -> x0, waiting for transfers between devices: 65.9 us -> none  [the longest x1 24 us: on_device(): lax.psum(jnp.dot(hidden_low, down_full, preferred_element_type=jnp.float3...]
    unnamed x19 -> x0, waiting for transfers between devices: 60.8 us -> none
  transfers between devices with their start and end apart: 18 -> 108, of which waited for: 16 -> 42; matrix products, arithmetic and copies ran while one was open for 7% -> 23% of each run, Pallas kernels for 0% -> 0%
where the time goes in v1:
time: 955 us; the launch traced here: 945 us
  waiting for transfers between devices  480 us (50%)
  matrix products  149 us (16%)
  starting transfers between devices  129 us (14%)
  local copies, waits for them, and re-layouts  87.9 us (9%)
  other arithmetic  86.4 us (9%)
    ppermute x86, waiting for transfers between devices, xor(): return lax.ppermute(x, BOTH, [(i, i ^ mask) for i in range(self.n)])  480 us
    ppermute x86, starting transfers between devices, xor(): return lax.ppermute(x, BOTH, [(i, i ^ mask) for i in range(self.n)])  126 us
    dot_general x5, matrix products, dot_nn(): lax.dot_general(left, right, (((1,), (0,)), ((), ())), preferred_element_...  45.6 us
    dot_general x5, matrix products, dot_tn(): lax.dot_general(left, right, (((0,), (0,)), ((), ())), preferred_element_...  39.3 us
    dot_general x5, matrix products, dot_nt(): lax.dot_general(left, right, (((1,), (1,)), ((), ())), preferred_element_...  38.2 us
    unnamed x203, local copies, waits for them, and re-layouts  26.8 us
    another operation x40, other arithmetic, pair(): jnp.stack([jnp.where(low, mine, theirs), jnp.where(low, theirs, mine)], a...  21.8 us
  transfers between devices with their start and end apart: 108, of which 42 were waited for; matrix products, arithmetic and copies ran while one was open for 23% of the time, Pallas kernels for 0%

profile of v1, /device:TPU:0, one launch (start us, length us, event | category | flops | bytes accessed | tf_op | source)
XLA Modules:
  0.0 945.3 jit_solution(3437582617222938682)
XLA Ops:
  92.8 18.1 %collective-permute-done.9 = bf16[384,1024]{1,0:T(8,128)(2,1)S(1)} collective-permute-done((bf16[384,1024]{1,0:T(8,128)(2,1)S(1)}, bf16[384,1024]{1,0:T(8,128)(2,1)S(1)}, u32[]{:S(2)}, u32[]{:S(2)}) %collective-permute-start.9) | collective-permute-done | bytes 786464 | tf_op jit(solution)/shard_map/ppermute | solution.py:81
  114.1 17.4 %collective-permute-done.22 = bf16[192,768]{1,0:T(8,128)(2,1)S(1)} collective-permute-done((bf16[192,768]{1,0:T(8,128)(2,1)S(1)}, bf16[192,768]{1,0:T(8,128)(2,1)S(1)}, u32[]{:S(2)}, u32[]{:S(2)}) %collective-permute-start.22) | collective-permute-done | bytes 294944 | tf_op jit(solution)/shard_map/ppermute | solution.py:81
  180.2 46.4 %collective-permute-done.14 = bf16[512,256]{0,1:T(8,128)(2,1)S(1)} collective-permute-done((bf16[512,256]{0,1:T(8,128)(2,1)S(1)}, bf16[512,256]{0,1:T(8,128)(2,1)S(1)}, u32[]{:S(2)}, u32[]{:S(2)}) %collective-permute-start.14) | collective-permute-done | bytes 262176 | tf_op jit(solution)/shard_map/ppermute | solution.py:81
  230.4 20.9 %while.31 = (s32[]{:T(128)}, f32[6,512]{1,0:T(8,128)S(1)}, f32[6,512]{1,0:T(8,128)S(1)}, f32[6,512,128]{2,1,0:T(8,128)}, pred[4]{0:T(512)(128)(4,1)S(1)}, /*inde...) while((s32[]{:T(128)}, f32[6,512]{1,0:T(8,128)S(1)}, ...), condition=%wide.region_6.7_spmd.clone, body=%wide.region_1.6_spmd.clone.sunk | while | flops 823924736 | bytes 41623880 | solution.py:362
  258.4 30.5 %collective-permute-done.37 = bf16[2,2,96,1152]{3,2,1,0:T(8,128)(2,1)} collective-permute-done((bf16[2,2,96,1152]{3,2,1,0:T(8,128)(2,1)}, bf16[2,2,96,1152]{3,2,1,0:T(8,128)(2,1)}, u32[]{:S(2)}, u32[]{:S(2)}) %collective-permute-start.37) | collective-permute-done | bytes 884768 | tf_op jit(solution)/shard_map/ppermute | solution.py:81
  299.6 13.5 %collective-permute-done.25 = bf16[256,1536]{1,0:T(8,128)(2,1)S(1)} collective-permute-done((bf16[256,1536]{1,0:T(8,128)(2,1)S(1)}, bf16[256,1536]{1,0:T(8,128)(2,1)S(1)}, u32[]{:S(2)}, u32[]{:S(2)}) %collective-permute-start.25) | collective-permute-done | bytes 786464 | tf_op jit(solution)/shard_map/ppermute | solution.py:81
  332.6 37.5 %collective-permute-done.36 = bf16[2,2,2,96,1152]{4,3,2,1,0:T(8,128)(2,1)S(1)} collective-permute-done((bf16[2,2,2,96,1152]{4,3,2,1,0:T(8,128)(2,1)S(1)}, bf16[2,2,2,96,1152]{4,3,2,1,0:T(8,128)(2,1)S(1)}, u32[]{:S(2)}, u32[]{:S(2)}) %collective-permute-start.36) | collective-permute-done | bytes 1769504 | tf_op jit(solution)/shard_map/ppermute | solution.py:81
  370.2 36.8 %collective-permute-done.40 = bf16[2,2,2,96,1152]{4,3,2,1,0:T(8,128)(2,1)S(1)} collective-permute-done((bf16[2,2,2,96,1152]{4,3,2,1,0:T(8,128)(2,1)S(1)}, bf16[2,2,2,96,1152]{4,3,2,1,0:T(8,128)(2,1)S(1)}, u32[]{:S(2)}, u32[]{:S(2)}) %collective-permute-start.40) | collective-permute-done | bytes 1769504 | tf_op jit(solution)/shard_map/ppermute | solution.py:81
  411.7 10.7 %fusion.137 = f32[2048,1152]{1,0:T(8,128)} fusion(bf16[2048,1536]{1,0:T(8,128)(2,1)S(1)} %constant_dynamic-update-slice_fusion.8, bf16[1536,1152]{1,0:T(8,128)(2,1)S(1)} %bitcast.551), kind=kOutput, calls=%fused_computation.471 | convolution fusion | flops 7247757312 | bytes 19267584 | tf_op jit(solution)/shard_map/dot_general | solution.py:48
  422.4 10.7 %fusion.136 = f32[2048,1152]{1,0:T(8,128)} fusion(bf16[2048,1536]{1,0:T(8,128)(2,1)S(1)} %constant_dynamic-update-slice_fusion.8, bf16[1536,1152]{1,0:T(8,128)(2,1)S(1)} %bitcast.555), kind=kOutput, calls=%fused_computation.470 | convolution fusion | flops 7247757312 | bytes 19267584 | tf_op jit(solution)/shard_map/dot_general | solution.py:48
  433.1 20.9 %multiply_convert_fusion = (bf16[2048,1152]{1,0:T(8,128)(2,1)}, bf16[2048,1152]{1,0:T(8,128)(2,1)}, bf16[2048,1152]{1,0:T(8,128)(2,1)}) fusion(f32[2048,1152]{1,0:T(8,128)} %fusion.136, f32[2048,1152]{1,0:T(8,128)} %fusion.137, bf16[2048,1536]{1,0:T(8,128)(2,1)} %constant_dynamic-update-slice_fusion.17, bf16[1536,1152]{1,0:T(8,128)(2,1)} %bitcast.553), kind=kOutput, calls=%fused_computation.51 | convolution fusion | flops 7283146752 | bytes 42860544 | tf_op jit(solution)/shard_map/dot_general | solution.py:48
  453.9 12.2 %convolution_convert_fusion = bf16[1536,1152]{1,0:T(8,128)(2,1)S(1)} fusion(bf16[2048,1536]{1,0:T(8,128)(2,1)} %constant_dynamic-update-slice_fusion.17, bf16[2048,1152]{1,0:T(8,128)(2,1)} %get-tuple-element.423), kind=kOutput, calls=%fused_computation.56 | convolution fusion | flops 7249526784 | bytes 14548992 | tf_op jit(solution)/shard_map/dot_general | solution.py:52
  475.3 14.6 %convolution_convert_fusion.2 = bf16[1536,1152]{1,0:T(8,128)(2,1)} fusion(bf16[2048,1536]{1,0:T(8,128)(2,1)S(1)} %bitcast.608, bf16[2048,1152]{1,0:T(8,128)(2,1)} %get-tuple-element.422), kind=kOutput, calls=%fused_computation.58 | convolution fusion | flops 7249526784 | bytes 14548992 | tf_op jit(solution)/shard_map/dot_general | solution.py:52
  490.0 13.2 %fusion.138 = f32[2048,1536]{1,0:T(8,128)} fusion(bf16[2048,1152]{1,0:T(8,128)(2,1)} %get-tuple-element.422, bf16[1536,1152]{1,0:T(8,128)(2,1)S(1)} %bitcast.556), kind=kOutput, calls=%fused_computation.472 | convolution fusion | flops 7247757312 | bytes 20840448 | tf_op jit(solution)/shard_map/dot_general | solution.py:56
  519.2 12.6 %add_convert_fusion = bf16[2048,1536]{1,0:T(8,128)(2,1)S(1)} fusion(f32[2048,1536]{1,0:T(8,128)} %fusion.138, bf16[2048,1152]{1,0:T(8,128)(2,1)} %get-tuple-element.421, bf16[1536,1152]{1,0:T(8,128)(2,1)S(1)} %bitcast.552), kind=kOutput, calls=%fused_computation.50 | convolution fusion | flops 7254048768 | bytes 27131904 | tf_op jit(solution)/shard_map/dot_general | solution.py:56
  550.9 10.8 %collective-permute-done.47 = bf16[128,1536]{1,0:T(8,128)(2,1)S(1)} collective-permute-done((bf16[128,1536]{1,0:T(8,128)(2,1)S(1)}, bf16[128,1536]{1,0:T(8,128)(2,1)S(1)}, u32[]{:S(2)}, u32[]{:S(2)}) %collective-permute-start.47) | collective-permute-done | bytes 393248 | tf_op jit(solution)/shard_map/ppermute | solution.py:81
  589.7 30.4 %collective-permute-done.93 = bf16[2,2,2,96,1152]{4,3,2,1,0:T(8,128)(2,1)S(1)} collective-permute-done((bf16[2,2,2,96,1152]{4,3,2,1,0:T(8,128)(2,1)S(1)}, bf16[2,2,2,96,1152]{4,3,2,1,0:T(8,128)(2,1)S(1)}, u32[]{:S(2)}, u32[]{:S(2)}) %collective-permute-start.93) | collective-permute-done | bytes 1769504 | tf_op jit(solution)/shard_map/ppermute | solution.py:81
  625.1 35.9 %collective-permute-done.65 = bf16[256,1536]{1,0:T(8,128)(2,1)S(1)} collective-permute-done((bf16[256,1536]{1,0:T(8,128)(2,1)S(1)}, bf16[256,1536]{1,0:T(8,128)(2,1)S(1)}, u32[]{:S(2)}, u32[]{:S(2)}) %collective-permute-start.65) | collective-permute-done | bytes 786464 | tf_op jit(solution)/shard_map/ppermute | solution.py:81
  664.8 11.2 %collective-permute-done.48 = bf16[256,1536]{1,0:T(8,128)(2,1)S(1)} collective-permute-done((bf16[256,1536]{1,0:T(8,128)(2,1)S(1)}, bf16[256,1536]{1,0:T(8,128)(2,1)S(1)}, u32[]{:S(2)}, u32[]{:S(2)}) %collective-permute-start.48) | collective-permute-done | bytes 786464 | tf_op jit(solution)/shard_map/ppermute | solution.py:81
  683.5 47.3 %collective-permute-done.99 = bf16[2,2,96,1152]{3,2,1,0:T(8,128)(2,1)} collective-permute-done((bf16[2,2,96,1152]{3,2,1,0:T(8,128)(2,1)}, bf16[2,2,96,1152]{3,2,1,0:T(8,128)(2,1)}, u32[]{:S(2)}, u32[]{:S(2)}) %collective-permute-start.99) | collective-permute-done | bytes 884768 | tf_op jit(solution)/shard_map/ppermute | solution.py:81
  737.7 12.0 %collective-permute-done.94 = bf16[2,2,96,1152]{3,2,1,0:T(8,128)(2,1)} collective-permute-done((bf16[2,2,96,1152]{3,2,1,0:T(8,128)(2,1)}, bf16[2,2,96,1152]{3,2,1,0:T(8,128)(2,1)}, u32[]{:S(2)}, u32[]{:S(2)}) %collective-permute-start.94) | collective-permute-done | bytes 884768 | tf_op jit(solution)/shard_map/ppermute | solution.py:81
  766.5 33.0 %while.32 = (s32[]{:T(128)}, f32[512,6,128]{2,0,1:T(8,128)}, bf16[4,512,256]{1,2,0:T(8,128)(2,1)}, pred[4]{0:T(512)(128)(4,1)S(1)}, bf16[4,512,256]{2,1,0:T(8,12...) while((s32[]{:T(128)}, f32[512,6,128]{2,0,1:T(8,128)}, ...), condition=%wide.region_12.13_spmd.clone, body=%wide.region_9.12_spmd.clone.sunk | while | flops 2031026176 | bytes 45003568 | solution.py:436
  767.9 12.0 %conditional.7 = (f32[512,6,128]{2,0,1:T(8,128)}, bf16[1,512,256]{1,2,0:T(8,128)(2,1)S(1)}) conditional(s32[]{:T(128)} %bitcast.541, f32[512,6,128]{2,0,1:T(8,128)} %get-tuple-element.743, (s32[4]{0:T(128)S(1)}, s32[]{:T(128)}, s32[512,512]{0,1:T(8,128)S(1)}, bf16[4,512,256]{2,1,0:T(8,128)(2,1)}, bf16[512,6,128]{0,2,1:T(8,128)(2,1)S(1)}, ...), branch_computations={%region_10.10_spmd, %region_11.11_spmd} | conditional | flops 2031026176 | bytes 39235636 | solution.py:433
  784.3 12.0 %conditional.7 = (f32[512,6,128]{2,0,1:T(8,128)}, bf16[1,512,256]{1,2,0:T(8,128)(2,1)S(1)}) conditional(s32[]{:T(128)} %bitcast.541, f32[512,6,128]{2,0,1:T(8,128)} %get-tuple-element.743, (s32[4]{0:T(128)S(1)}, s32[]{:T(128)}, s32[512,512]{0,1:T(8,128)S(1)}, bf16[4,512,256]{2,1,0:T(8,128)(2,1)}, bf16[512,6,128]{0,2,1:T(8,128)(2,1)S(1)}, ...), branch_computations={%region_10.10_spmd, %region_11.11_spmd} | conditional | flops 2031026176 | bytes 39235636 | solution.py:433
  (729 shorter events, 504.5 us)
Async XLA Ops:
  80.0 61.3 %collective-permute-start.33 = (bf16[3,96,1152]{2,1,0:T(8,128)(2,1)S(1)}, bf16[3,96,1152]{2,1,0:T(8,128)(2,1)S(1)}, u32[]{:S(2)}, u32[]{:S(2)}) collective-permute-start(bf16[3,96,1152]{2,1,0:T(8,128)(2,1)S(1)} %get-tuple-element.460), channel_id=1, source_target_pairs={{0,8},{2,10},{4,12},{6,14},{8,0},{10,2},{12,4},{14,6},{16,24},{18,... | collective-permute-start | bytes 1990664 | tf_op jit(solution)/shard_map/ppermute | solution.py:81
  142.4 156.4 %collective-permute-start.57 = (bf16[256,1536]{1,0:T(8,128)(2,1)}, bf16[256,1536]{1,0:T(8,128)(2,1)}, u32[]{:S(2)}, u32[]{:S(2)}) collective-permute-start(bf16[256,1536]{1,0:T(8,128)(2,1)} %pad_maximum_fusion.32), channel_id=1, source_target_pairs={{0,1},{1,0},{2,3},{3,2},{4,5},{5,4},{6,7},{7,6},{8,9},{9,8},{10,11... | collective-permute-start | bytes 2359304 | tf_op jit(solution)/shard_map/ppermute | solution.py:84
  150.1 141.6 %collective-permute-start.35 = (bf16[2,2,96,1152]{3,2,1,0:T(8,128)(2,1)}, bf16[2,2,96,1152]{3,2,1,0:T(8,128)(2,1)}, u32[]{:S(2)}, u32[]{:S(2)}) collective-permute-start(bf16[2,2,96,1152]{3,2,1,0:T(8,128)(2,1)} %get-tuple-element.455), channel_id=1, source_target_pairs={{0,4},{2,6},{4,0},{6,2},{8,12},{10,14},{12,8},{14,10},{16,20},{18,... | collective-permute-start | bytes 2654216 | tf_op jit(solution)/shard_map/ppermute | solution.py:81
  162.4 64.2 %collective-permute-start.14 = (bf16[512,256]{0,1:T(8,128)(2,1)S(1)}, bf16[512,256]{0,1:T(8,128)(2,1)S(1)}, u32[]{:S(2)}, u32[]{:S(2)}) collective-permute-start(bf16[512,256]{0,1:T(8,128)(2,1)S(1)} %get-tuple-element.555), channel_id=1, source_target_pairs={{0,4},{2,6},{4,0},{6,2},{8,12},{10,14},{12,8},{14,10},{16,20},{18,... | collective-permute-start | bytes 786440 | tf_op jit(solution)/shard_map/ppermute | solution.py:81
  177.2 117.5 %collective-permute-start.39 = (bf16[2,2,96,1152]{3,2,1,0:T(8,128)(2,1)}, bf16[2,2,96,1152]{3,2,1,0:T(8,128)(2,1)}, u32[]{:S(2)}, u32[]{:S(2)}) collective-permute-start(bf16[2,2,96,1152]{3,2,1,0:T(8,128)(2,1)} %get-tuple-element.454), channel_id=1, source_target_pairs={{0,4},{2,6},{4,0},{6,2},{8,12},{10,14},{12,8},{14,10},{16,20},{18,... | collective-permute-start | bytes 2654216 | tf_op jit(solution)/shard_map/ppermute | solution.py:81
  226.6 62.3 %collective-permute-start.37 = (bf16[2,2,96,1152]{3,2,1,0:T(8,128)(2,1)}, bf16[2,2,96,1152]{3,2,1,0:T(8,128)(2,1)}, u32[]{:S(2)}, u32[]{:S(2)}) collective-permute-start(bf16[2,2,96,1152]{3,2,1,0:T(8,128)(2,1)} %get-tuple-element.456), channel_id=1, source_target_pairs={{0,4},{2,6},{4,0},{6,2},{8,12},{10,14},{12,8},{14,10},{16,20},{18,... | collective-permute-start | bytes 2654216 | tf_op jit(solution)/shard_map/ppermute | solution.py:81
  298.7 71.4 %collective-permute-start.36 = (bf16[2,2,2,96,1152]{4,3,2,1,0:T(8,128)(2,1)S(1)}, bf16[2,2,2,96,1152]{4,3,2,1,0:T(8,128)(2,1)S(1)}, u32[]{:S(2)}, u32[]{:S(2)}) collective-permute-start(bf16[2,2,2,96,1152]{4,3,2,1,0:T(8,128)(2,1)S(1)} %pad_maximum_fusion.7), channel_id=1, source_target_pairs={{0,16},{2,18},{4,20},{6,22},{8,24},{10,26},{12,28},{14,30},{16,0},... | collective-permute-start | bytes 5308424 | tf_op jit(solution)/shard_map/ppermute | solution.py:81
  313.1 93.8 %collective-permute-start.40 = (bf16[2,2,2,96,1152]{4,3,2,1,0:T(8,128)(2,1)S(1)}, bf16[2,2,2,96,1152]{4,3,2,1,0:T(8,128)(2,1)S(1)}, u32[]{:S(2)}, u32[]{:S(2)}) collective-permute-start(bf16[2,2,2,96,1152]{4,3,2,1,0:T(8,128)(2,1)S(1)} %pad_maximum_fusion.9), channel_id=1, source_target_pairs={{0,16},{2,18},{4,20},{6,22},{8,24},{10,26},{12,28},{14,30},{16,0},... | collective-permute-start | bytes 5308424 | tf_op jit(solution)/shard_map/ppermute | solution.py:81
  328.1 83.2 %collective-permute-start.26 = (bf16[256,1536]{1,0:T(8,128)(2,1)S(1)}, bf16[256,1536]{1,0:T(8,128)(2,1)S(1)}, u32[]{:S(2)}, u32[]{:S(2)}) collective-permute-start(bf16[256,1536]{1,0:T(8,128)(2,1)S(1)} %collective-permute-done.25), channel_id=1, source_target_pairs={{0,1},{1,0},{2,3},{3,2},{4,5},{5,4},{6,7},{7,6},{8,9},{9,8},{10,11... | collective-permute-start | bytes 2359304 | tf_op jit(solution)/shard_map/ppermute | solution.py:84
  329.7 81.8 %collective-permute-start.28 = (bf16[256,1536]{1,0:T(8,128)(2,1)S(1)}, bf16[256,1536]{1,0:T(8,128)(2,1)S(1)}, u32[]{:S(2)}, u32[]{:S(2)}) collective-permute-start(bf16[256,1536]{1,0:T(8,128)(2,1)S(1)} %collective-permute-done.27), channel_id=1, source_target_pairs={{0,1},{1,0},{2,3},{3,2},{4,5},{5,4},{6,7},{7,6},{8,9},{9,8},{10,11... | collective-permute-start | bytes 2359304 | tf_op jit(solution)/shard_map/ppermute | solution.py:84
  332.3 79.4 %collective-permute-start.31 = (bf16[256,1536]{1,0:T(8,128)(2,1)S(1)}, bf16[256,1536]{1,0:T(8,128)(2,1)S(1)}, u32[]{:S(2)}, u32[]{:S(2)}) collective-permute-start(bf16[256,1536]{1,0:T(8,128)(2,1)S(1)} %pad_maximum_fusion.29), channel_id=1, source_target_pairs={{0,1},{1,0},{2,3},{3,2},{4,5},{5,4},{6,7},{7,6},{8,9},{9,8},{10,11... | collective-permute-start | bytes 2359304 | tf_op jit(solution)/shard_map/ppermute | solution.py:84
  504.5 76.8 %collective-permute-start.103 = (bf16[2,2,2,96,1152]{4,3,2,1,0:T(8,128)(2,1)}, bf16[2,2,2,96,1152]{4,3,2,1,0:T(8,128)(2,1)}, u32[]{:S(2)}, u32[]{:S(2)}) collective-permute-start(bf16[2,2,2,96,1152]{4,3,2,1,0:T(8,128)(2,1)} %dynamic-slice_bitcast_fusion.2), channel_id=1, source_target_pairs={{0,16},{2,18},{4,20},{6,22},{8,24},{10,26},{12,28},{14,30},{16,0},... | collective-permute-start | bytes 5308424 | tf_op jit(solution)/shard_map/ppermute | solution.py:81
  515.9 69.6 %collective-permute-start.98 = (bf16[2,2,2,96,1152]{4,3,2,1,0:T(8,128)(2,1)}, bf16[2,2,2,96,1152]{4,3,2,1,0:T(8,128)(2,1)}, u32[]{:S(2)}, u32[]{:S(2)}) collective-permute-start(bf16[2,2,2,96,1152]{4,3,2,1,0:T(8,128)(2,1)} %dynamic-slice_bitcast_fusion.3), channel_id=1, source_target_pairs={{0,16},{2,18},{4,20},{6,22},{8,24},{10,26},{12,28},{14,30},{16,0},... | collective-permute-start | bytes 5308424 | tf_op jit(solution)/shard_map/ppermute | solution.py:81
  536.6 83.5 %collective-permute-start.93 = (bf16[2,2,2,96,1152]{4,3,2,1,0:T(8,128)(2,1)S(1)}, bf16[2,2,2,96,1152]{4,3,2,1,0:T(8,128)(2,1)S(1)}, u32[]{:S(2)}, u32[]{:S(2)}) collective-permute-start(bf16[2,2,2,96,1152]{4,3,2,1,0:T(8,128)(2,1)S(1)} %dynamic-slice_bitcast_fusion.4), channel_id=1, source_target_pairs={{0,16},{2,18},{4,20},{6,22},{8,24},{10,26},{12,28},{14,30},{16,0},... | collective-permute-start | bytes 5308424 | tf_op jit(solution)/shard_map/ppermute | solution.py:81
  537.6 124.1 %collective-permute-start.41 = (bf16[256,1536]{1,0:T(8,128)(2,1)}, bf16[256,1536]{1,0:T(8,128)(2,1)S(1)}, u32[]{:S(2)}, u32[]{:S(2)}) collective-permute-start(bf16[256,1536]{1,0:T(8,128)(2,1)} %get-tuple-element.431), channel_id=1, source_target_pairs={{0,1},{1,0},{2,3},{3,2},{4,5},{5,4},{6,7},{7,6},{8,9},{9,8},{10,11... | collective-permute-start | bytes 2359304 | tf_op jit(solution)/shard_map/ppermute | solution.py:84
  581.4 83.4 %collective-permute-start.45 = (bf16[256,1536]{1,0:T(8,128)(2,1)S(1)}, bf16[256,1536]{1,0:T(8,128)(2,1)S(1)}, u32[]{:S(2)}, u32[]{:S(2)}) collective-permute-start(bf16[256,1536]{1,0:T(8,128)(2,1)S(1)} %pad_maximum_fusion.30), channel_id=1, source_target_pairs={{0,8},{2,10},{4,12},{6,14},{8,0},{10,2},{12,4},{14,6},{16,24},{18,... | collective-permute-start | bytes 2359304 | tf_op jit(solution)/shard_map/ppermute | solution.py:81
  660.9 69.9 %collective-permute-start.99 = (bf16[2,2,96,1152]{3,2,1,0:T(8,128)(2,1)}, bf16[2,2,96,1152]{3,2,1,0:T(8,128)(2,1)}, u32[]{:S(2)}, u32[]{:S(2)}) collective-permute-start(bf16[2,2,96,1152]{3,2,1,0:T(8,128)(2,1)} %dynamic-slice_bitcast_fusion.6), channel_id=1, source_target_pairs={{0,4},{2,6},{4,0},{6,2},{8,12},{10,14},{12,8},{14,10},{16,20},{18,... | collective-permute-start | bytes 2654216 | tf_op jit(solution)/shard_map/ppermute | solution.py:81
  661.8 87.9 %collective-permute-start.94 = (bf16[2,2,96,1152]{3,2,1,0:T(8,128)(2,1)}, bf16[2,2,96,1152]{3,2,1,0:T(8,128)(2,1)}, u32[]{:S(2)}, u32[]{:S(2)}) collective-permute-start(bf16[2,2,96,1152]{3,2,1,0:T(8,128)(2,1)} %dynamic-slice_bitcast_fusion.7), channel_id=1, source_target_pairs={{0,4},{2,6},{4,0},{6,2},{8,12},{10,14},{12,8},{14,10},{16,20},{18,... | collective-permute-start | bytes 2654216 | tf_op jit(solution)/shard_map/ppermute | solution.py:81
  679.7 74.8 %collective-permute-start.66 = (bf16[256,1536]{1,0:T(8,128)(2,1)}, bf16[256,1536]{1,0:T(8,128)(2,1)}, u32[]{:S(2)}, u32[]{:S(2)}) collective-permute-start(bf16[256,1536]{1,0:T(8,128)(2,1)} %get-tuple-element.411), channel_id=1, source_target_pairs={{0,1},{1,0},{2,3},{3,2},{4,5},{5,4},{6,7},{7,6},{8,9},{9,8},{10,11... | collective-permute-start | bytes 2359304 | tf_op jit(solution)/shard_map/ppermute | solution.py:84
  680.3 124.2 %collective-permute-start.49 = (bf16[256,1536]{1,0:T(8,128)(2,1)}, bf16[256,1536]{1,0:T(8,128)(2,1)}, u32[]{:S(2)}, u32[]{:S(2)}) collective-permute-start(bf16[256,1536]{1,0:T(8,128)(2,1)} %get-tuple-element.483), channel_id=1, source_target_pairs={{0,1},{1,0},{2,3},{3,2},{4,5},{5,4},{6,7},{7,6},{8,9},{9,8},{10,11... | collective-permute-start | bytes 2359304 | tf_op jit(solution)/shard_map/ppermute | solution.py:84
  683.5 134.7 %collective-permute-start.105 = (bf16[96,1152]{1,0:T(8,128)(2,1)}, bf16[96,1152]{1,0:T(8,128)(2,1)}, u32[]{:S(2)}, u32[]{:S(2)}) collective-permute-start(bf16[96,1152]{1,0:T(8,128)(2,1)} %get-tuple-element.507), channel_id=1, source_target_pairs={{0,2},{2,0},{4,6},{6,4},{8,10},{10,8},{12,14},{14,12},{16,18},{18,... | collective-permute-start | bytes 663560 | tf_op jit(solution)/shard_map/ppermute | solution.py:81
  730.8 91.8 %collective-permute-start.106 = (bf16[96,1152]{1,0:T(8,128)(2,1)}, bf16[96,1152]{1,0:T(8,128)(2,1)}, u32[]{:S(2)}, u32[]{:S(2)}) collective-permute-start(bf16[96,1152]{1,0:T(8,128)(2,1)} %get-tuple-element.509), channel_id=1, source_target_pairs={{0,8},{2,10},{4,12},{6,14},{8,0},{10,2},{12,4},{14,6},{16,24},{18,... | collective-permute-start | bytes 663560 | tf_op jit(solution)/shard_map/ppermute | solution.py:81
  749.7 73.1 %collective-permute-start.107 = (bf16[96,1152]{1,0:T(8,128)(2,1)}, bf16[96,1152]{1,0:T(8,128)(2,1)}, u32[]{:S(2)}, u32[]{:S(2)}) collective-permute-start(bf16[96,1152]{1,0:T(8,128)(2,1)} %get-tuple-element.508), channel_id=1, source_target_pairs={{0,10},{2,8},{4,14},{6,12},{8,2},{10,0},{12,6},{14,4},{16,26},{18,... | collective-permute-start | bytes 663560 | tf_op jit(solution)/shard_map/ppermute | solution.py:81
  754.4 71.7 %collective-permute-start.100 = (bf16[96,1152]{1,0:T(8,128)(2,1)}, bf16[96,1152]{1,0:T(8,128)(2,1)}, u32[]{:S(2)}, u32[]{:S(2)}) collective-permute-start(bf16[96,1152]{1,0:T(8,128)(2,1)} %get-tuple-element.512), channel_id=1, source_target_pairs={{0,2},{2,0},{4,6},{6,4},{8,10},{10,8},{12,14},{14,12},{16,18},{18,... | collective-permute-start | bytes 663560 | tf_op jit(solution)/shard_map/ppermute | solution.py:81
  (183 other events, 3253.6 us)

commit v2 on v1

v2 whole, which is shorter than its diff:
```python
import functools

import jax
import jax.numpy as jnp
from jax import lax
from jax.experimental import pallas as pl
from jax.experimental.pallas import tpu as pltpu
from jax.sharding import PartitionSpec as P

EPSILON = 1e-06
ROPE_BASE = 1000000.0
MASKED = -1e30
LANES = 128
BOTH = ("fsdp", "context")
KERNEL_BYTES = 56 << 20
BF = jnp.bfloat16
F32 = jnp.float32


def tables(positions, head_width):
    ladder = jnp.arange(head_width // 2, dtype=F32)
    inverse = jnp.exp(-jnp.log(ROPE_BASE) * 2.0 * ladder / head_width)
    angles = positions.astype(F32)[:, None] * inverse[None, :]
    return (jnp.cos(angles), jnp.sin(angles))


def rotate(field, cosine, sine):
    middle = field.shape[-1] // 2
    first_half = field[..., :middle]
    second_half = field[..., middle:]
    cos_rows = cosine[:, None, :]
    sin_rows = sine[:, None, :]
    return jnp.concatenate(
        [
            first_half * cos_rows - second_half * sin_rows,
            second_half * cos_rows + first_half * sin_rows,
        ],
        axis=-1,
    )


def unrotate(gradient, cosine, sine):
    return rotate(gradient, cosine, -sine)


def locate(blocks, prompt_slots, block_rows):
    segment = jnp.where(blocks < prompt_slots, 0, blocks - prompt_slots + 1)
    anchor = jnp.where(blocks < prompt_slots, blocks * block_rows, prompt_slots * block_rows)
    return (segment, anchor)


def dot_nn(left, right):
    return lax.dot_general(left, right, (((1,), (0,)), ((), ())), preferred_element_type=F32)


def dot_tn(left, right):
    return lax.dot_general(left, right, (((0,), (0,)), ((), ())), preferred_element_type=F32)


def dot_nt(left, right):
    return lax.dot_general(left, right, (((1,), (1,)), ((), ())), preferred_element_type=F32)


def norm_back(grad_normed, rows_normed, inv_rms, gain):
    grad_rows = grad_normed * gain.astype(F32)
    return inv_rms * (
        grad_rows - rows_normed * jnp.mean(grad_rows * rows_normed, axis=-1, keepdims=True)
    )


def attend_kernel(count, scale, seen, q_ref, *refs):
    pairs = refs[:count]
    out_ref, low_ref, lse_ref, peak_ref, total_ref, sum_ref = refs[count:]
    wide = q_ref.shape[1]
    query = q_ref[...]

    def piece(r):
        scores = dot_nt(pairs[r][:, :wide], query) * scale
        if r == 0:
            rows = lax.broadcasted_iota(jnp.int32, scores.shape, 0)
            columns = lax.broadcasted_iota(jnp.int32, scores.shape, 1)
            scores = jnp.where(rows <= columns, scores, MASKED)
            peak = jnp.max(scores, axis=0, keepdims=True)
        else:
            old = peak_ref[...]
            peak = jnp.maximum(old, jnp.max(scores, axis=0, keepdims=True))
        probs = jnp.exp(scores - peak)
        total = jnp.sum(probs, axis=0, keepdims=True)
        mixed = dot_tn(pairs[r][:, wide:], probs.astype(BF))
        if r:
            shrink = jnp.exp(old - peak)
            total = total + total_ref[...] * shrink
            mixed = mixed + sum_ref[...] * shrink
        peak_ref[...] = peak
        total_ref[...] = total
        sum_ref[...] = mixed

    piece(0)
    for r in range(1, count):
        pl.when(seen[r] != 0)(functools.partial(piece, r))
    total = total_ref[...]
    out = jnp.transpose(sum_ref[...] / total)
    out_ref[...] = out
    low_ref[...] = out.astype(BF)
    lse_ref[...] = (peak_ref[...] + jnp.log(total))[None]


def attend(seen, queries, pairs, heads, scale):
    rows = queries.shape[0]
    wide = queries.shape[1] // heads
    count = len(pairs)
    head = pl.BlockSpec((rows, wide), lambda h, seen: (0, h))
    whole = pl.BlockSpec(pairs[0].shape, lambda h, seen: (0, 0))
    return pl.pallas_call(
        functools.partial(attend_kernel, count, scale),
        grid_spec=pltpu.PrefetchScalarGridSpec(
            num_scalar_prefetch=1,
            grid=(heads,),
            in_specs=[head] + [whole] * count,
            out_specs=[head, head, pl.BlockSpec((1, 1, rows), lambda h, seen: (h, 0, 0))],
            scratch_shapes=[
                pltpu.VMEM((1, rows), F32),
                pltpu.VMEM((1, rows), F32),
                pltpu.VMEM((wide, rows), F32),
            ],
        ),
        out_shape=[
            jax.ShapeDtypeStruct(queries.shape, F32),
            jax.ShapeDtypeStruct(queries.shape, BF),
            jax.ShapeDtypeStruct((heads, 1, rows), F32),
        ],
        compiler_params=pltpu.CompilerParams(vmem_limit_bytes=KERNEL_BYTES),
        cost_estimate=pl.CostEstimate(
            flops=100 * rows * queries.size, bytes_accessed=8 * queries.size, transcendentals=0
        ),
    )(seen, queries, *pairs)


def attend_back_kernel(count, scale, seen, q_ref, g_ref, out_ref, lse_ref, *refs):
    pairs = refs[:count]
    dq_ref = refs[count]
    grads = refs[count + 1 : 2 * count + 1]
    held, sum_ref = refs[2 * count + 1 :]
    wide = q_ref.shape[1]
    step = pl.program_id(0)
    query = q_ref[...]
    grad = g_ref[...]
    delta = jnp.sum(grad.astype(F32) * out_ref[...], axis=1, keepdims=True)
    delta = jnp.transpose(jnp.broadcast_to(delta, q_ref.shape))[:1]
    lse = lse_ref[0]

    @pl.when(step == 0)
    def _():
        held[...] = jnp.zeros_like(held)

    def piece(r):
        key = pairs[r][:, :wide]
        probs = jnp.exp(dot_nt(key, query) * scale - lse)
        if r == 0:
            rows = lax.broadcasted_iota(jnp.int32, probs.shape, 0)
            columns = lax.broadcasted_iota(jnp.int32, probs.shape, 1)
            probs = jnp.where(rows <= columns, probs, 0.0)
        grad_scores = (probs * (dot_nt(pairs[r][:, wide:], grad) - delta)).astype(BF)
        held[r, :, wide:] += dot_nn(probs.astype(BF), grad)
        held[r, :, :wide] += dot_nn(grad_scores, query) * scale
        term = dot_tn(key, grad_scores)
        sum_ref[...] = term if r == 0 else sum_ref[...] + term

    piece(0)
    for r in range(1, count):
        pl.when(seen[r] != 0)(functools.partial(piece, r))
    dq_ref[...] = jnp.transpose(sum_ref[...]) * scale

    @pl.when(step == pl.num_programs(0) - 1)
    def _():
        for r in range(count):
            grads[r][...] = held[r].astype(grads[r].dtype)


def attend_back(seen, queries, grads, outs, lse, pairs, heads, scale):
    rows = queries.shape[0]
    wide = queries.shape[1] // heads
    count = len(pairs)
    head = pl.BlockSpec((rows, wide), lambda h, seen: (0, h))
    whole = pl.BlockSpec(pairs[0].shape, lambda h, seen: (0, 0))
    results = pl.pallas_call(
        functools.partial(attend_back_kernel, count, scale),
        grid_spec=pltpu.PrefetchScalarGridSpec(
            num_scalar_prefetch=1,
            grid=(heads,),
            in_specs=[head] * 3
            + [pl.BlockSpec((1, 1, rows), lambda h, seen: (h, 0, 0))]
            + [whole] * count,
            out_specs=[head] + [whole] * count,
            scratch_shapes=[
                pltpu.VMEM((count,) + pairs[0].shape, F32),
                pltpu.VMEM((wide, rows), F32),
            ],
        ),
        out_shape=[jax.ShapeDtypeStruct(queries.shape, F32)]
        + [jax.ShapeDtypeStruct(pairs[0].shape, F32 if r == 0 else BF) for r in range(count)],
        compiler_params=pltpu.CompilerParams(vmem_limit_bytes=KERNEL_BYTES),
        cost_estimate=pl.CostEstimate(
            flops=150 * rows * queries.size, bytes_accessed=16 * queries.size, transcendentals=0
        ),
    )(seen, queries, grads, outs, lse, *pairs)
    return results[0], results[1:]


def hidden_kernel(n_ref, d_ref, wg_ref, wu_ref, wd_ref, act_ref, dg_ref, du_ref):
    gate = dot_nn(n_ref[...], wg_ref[...])
    up = dot_nn(n_ref[...], wu_ref[...])
    sigmoid = jax.nn.sigmoid(gate)
    silu = gate * sigmoid
    act_ref[...] = (silu * up).astype(BF)
    grad = dot_nn(d_ref[...], wd_ref[...])
    du_ref[...] = (grad * silu).astype(BF)
    dg_ref[...] = (grad * up * (sigmoid + silu * (1.0 - sigmoid))).astype(BF)


def hidden_units(normed, grads, gate_w, up_w, down_w):
    tokens, depth = normed.shape
    units = gate_w.shape[1]
    tm = min(tokens, 256)
    rows = pl.BlockSpec((tm, depth), lambda m: (m, 0))
    weight = pl.BlockSpec((depth, units), lambda m: (0, 0))
    out = pl.BlockSpec((tm, units), lambda m: (m, 0))
    flops = 6 * tokens * depth * units
    return pl.pallas_call(
        hidden_kernel,
        grid=(tokens // tm,),
        in_specs=[rows, rows, weight, weight, weight],
        out_specs=[out] * 3,
        out_shape=[jax.ShapeDtypeStruct((tokens, units), BF)] * 3,
        compiler_params=pltpu.CompilerParams(vmem_limit_bytes=KERNEL_BYTES),
        cost_estimate=pl.CostEstimate(
            flops=flops, bytes_accessed=2 * units * (depth + tokens) * 3, transcendentals=0
        ),
    )(normed, grads, gate_w, up_w, down_w)


def back_kernel(dg_ref, du_ref, wg_ref, wu_ref, out_ref):
    out_ref[...] = (
        dot_nt(dg_ref[...], wg_ref[...]) + dot_nt(du_ref[...], wu_ref[...])
    ).astype(BF)


def hidden_back(grad_gate, grad_up, gate_w, up_w):
    tokens, units = grad_gate.shape
    depth = gate_w.shape[0]
    tm = min(tokens, 512)
    rows = pl.BlockSpec((tm, units), lambda m: (m, 0))
    weight = pl.BlockSpec((depth, units), lambda m: (0, 0))
    return pl.pallas_call(
        back_kernel,
        grid=(tokens // tm,),
        in_specs=[rows, rows, weight, weight],
        out_specs=pl.BlockSpec((tm, depth), lambda m: (m, 0)),
        out_shape=jax.ShapeDtypeStruct((tokens, depth), BF),
        compiler_params=pltpu.CompilerParams(vmem_limit_bytes=KERNEL_BYTES),
        cost_estimate=pl.CostEstimate(
            flops=4 * tokens * depth * units,
            bytes_accessed=4 * units * (depth + tokens),
            transcendentals=0,
        ),
    )(grad_gate, grad_up, gate_w, up_w)


def after(x, *earlier):
    return lax.optimization_barrier((x,) + earlier)[0]


class Grid:
    def __init__(self):
        self.nf = lax.axis_size("fsdp")
        self.nc = lax.axis_size("context")
        self.n = self.nf * self.nc
        self.cbits = self.nc.bit_length() - 1
        self.fbits = self.nf.bit_length() - 1
        self.me = lax.axis_index("fsdp") * self.nc + lax.axis_index("context")
        self.my_slot = lax.axis_index("context")
        self.core = lax.axis_index("tensor")
        self.last = {}
        self.zm = 1
        self.xm = self.nc
        self.deep = list(range(1, self.cbits)) + list(range(self.cbits + 1, self.cbits + self.fbits))

    def bit(self, b):
        return (self.me >> b) & 1

    def lanes(self, mask):
        found = set()
        for b in range(self.cbits + self.fbits):
            if mask >> b & 1:
                if b == 0:
                    found.add("near")
                elif b < self.cbits:
                    found.add("far")
                elif b == self.cbits:
                    found.add("x")
                else:
                    found.add("y")
        return found

    def xor(self, x, mask):
        return lax.ppermute(x, BOTH, [(i, i ^ mask) for i in range(self.n)])

    def send(self, pairs, free=False, wait=None):
        lanes = set().union(*[self.lanes(mask) for _, mask in pairs])
        earlier = []
        if wait is not None:
            earlier = list(wait)
        elif not free:
            for lane in sorted(lanes):
                earlier += self.last.get(lane, [])
        outs = []
        for x, mask in pairs:
            outs.append(self.xor(after(x, *earlier) if earlier else x, mask))
        for lane in lanes:
            self.last[lane] = list(outs)
        return outs

    def one(self, x, mask, free=False):
        return self.send([(x, mask)], free)[0]

    def swap(self, x):
        return lax.ppermute(x, "tensor", [(0, 1), (1, 0)])

    def pair(self, b, mine, theirs, axis):
        low = self.bit(b) == 0
        return jnp.stack([jnp.where(low, mine, theirs), jnp.where(low, theirs, mine)], axis)

    def ordered(self, pieces, bits):
        if len(bits) == 0:
            return pieces[0]
        half = len(pieces) // 2
        low = self.ordered(pieces[:half], bits[:-1])
        high = self.ordered(pieces[half:], bits[:-1])
        return self.pair(bits[-1], low, high, 0)

    def gather_context(self, x, bits):
        rows, columns = x.shape
        w, held = x[None], []
        w = x
        for b in bits:
            w = self.pair(b, w, self.one(w, 1 << b), 0) if not held else self.deepen(w, held, b)
            if not held:
                held.append(b)
        return w, held

    def gather_fsdp(self, x):
        rows, columns = x.shape
        if self.fbits == 2:
            xm, ym = self.xm, 2 * self.xm
            gx, gy = self.one(x, xm), self.one(x, ym)
            cut = rows // 2
            by_y, by_x = self.one(gx[:cut], ym), self.one(gy[cut:], xm)
            pieces = [x, gx, gy, jnp.concatenate([by_y, by_x], 0)]
            x = self.ordered(pieces, [self.cbits, self.cbits + 1])
        else:
            pieces = [x] + self.send([(x, r * self.nc) for r in range(1, self.nf)])
            x = self.ordered(pieces, [self.cbits + k for k in range(self.fbits)])
        return x.reshape(self.nf * rows, columns)

    def scatter_fsdp(self, x):
        columns = x.shape[1]
        x = x.reshape(self.nf, -1, columns)
        rows = x.shape[1]
        mine = lax.axis_index("fsdp")
        take = lambda r: lax.dynamic_index_in_dim(x, mine ^ r, 0, keepdims=False)
        if self.fbits == 2:
            xm, ym = self.xm, 2 * self.xm
            cut = rows // 2
            far = take(3)
            by_y, by_x = self.one(far[:cut], ym), self.one(far[cut:], xm)
            px, py = take(1), take(2)
            px = jnp.concatenate([px[:cut].astype(F32) + by_y.astype(F32), px[cut:].astype(F32)], 0)
            py = jnp.concatenate([py[:cut].astype(F32), py[cut:].astype(F32) + by_x.astype(F32)], 0)
            rx = self.one(px.astype(BF), xm)
            ry = self.one(py.astype(BF), ym)
            x = take(0).astype(F32) + rx.astype(F32) + ry.astype(F32)
        else:
            parts = self.send([(take(r), r * self.nc) for r in range(1, self.nf)])
            x = take(0).astype(F32)
            for part in parts:
                x = x + part.astype(F32)
        return x.astype(BF)

    def scatter_context(self, x):
        columns = x.shape[1]
        x = x.reshape(self.nc, -1, columns)
        pick = lambda r: lax.dynamic_index_in_dim(x, self.my_slot ^ r, 0, keepdims=False)
        parts = self.send([(pick(r), r) for r in range(1, self.nc)])
        total = pick(0).astype(F32)
        for part in parts:
            total = total + part.astype(F32)
        return total

    def scatter_small(self, x):
        columns = x.shape[1]
        x = x.reshape(self.nf, self.nc, columns)
        mine = lax.axis_index("fsdp")
        take = lambda r: lax.dynamic_index_in_dim(x, mine ^ r, 0, keepdims=False)
        total = take(0)
        for part in [self.xor(take(r), r * self.nc) for r in range(1, self.nf)]:
            total = total + part
        pick = lambda r: lax.dynamic_index_in_dim(total, self.my_slot ^ r, 0, keepdims=True)
        final = pick(0)
        for part in [self.xor(pick(r), r) for r in range(1, self.nc)]:
            final = final + part
        return final

    def tokens_in(self, x, other=None):
        zm, xm = self.zm, self.xm
        cut = x.shape[0] // 2
        if other is None:
            other = self.swap(x)
        px, pz = self.one(x, xm), self.one(x, zm)
        by_z, by_x = self.one(px[:cut], zm), self.one(pz[cut:], xm)
        got = jnp.concatenate([px, pz, by_z, by_x], 0)
        return jnp.concatenate([x, got, other, self.swap(got)], 0)

    def tokens_out(self, part):
        zm, xm = self.zm, self.xm
        rows = part.shape[0] // 8
        cut = rows // 2
        part = part[: 4 * rows].astype(F32) + self.swap(part[4 * rows :]).astype(F32)
        own, px, pz, far = [part[k * rows : (k + 1) * rows] for k in range(4)]
        by_z = self.one(far[:cut].astype(BF), zm)
        by_x = self.one(far[cut:].astype(BF), xm)
        px = jnp.concatenate([px[:cut] + by_z.astype(F32), px[cut:]], 0).astype(BF)
        pz = jnp.concatenate([pz[:cut], pz[cut:] + by_x.astype(F32)], 0).astype(BF)
        total = own + self.one(px, xm).astype(F32) + self.one(pz, zm).astype(F32)
        return total, (by_z, by_x)

    def quarter_masks(self):
        return (0, self.zm, self.xm, self.xm + self.zm)

    def my_quarter(self):
        return 2 * self.bit(self.cbits) + self.bit(0)

    def quarters_in(self, w, wait):
        rows, width = w.shape[0], w.shape[1] // 4
        q = self.my_quarter()
        blocks = [lax.dynamic_slice(w, (0, (q ^ r) * width), (rows, width)) for r in range(4)]
        got = self.send(list(zip(blocks[1:], self.quarter_masks()[1:])), wait=wait)
        return self.ordered(blocks[:1] + got, [0, self.cbits])

    def quarter_x(self, w):
        half = w.shape[1] // 2
        take = lambda k: lax.dynamic_slice(w, (0, k * half), (w.shape[0], half))
        xb = self.bit(self.cbits)
        return self.pair(self.cbits, take(xb), self.one(take(1 - xb), self.xm), 0)

    def quarter_z(self, w):
        half = w.shape[2] // 2
        take = lambda k: lax.dynamic_slice(w, (0, 0, k * half), w.shape[:2] + (half,))
        zb = self.bit(0)
        return self.pair(0, take(zb), self.one(take(1 - zb), self.zm), 1)

    def quarters_out(self, g):
        rows, width = g.shape[2:]
        g = g.reshape(4, rows, width)
        q = self.my_quarter()
        blocks = [lax.dynamic_index_in_dim(g, q ^ r, 0, keepdims=False) for r in range(4)]
        got = self.send(list(zip(blocks[1:], self.quarter_masks()[1:])))
        full = self.ordered(blocks[:1] + got, [0, self.cbits]).reshape(4, rows, width)
        return full.transpose(1, 0, 2).reshape(rows, 4 * width).astype(F32)

    def deepen(self, w, held, b):
        axis = sum(1 for h in held if h > b)
        held.append(b)
        got = self.one(w, 1 << b)
        self.got = got
        return self.pair(b, w, got, axis)

    def fold(self, g, held, b):
        axis = held.index(b)
        held.remove(b)
        give = lax.dynamic_index_in_dim(g, 1 - self.bit(b), axis, keepdims=False)
        keep = lax.dynamic_index_in_dim(g, self.bit(b), axis, keepdims=False)
        return (keep.astype(F32) + self.one(give, 1 << b).astype(F32)).astype(BF)


def on_device(
    tokens,
    block_order,
    norm_one,
    w_query,
    b_query,
    w_key,
    b_key,
    w_value,
    b_value,
    w_out,
    norm_two,
    w_gate,
    w_up,
    w_down,
    cotangent,
):
    grid = Grid()
    block_rows, width = tokens.shape
    shard = norm_one.shape[0]
    slot_count = grid.nc
    prompt_slots = slot_count // 2
    head_width = w_key.shape[1]
    query_width = w_query.shape[1]
    head_group = query_width // head_width
    score_scale = head_width ** (-0.5)
    cores = lax.axis_size("tensor")
    own_rows = block_rows // cores
    owners = block_order[0]
    my_block = lax.dynamic_index_in_dim(owners, grid.my_slot, 0, keepdims=False)
    query_anchor = locate(my_block, prompt_slots, block_rows)[1]
    query_pos = query_anchor + jnp.arange(block_rows)

    def own(x):
        return lax.dynamic_slice(x, (grid.core * own_rows, 0), (own_rows, x.shape[1]))

    def others(x):
        return lax.dynamic_slice(x, ((1 - grid.core) * own_rows, 0), (own_rows, x.shape[1]))

    def both(x):
        other = grid.swap(x)
        first = grid.core == 0
        return jnp.concatenate([jnp.where(first, x, other), jnp.where(first, other, x)], 0)

    def summed(part):
        give = lax.dynamic_slice(part, ((1 - grid.core) * own_rows, 0), (own_rows, width))
        return own(part) + grid.swap(give.astype(BF)).astype(F32)

    bias_shard = b_query.shape[1]
    small_bias = b_key.shape[1]
    vector = jnp.concatenate([norm_one[None], norm_two[None], b_query, b_key, b_value], axis=1)
    columns = query_width + 2 * head_width
    vector = jnp.pad(vector, ((0, 7), (0, columns - vector.shape[1])))
    packed = jnp.concatenate(
        [jnp.concatenate([w_query, w_key, w_value], axis=1), vector], axis=0
    )
    hidden = w_gate.shape[1]
    quarter = -(-hidden // (4 * LANES)) * LANES
    pad = ((0, 0), (0, 4 * quarter - hidden))
    w_out_t = lax.all_gather(w_out.T, BOTH, axis=0, tiled=True)

    context_deep = [b for b in grid.deep if b < grid.cbits]
    fsdp_deep = [b for b in grid.deep if b > grid.cbits]
    deep_first = context_deep[::-1]
    packed, held = grid.gather_context(packed, deep_first)
    w_one = grid.quarters_in(jnp.pad(w_gate, pad), wait=[])
    grid.last["near"] = []
    packed = grid.deepen(packed, held, 0).reshape(grid.nc * (shard + 8), columns)
    w_two = grid.quarter_x(jnp.pad(w_up, pad))
    grid.last["x"] = []
    w_two = grid.quarter_z(w_two)
    packed = grid.gather_fsdp(packed).reshape(grid.n, shard + 8, columns)
    w_qkv = packed[:, :shard].reshape(grid.n * shard, columns)
    vectors = packed[:, shard]
    gain_one = vectors[:, :shard].reshape(-1)
    gain_two = vectors[:, shard : 2 * shard].reshape(-1)
    start = 2 * shard
    bias = jnp.concatenate(
        [
            vectors[:, start : start + bias_shard].reshape(-1),
            vectors[:, start + bias_shard : start + bias_shard + small_bias].reshape(-1),
            vectors[
                :, start + bias_shard + small_bias : start + bias_shard + 2 * small_bias
            ].reshape(-1),
        ]
    ).astype(F32)
    held_one, held_two, held_three = [[0, grid.cbits] for _ in range(3)]
    grid.last["far"] = []
    for b in context_deep:
        w_one = grid.deepen(w_one, held_one, b)
    for b in context_deep:
        w_two = grid.deepen(w_two, held_two, b)
    second_deep = grid.last["far"]
    for b in fsdp_deep:
        w_one = grid.deepen(w_one, held_one, b)

    inputs = tokens.astype(F32)
    inv_one = lax.rsqrt(jnp.mean(inputs * inputs, axis=-1, keepdims=True) + EPSILON)
    rows_one = inputs * inv_one
    normed_one = (rows_one * gain_one.astype(F32)).astype(BF)
    cosine, sine = tables(query_pos, head_width)
    qkv = dot_nn(normed_one, w_qkv) + bias
    queries = (
        rotate(qkv[:, :query_width].reshape(block_rows, head_group, head_width), cosine, sine)
        .reshape(block_rows, query_width)
        .astype(BF)
    )
    keys = (
        rotate(
            qkv[:, query_width : query_width + head_width].reshape(block_rows, 1, head_width),
            cosine,
            sine,
        )
        .reshape(block_rows, head_width)
        .astype(BF)
    )
    values = qkv[:, query_width + head_width :].astype(BF)
    pair = jnp.concatenate([keys, values], axis=1)
    pairs = [pair] + grid.send([(pair, r) for r in range(1, slot_count)], wait=[])
    grid.last["far"] = second_deep
    grid.last["near"] = pairs[1:]
    w_three = grid.quarter_z(grid.quarter_x(jnp.pad(after(w_down, w_qkv).T, pad)))
    grads_in = grid.tokens_in(own(cotangent), others(cotangent))
    for b in fsdp_deep:
        w_two = grid.deepen(w_two, held_two, b)
    for b in context_deep + fsdp_deep:
        w_three = grid.deepen(w_three, held_three, b)
    gate_full, up_full, down_full = [
        w.reshape(grid.n * shard, quarter) for w in (w_one, w_two, w_three)
    ]
    piece_block = owners[grid.my_slot ^ jnp.arange(slot_count)]
    seen = ((piece_block < prompt_slots) & (piece_block < my_block)).astype(jnp.int32)
    attn_heads, out_low, log_total = attend(seen, queries, pairs, head_group, score_scale)
    hidden_one = own(tokens).astype(F32) + summed(dot_nt(after(out_low, *second_deep), w_out_t))

    inv_two = lax.rsqrt(jnp.mean(hidden_one * hidden_one, axis=-1, keepdims=True) + EPSILON)
    rows_two = hidden_one * inv_two
    normed_two = (rows_two * gain_two.astype(F32)).astype(BF)
    normed_in = grid.tokens_in(normed_two)
    act, grad_gate, grad_up = hidden_units(normed_in, grads_in, gate_full, up_full, down_full)
    top = sorted(range(grid.cbits + grid.fbits), reverse=True)
    shape = (2,) * len(top) + (shard, quarter)
    helds = [list(top) for _ in range(3)]
    down_first = fsdp_deep[::-1] + context_deep[::-1]
    grad_wdown = dot_tn(grads_in, act).astype(BF)
    grad_normed_two = hidden_back(after(grad_gate, grad_wdown), grad_up, gate_full, up_full)
    grad_normed_parts = grad_normed_two
    grad_wdown = grad_wdown.reshape(shape)
    for b in fsdp_deep[::-1]:
        grad_wdown = grid.fold(grad_wdown, helds[0], b)
    grad_normed_two, started = grid.tokens_out(grad_normed_two)
    grad_wgate = dot_tn(normed_in, after(grad_gate, grad_normed_parts)).astype(BF)
    grad_wup = dot_tn(normed_in, after(grad_up, grad_wgate, *started)).astype(BF).reshape(shape)
    grad_wgate = grad_wgate.reshape(shape)
    for b in context_deep[::-1]:
        grad_wdown = grid.fold(grad_wdown, helds[0], b)
    for b in fsdp_deep[::-1]:
        grad_wgate = grid.fold(grad_wgate, helds[1], b)
    for b in context_deep[::-1]:
        grad_wgate = grid.fold(grad_wgate, helds[1], b)
    for b in fsdp_deep[::-1]:
        grad_wup = grid.fold(grad_wup, helds[2], b)

    grad_gain_two = jnp.sum(grad_normed_two * rows_two, axis=0)
    grad_hidden_one = own(cotangent).astype(F32) + norm_back(
        grad_normed_two, rows_two, inv_two, gain_two
    )

    grad_low = both(grad_hidden_one.astype(BF))
    grad_wout = dot_tn(grad_low, out_low).astype(BF)
    grad_heads = dot_nn(grad_low, w_out_t).astype(BF)
    grad_query, grad_pairs = attend_back(
        seen, queries, grad_heads, attn_heads, log_total, pairs, head_group, score_scale
    )
    grad_query_lin = (
        unrotate(grad_query.reshape(block_rows, head_group, head_width), cosine, sine)
        .reshape(block_rows, query_width)
        .astype(BF)
    )
    grad_pair = grad_pairs[0]
    mlp_part = dot_nt(after(act, grad_wup, grad_heads), down_full).astype(BF)
    for part in grid.send([(grad_pairs[r], r) for r in range(1, slot_count)]):
        grad_pair = grad_pair + part.astype(F32)
    grad_wquery = dot_tn(normed_one, grad_query_lin).astype(BF)
    grad_attn = grid.scatter_fsdp(jnp.concatenate([grad_wquery, grad_wout], axis=1))
    for b in context_deep[::-1]:
        grad_wup = grid.fold(grad_wup, helds[2], b)
    grad_key_lin = unrotate(
        grad_pair[:, :head_width].reshape(block_rows, 1, head_width), cosine, sine
    ).reshape(block_rows, head_width)
    grad_kv = jnp.concatenate([grad_key_lin, grad_pair[:, head_width:]], axis=1).astype(BF)
    mlp_total, _ = grid.tokens_out(mlp_part)
    result = both((after(hidden_one, grad_query) + mlp_total).astype(BF))
    grad_wkv = grid.scatter_fsdp(dot_tn(normed_one, grad_kv).astype(BF))
    grad_dg = grid.quarters_out(jnp.concatenate([grad_wdown, grad_wgate], axis=2))
    grad_wdown, grad_wgate = grad_dg[:shard], grad_dg[shard:]
    grad_attn = grid.scatter_context(jnp.concatenate([grad_attn, grad_wkv], axis=1))
    grad_wup = grid.quarters_out(grad_wup)
    grad_qkv = jnp.concatenate([grad_query_lin, grad_kv], axis=1)
    grad_bias = jnp.sum(grad_qkv.astype(F32), axis=0)
    grad_normed_one = summed(dot_nt(grad_qkv, w_qkv))
    rows_own = own(rows_one)
    inv_own = own(inv_one)
    grad_gain_one = jnp.sum(grad_normed_one * rows_own, axis=0)
    grad_inputs = grad_hidden_one + norm_back(grad_normed_one, rows_own, inv_own, gain_one)
    grad_tokens = both(grad_inputs.astype(BF))

    gains = jnp.concatenate(
        [grad_gain_one.reshape(-1, shard), grad_gain_two.reshape(-1, shard)], axis=1
    )
    gains = gains + grid.swap(gains)
    small = jnp.concatenate(
        [
            gains,
            grad_bias[:query_width].reshape(-1, bias_shard),
            grad_bias[query_width : query_width + head_width].reshape(-1, small_bias),
            grad_bias[query_width + head_width :].reshape(-1, small_bias),
        ],
        axis=1,
    )
    small = grid.scatter_small(small)
    return (
        result,
        grad_tokens,
        small[0, :shard],
        grad_attn[:, :query_width],
        small[:, start : start + bias_shard],
        grad_attn[:, 2 * query_width : 2 * query_width + head_width],
        small[:, start + bias_shard : start + bias_shard + small_bias],
        grad_attn[:, 2 * query_width + head_width :],
        small[:, start + bias_shard + small_bias :],
        grad_attn[:, query_width : 2 * query_width].T,
        small[0, shard : 2 * shard],
        grad_wgate[:, :hidden],
        grad_wup[:, :hidden],
        grad_wdown[:, :hidden].T,
    )


def solution(mesh):
    rows = P(("fsdp", "context"), None)
    split = P(("fsdp", "context"))
    into = P(("fsdp", "context"), "tensor")
    back = P("tensor", ("fsdp", "context"))
    return jax.shard_map(
        on_device,
        mesh=mesh,
        in_specs=(
            rows,
            P("fsdp", None),
            split,
            into,
            back,
            into,
            back,
            into,
            back,
            back,
            split,
            into,
            into,
            back,
            rows,
        ),
        out_specs=(
            rows,
            rows,
            split,
            into,
            back,
            into,
            back,
            into,
            back,
            back,
            split,
            into,
            into,
            back,
        ),
        check_vma=False,
    )
```

time: 955 us -> 763 us (0.80)
  waiting for transfers between devices: 480 us -> 313 us
  Pallas kernels: 0 us -> 92.1 us
  matrix products: 149 us -> 64.9 us
  starting transfers between devices: 129 us -> 108 us
  between operations: 4.47 us -> 17.2 us
    ppermute x86 -> x70, waiting for transfers between devices: 480 us -> 312 us  [xor(): return lax.ppermute(x, BOTH, [(i, i ^ mask) for i in range(self.n)])]
    pallas_call x0 -> x4, Pallas kernels: none -> 92.1 us  [the longest x1 33.1 us: hidden_units(): pl.pallas_call(hidden_kernel, grid=(tokens // tm,), in_specs=[rows, rows,...]
    dot_general x5 -> x2, matrix products: 45.6 us -> 6 us  [dot_nn(): lax.dot_general(left, right, (((1,), (0,)), ((), ())), preferred_element_...]
    dot_general x14 -> x0, matrix products: 25.6 us -> none  [the longest x2 7.2 us: update_block(): jnp.einsum('hqk,kd->qhd', grad_scores, key_blk, preferred_element_type=F32)]
    ppermute x86 -> x70, starting transfers between devices: 126 us -> 107 us  [xor(): return lax.ppermute(x, BOTH, [(i, i ^ mask) for i in range(self.n)])]
    dot_general x5 -> x3, matrix products: 38.2 us -> 20 us  [dot_nt(): lax.dot_general(left, right, (((1,), (1,)), ((), ())), preferred_element_...]
    unnamed x203 -> x194, local copies, waits for them, and re-layouts: 26.8 us -> 19.3 us
    another operation x40 -> x35, other arithmetic: 21.8 us -> 19.8 us  [pair(): jnp.stack([jnp.where(low, mine, theirs), jnp.where(low, theirs, mine)], a...]
  transfers between devices with their start and end apart: 108 -> 82, of which waited for: 42 -> 31; matrix products, arithmetic and copies ran while one was open for 23% -> 26% of each run, Pallas kernels for 0% -> 5%
where the time goes in v2:
time: 763 us; the launch traced here: 759 us
  waiting for transfers between devices  313 us (41%)
  starting transfers between devices  108 us (14%)
  Pallas kernels  92.1 us (12%)
  other arithmetic  82.5 us (11%)
  local copies, waits for them, and re-layouts  81.7 us (11%)
  matrix products  64.9 us (9%)
  between operations  17.2 us (2%)
    ppermute x70, waiting for transfers between devices, xor(): return lax.ppermute(x, BOTH, [(i, i ^ mask) for i in range(self.n)])  312 us
    ppermute x70, starting transfers between devices, xor(): return lax.ppermute(x, BOTH, [(i, i ^ mask) for i in range(self.n)])  107 us
    dot_general x6, matrix products, dot_tn(): lax.dot_general(left, right, (((0,), (0,)), ((), ())), preferred_element_...  38.9 us
    pallas_call x1, Pallas kernels, hidden_units(): pl.pallas_call(hidden_kernel, grid=(tokens // tm,), in_specs=[rows, rows,...  33.1 us
    pallas_call x1, Pallas kernels, hidden_back(): pl.pallas_call(back_kernel, grid=(tokens // tm,), in_specs=[rows, rows, w...  23.4 us
    dot_general x3, matrix products, dot_nt(): lax.dot_general(left, right, (((1,), (1,)), ((), ())), preferred_element_...  20 us
    pallas_call x1, Pallas kernels, attend_back(): pl.pallas_call(functools.partial(attend_back_kernel, count, scale), grid_...  19.8 us
    another operation x35, other arithmetic, pair(): jnp.stack([jnp.where(low, mine, theirs), jnp.where(low, theirs, mine)], a...  19.8 us
  transfers between devices with their start and end apart: 82, of which 31 were waited for; matrix products, arithmetic and copies ran while one was open for 26% of the time, Pallas kernels for 5%

profile of v2, /device:TPU:0, one launch (start us, length us, event | category | flops | bytes accessed | tf_op | source)
XLA Modules:
  0.0 759.0 jit_solution(1002336444296997698)
XLA Ops:
  41.9 13.1 %collective-permute-done.12 = bf16[96,2304]{1,0:T(8,128)(2,1)S(1)} collective-permute-done((bf16[96,2304]{1,0:T(8,128)(2,1)S(1)}, bf16[96,2304]{1,0:T(8,128)(2,1)S(1)}, u32[]{:S(2)}, u32[]{:S(2)}) %collective-permute-start.12) | collective-permute-done | bytes 442400 | tf_op jit(solution)/shard_map/ppermute | solution.py:306
  59.3 23.1 %collective-permute-done.13 = bf16[2,96,1152]{2,1,0:T(8,128)(2,1)S(1)} collective-permute-done((bf16[2,96,1152]{2,1,0:T(8,128)(2,1)S(1)}, bf16[2,96,1152]{2,1,0:T(8,128)(2,1)S(1)}, u32[]{:S(2)}, u32[]{:S(2)}) %collective-permute-start.13) | collective-permute-done | bytes 442400 | tf_op jit(solution)/shard_map/ppermute | solution.py:306
  83.7 25.0 %collective-permute-done.14 = bf16[2,2,96,1152]{3,2,0,1:T(8,128)(2,1)S(1)} collective-permute-done((bf16[2,2,96,1152]{3,2,0,1:T(8,128)(2,1)S(1)}, bf16[2,2,96,1152]{3,2,0,1:T(8,128)(2,1)S(1)}, u32[]{:S(2)}, u32[]{:S(2)}) %collective-permute-start.14) | collective-permute-done | bytes 884768 | tf_op jit(solution)/shard_map/ppermute | solution.py:306
  112.1 20.9 %collective-permute-start.5 = (bf16[208,1024]{1,0:T(8,128)(2,1)S(1)}, bf16[208,1024]{1,0:T(8,128)(2,1)S(1)}, u32[]{:S(2)}, u32[]{:S(2)}) collective-permute-start(bf16[208,1024]{1,0:T(8,128)(2,1)S(1)} %slice.363), channel_id=1, source_target_pairs={{0,8},{2,10},{4,12},{6,14},{8,0},{10,2},{12,4},{14,6},{16,24},{18,... | collective-permute-start | bytes 1277960 | tf_op jit(solution)/shard_map/ppermute | solution.py:306
  170.6 15.9 %shard_map.254 = (f32[512,768]{1,0:T(8,128)}, bf16[512,768]{1,0:T(8,128)(2,1)}, f32[6,1,512]{2,1,0:T(1,128)}) custom-call(s32[4]{0:T(128)} %and_convert_fusion.seen, bf16[512,768]{1,0:T(8,128)(2,1)} %copy.101.q_ref, bf16[512,256]{1,0:T(8,128)(2,1)} %pad_maximum_fusion.42.refs_0_, bf16[512,256]{1,0:T(8,128)(2,1)} %collective-permute-done.6.refs_1_, ...), custom_call_target="tpu_custom_call" | custom-call | flops 20132659200 | bytes 3145728 | tf_op jit(solution)/shard_map/pallas_call | solution.py:114
  192.5 13.6 %collective-permute-done.18 = bf16[2,96,1152]{2,1,0:T(8,128)(2,1)S(1)} collective-permute-done((bf16[2,96,1152]{2,1,0:T(8,128)(2,1)S(1)}, bf16[2,96,1152]{2,1,0:T(8,128)(2,1)S(1)}, u32[]{:S(2)}, u32[]{:S(2)}) %collective-permute-start.18) | collective-permute-done | bytes 442400 | tf_op jit(solution)/shard_map/ppermute | solution.py:306
  210.5 25.8 %collective-permute-done.19 = bf16[256,1536]{1,0:T(8,128)(2,1)S(1)} collective-permute-done((bf16[256,1536]{1,0:T(8,128)(2,1)S(1)}, bf16[256,1536]{1,0:T(8,128)(2,1)S(1)}, u32[]{:S(2)}, u32[]{:S(2)}) %collective-permute-start.19) | collective-permute-done | bytes 786464 | tf_op jit(solution)/shard_map/ppermute | solution.py:306
  258.6 10.9 %collective-permute-done.31 = bf16[2,2,2,96,1152]{4,3,0,2,1:T(8,128)(2,1)} collective-permute-done((bf16[2,2,2,96,1152]{4,3,0,2,1:T(8,128)(2,1)}, bf16[2,2,2,96,1152]{4,3,0,2,1:T(8,128)(2,1)}, u32[]{:S(2)}, u32[]{:S(2)}) %collective-permute-start.31) | collective-permute-done | bytes 1769504 | tf_op jit(solution)/shard_map/ppermute | solution.py:306
  286.7 16.7 %collective-permute-done.33 = bf16[2,2,2,96,1152]{4,3,0,2,1:T(8,128)(2,1)S(1)} collective-permute-done((bf16[2,2,2,96,1152]{4,3,0,2,1:T(8,128)(2,1)S(1)}, bf16[2,2,2,96,1152]{4,3,0,2,1:T(8,128)(2,1)S(1)}, u32[]{:S(2)}, u32[]{:S(2)}) %collective-permute-start.33) | collective-permute-done | bytes 1769504 | tf_op jit(solution)/shard_map/ppermute | solution.py:306
  312.4 33.1 %shard_map.255 = (bf16[2048,1152]{1,0:T(8,128)(2,1)}, bf16[2048,1152]{1,0:T(8,128)(2,1)}, bf16[2048,1152]{1,0:T(8,128)(2,1)}) custom-call(bf16[2048,1536]{1,0:T(8,128)(2,1)} %constant_dynamic-update-slice_fusion.2.n_ref, bf16[2048,1536]{1,0:T(8,128)(2,1)} %copy-done.71, bf16[1536,1152]{1,0:T(8,128)(2,1)} %bitcast.307, bf16[1536,1152]{1,0:T(8,128)(2,1)} %bitcast.309, ...), custom_call_target="tpu_custom_call" | custom-call | flops 21743271936 | bytes 24772608 | tf_op jit(solution)/shard_map/pallas_call | solution.py:229
  345.4 11.9 %convolution_convert_fusion.3 = bf16[1536,1152]{1,0:T(8,128)(2,1)S(1)} fusion(bf16[2048,1536]{1,0:T(8,128)(2,1)} %copy-done.71, bf16[2048,1152]{1,0:T(8,128)(2,1)} %get-tuple-element.124), kind=kOutput, calls=%fused_computation.4 | convolution fusion | flops 7249526784 | bytes 14548992 | tf_op jit(solution)/shard_map/dot_general | solution.py:57
  357.4 23.4 %shard_map.256 = bf16[2048,1536]{1,0:T(8,128)(2,1)} custom-call(bf16[2048,1152]{1,0:T(8,128)(2,1)} %get-tuple-element.119.dg_ref, bf16[2048,1152]{1,0:T(8,128)(2,1)} %get-tuple-element.120.du_ref, bf16[1536,1152]{1,0:T(8,128)(2,1)} %bitcast.308, bf16[1536,1152]{1,0:T(8,128)(2,1)} %bitcast.310), custom_call_target="tpu_custom_call" | custom-call | flops 14495514624 | bytes 16515072 | tf_op jit(solution)/shard_map/pallas_call | solution.py:254
  384.0 10.8 %convolution_convert_fusion.2 = bf16[1536,1152]{1,0:T(8,128)(2,1)S(1)} fusion(bf16[2048,1536]{1,0:T(8,128)(2,1)} %constant_dynamic-update-slice_fusion.2.n_ref, bf16[2048,1152]{1,0:T(8,128)(2,1)S(1)} %copy-done.85), kind=kOutput, calls=%fused_computation.3 | convolution fusion | flops 7249526784 | bytes 14548992 | tf_op jit(solution)/shard_map/dot_general | solution.py:57
  395.4 23.9 %collective-permute-done.40 = bf16[2,2,2,96,1152]{4,3,2,1,0:T(8,128)(2,1)S(1)} collective-permute-done((bf16[2,2,2,96,1152]{4,3,2,1,0:T(8,128)(2,1)S(1)}, bf16[2,2,2,96,1152]{4,3,2,1,0:T(8,128)(2,1)S(1)}, u32[]{:S(2)}, u32[]{:S(2)}) %collective-permute-start.40) | collective-permute-done | bytes 1769504 | tf_op jit(solution)/shard_map/ppermute | solution.py:306
  426.8 24.3 %collective-permute-done.44 = bf16[2,2,96,1152]{3,2,1,0:T(8,128)(2,1)} collective-permute-done((bf16[2,2,96,1152]{3,2,1,0:T(8,128)(2,1)}, bf16[2,2,96,1152]{3,2,1,0:T(8,128)(2,1)}, u32[]{:S(2)}, u32[]{:S(2)}) %collective-permute-start.44) | collective-permute-done | bytes 884768 | tf_op jit(solution)/shard_map/ppermute | solution.py:306
  453.9 12.3 %convolution_convert_fusion.1 = bf16[1536,1152]{1,0:T(8,128)(2,1)S(1)} fusion(bf16[2048,1536]{1,0:T(8,128)(2,1)} %constant_dynamic-update-slice_fusion.2.n_ref, bf16[2048,1152]{1,0:T(8,128)(2,1)} %get-tuple-element.120.du_ref), kind=kOutput, calls=%fused_computation.2 | convolution fusion | flops 7249526784 | bytes 14548992 | tf_op jit(solution)/shard_map/dot_general | solution.py:57
  482.4 30.4 %collective-permute-done.45 = bf16[2,2,96,1152]{3,2,1,0:T(8,128)(2,1)} collective-permute-done((bf16[2,2,96,1152]{3,2,1,0:T(8,128)(2,1)}, bf16[2,2,96,1152]{3,2,1,0:T(8,128)(2,1)}, u32[]{:S(2)}, u32[]{:S(2)}) %collective-permute-start.45) | collective-permute-done | bytes 884768 | tf_op jit(solution)/shard_map/ppermute | solution.py:306
  519.8 19.8 %shard_map.257 = (f32[512,768]{1,0:T(8,128)}, f32[512,256]{1,0:T(8,128)}, bf16[512,256]{1,0:T(8,128)(2,1)}, bf16[512,256]{1,0:T(8,128)(2,1)}, bf16[512,256]{1,0:T(8,128)(2,1)}) custom-call(s32[4]{0:T(128)} %and_convert_fusion.seen, bf16[512,768]{1,0:T(8,128)(2,1)} %copy.101.q_ref, bf16[512,768]{1,0:T(8,128)(2,1)} %convolution_convert_fusion.7.g_ref, ...), custom_call_target="tpu_custom_call" | custom-call | flops 30198988800 | bytes 6291456 | tf_op jit(solution)/shard_map/pallas_call | solution.py:186
  566.8 10.9 %convolution_convert_fusion = bf16[2048,1536]{1,0:T(8,128)(2,1)S(1)} fusion(bf16[2048,1152]{1,0:T(8,128)(2,1)} %get-tuple-element.124, bf16[1536,1152]{1,0:T(8,128)(2,1)S(1)} %bitcast.306), kind=kOutput, calls=%fused_computation.1 | convolution fusion | flops 7250903040 | bytes 14548992 | tf_op jit(solution)/shard_map/dot_general | solution.py:61
  628.2 9.3 %collective-permute-done.64 = f32[1,256]{1,0:T(1,128)S(1)} collective-permute-done((f32[1,256]{1,0:T(1,128)S(1)}, f32[1,256]{1,0:T(1,128)S(1)}, u32[]{:S(2)}, u32[]{:S(2)}) %collective-permute-start.64) | collective-permute-done | bytes 1056 | tf_op jit(solution)/shard_map/ppermute | solution.py:306
  643.6 9.2 %collective-permute-done.52 = bf16[384,1536]{1,0:T(8,128)(2,1)S(1)} collective-permute-done((bf16[384,1536]{1,0:T(8,128)(2,1)S(1)}, bf16[384,1536]{1,0:T(8,128)(2,1)S(1)}, u32[]{:S(2)}, u32[]{:S(2)}) %collective-permute-start.52) | collective-permute-done | bytes 1179680 | tf_op jit(solution)/shard_map/ppermute | solution.py:306
  667.8 11.8 %collective-permute-done.54 = bf16[256,1536]{1,0:T(8,128)(2,1)S(1)} collective-permute-done((bf16[256,1536]{1,0:T(8,128)(2,1)S(1)}, bf16[256,1536]{1,0:T(8,128)(2,1)S(1)}, u32[]{:S(2)}, u32[]{:S(2)}) %collective-permute-start.54) | collective-permute-done | bytes 786464 | tf_op jit(solution)/shard_map/ppermute | solution.py:306
  695.9 9.3 %collective-permute-done.72 = bf16[192,1152]{1,0:T(8,128)(2,1)S(1)} collective-permute-done((bf16[192,1152]{1,0:T(8,128)(2,1)S(1)}, bf16[192,1152]{1,0:T(8,128)(2,1)S(1)}, u32[]{:S(2)}, u32[]{:S(2)}) %collective-permute-start.72) | collective-permute-done | bytes 442400 | tf_op jit(solution)/shard_map/ppermute | solution.py:306
  722.6 11.1 %collective-permute-done.76 = bf16[96,1792]{1,0:T(8,128)(2,1)S(1)} collective-permute-done((bf16[96,1792]{1,0:T(8,128)(2,1)S(1)}, bf16[96,1792]{1,0:T(8,128)(2,1)S(1)}, u32[]{:S(2)}, u32[]{:S(2)}) %collective-permute-start.76) | collective-permute-done | bytes 344096 | tf_op jit(solution)/shard_map/ppermute | solution.py:306
  (538 shorter events, 325.4 us)
Async XLA Ops:
  7.2 234.7 %all-gather.2.cloned.1.call-start = ((), (), s32[]{:S(2)}) async-start(), calls=%async_computation | async-start | bytes 2506752 | tf_op jit(solution)/shard_map/all_gather | solution.py:544
  55.7 52.9 %collective-permute-start.14 = (bf16[2,2,96,1152]{3,2,0,1:T(8,128)(2,1)S(1)}, bf16[2,2,96,1152]{3,2,0,1:T(8,128)(2,1)S(1)}, u32[]{:S(2)}, u32[]{:S(2)}) collective-permute-start(bf16[2,2,96,1152]{3,2,0,1:T(8,128)(2,1)S(1)} %pad_maximum_fusion.24), channel_id=1, source_target_pairs={{0,4},{2,6},{4,0},{6,2},{8,12},{10,14},{12,8},{14,10},{16,20},{18,... | collective-permute-start | bytes 2654216 | tf_op jit(solution)/shard_map/ppermute | solution.py:306
  56.2 52.8 %collective-permute-start.3 = (bf16[416,1024]{1,0:T(8,128)(2,1)S(1)}, bf16[416,1024]{1,0:T(8,128)(2,1)S(1)}, u32[]{:S(2)}, u32[]{:S(2)}) collective-permute-start(bf16[416,1024]{1,0:T(8,128)(2,1)S(1)} %bitcast.323), channel_id=1, source_target_pairs={{0,16},{2,18},{4,20},{6,22},{8,24},{10,26},{12,28},{14,30},{16,0},... | collective-permute-start | bytes 2555912 | tf_op jit(solution)/shard_map/ppermute | solution.py:306
  57.6 51.4 %collective-permute-start.2 = (bf16[416,1024]{1,0:T(8,128)(2,1)S(1)}, bf16[416,1024]{1,0:T(8,128)(2,1)S(1)}, u32[]{:S(2)}, u32[]{:S(2)}) collective-permute-start(bf16[416,1024]{1,0:T(8,128)(2,1)S(1)} %bitcast.324), channel_id=1, source_target_pairs={{0,8},{2,10},{4,12},{6,14},{8,0},{10,2},{12,4},{14,6},{16,24},{18,... | collective-permute-start | bytes 2555912 | tf_op jit(solution)/shard_map/ppermute | solution.py:306
  108.7 80.7 %collective-permute-start.15 = (bf16[2,2,96,1152]{3,2,0,1:T(8,128)(2,1)}, bf16[2,2,96,1152]{3,2,0,1:T(8,128)(2,1)}, u32[]{:S(2)}, u32[]{:S(2)}) collective-permute-start(bf16[2,2,96,1152]{3,2,0,1:T(8,128)(2,1)} %pad_maximum_fusion.23), channel_id=1, source_target_pairs={{0,4},{2,6},{4,0},{6,2},{8,12},{10,14},{12,8},{14,10},{16,20},{18,... | collective-permute-start | bytes 2654216 | tf_op jit(solution)/shard_map/ppermute | solution.py:306
  169.6 68.5 %collective-permute-start.30 = (bf16[2,2,2,96,1152]{4,3,0,2,1:T(8,128)(2,1)}, bf16[2,2,2,96,1152]{4,3,0,2,1:T(8,128)(2,1)S(1)}, u32[]{:S(2)}, u32[]{:S(2)}) collective-permute-start(bf16[2,2,2,96,1152]{4,3,0,2,1:T(8,128)(2,1)} %pad_maximum_fusion.7), channel_id=1, source_target_pairs={{0,16},{2,18},{4,20},{6,22},{8,24},{10,26},{12,28},{14,30},{16,0},... | collective-permute-start | bytes 5308424 | tf_op jit(solution)/shard_map/ppermute | solution.py:306
  207.4 38.1 %collective-permute-start.32 = (bf16[2,2,96,1152]{3,2,0,1:T(8,128)(2,1)}, bf16[2,2,96,1152]{3,2,0,1:T(8,128)(2,1)}, u32[]{:S(2)}, u32[]{:S(2)}) collective-permute-start(bf16[2,2,96,1152]{3,2,0,1:T(8,128)(2,1)} %pad_maximum_fusion.25), channel_id=1, source_target_pairs={{0,4},{2,6},{4,0},{6,2},{8,12},{10,14},{12,8},{14,10},{16,20},{18,... | collective-permute-start | bytes 2654216 | tf_op jit(solution)/shard_map/ppermute | solution.py:306
  238.1 31.3 %collective-permute-start.31 = (bf16[2,2,2,96,1152]{4,3,0,2,1:T(8,128)(2,1)}, bf16[2,2,2,96,1152]{4,3,0,2,1:T(8,128)(2,1)}, u32[]{:S(2)}, u32[]{:S(2)}) collective-permute-start(bf16[2,2,2,96,1152]{4,3,0,2,1:T(8,128)(2,1)} %pad_maximum_fusion.8), channel_id=1, source_target_pairs={{0,16},{2,18},{4,20},{6,22},{8,24},{10,26},{12,28},{14,30},{16,0},... | collective-permute-start | bytes 5308424 | tf_op jit(solution)/shard_map/ppermute | solution.py:306
  269.4 34.0 %collective-permute-start.33 = (bf16[2,2,2,96,1152]{4,3,0,2,1:T(8,128)(2,1)S(1)}, bf16[2,2,2,96,1152]{4,3,0,2,1:T(8,128)(2,1)S(1)}, u32[]{:S(2)}, u32[]{:S(2)}) collective-permute-start(bf16[2,2,2,96,1152]{4,3,0,2,1:T(8,128)(2,1)S(1)} %pad_maximum_fusion.9), channel_id=1, source_target_pairs={{0,16},{2,18},{4,20},{6,22},{8,24},{10,26},{12,28},{14,30},{16,0},... | collective-permute-start | bytes 5308424 | tf_op jit(solution)/shard_map/ppermute | solution.py:306
  383.2 36.1 %collective-permute-start.40 = (bf16[2,2,2,96,1152]{4,3,2,1,0:T(8,128)(2,1)S(1)}, bf16[2,2,2,96,1152]{4,3,2,1,0:T(8,128)(2,1)S(1)}, u32[]{:S(2)}, u32[]{:S(2)}) collective-permute-start(bf16[2,2,2,96,1152]{4,3,2,1,0:T(8,128)(2,1)S(1)} %dynamic-slice_bitcast_fusion), channel_id=1, source_target_pairs={{0,16},{2,18},{4,20},{6,22},{8,24},{10,26},{12,28},{14,30},{16,0},... | collective-permute-start | bytes 5308424 | tf_op jit(solution)/shard_map/ppermute | solution.py:306
  383.5 37.4 %collective-permute-start.34 = (bf16[1024,1536]{1,0:T(8,128)(2,1)S(1)}, bf16[1024,1536]{1,0:T(8,128)(2,1)}, u32[]{:S(2)}, u32[]{:S(2)}) collective-permute-start(bf16[1024,1536]{1,0:T(8,128)(2,1)S(1)} %slice.383), channel_id=1, source_target_pairs={{0,1},{1,0},{2,3},{3,2},{4,5},{5,4},{6,7},{7,6},{8,9},{9,8},{10,11... | collective-permute-start | bytes 9437192 | tf_op jit(solution)/shard_map/ppermute | solution.py:327
  420.7 30.4 %collective-permute-start.44 = (bf16[2,2,96,1152]{3,2,1,0:T(8,128)(2,1)}, bf16[2,2,96,1152]{3,2,1,0:T(8,128)(2,1)}, u32[]{:S(2)}, u32[]{:S(2)}) collective-permute-start(bf16[2,2,96,1152]{3,2,1,0:T(8,128)(2,1)} %dynamic-slice_bitcast_fusion.3), channel_id=1, source_target_pairs={{0,4},{2,6},{4,0},{6,2},{8,12},{10,14},{12,8},{14,10},{16,20},{18,... | collective-permute-start | bytes 2654216 | tf_op jit(solution)/shard_map/ppermute | solution.py:306
  420.7 47.1 %collective-permute-start.41 = (bf16[2,2,2,96,1152]{4,3,2,0,1:T(8,128)(2,1)S(1)}, bf16[2,2,2,96,1152]{4,3,2,0,1:T(8,128)(2,1)S(1)}, u32[]{:S(2)}, u32[]{:S(2)}) collective-permute-start(bf16[2,2,2,96,1152]{4,3,2,0,1:T(8,128)(2,1)S(1)} %bitcast.331), channel_id=1, source_target_pairs={{0,16},{2,18},{4,20},{6,22},{8,24},{10,26},{12,28},{14,30},{16,0},... | collective-permute-start | bytes 5308424 | tf_op jit(solution)/shard_map/ppermute | solution.py:306
  472.2 40.5 %collective-permute-start.45 = (bf16[2,2,96,1152]{3,2,1,0:T(8,128)(2,1)}, bf16[2,2,96,1152]{3,2,1,0:T(8,128)(2,1)}, u32[]{:S(2)}, u32[]{:S(2)}) collective-permute-start(bf16[2,2,96,1152]{3,2,1,0:T(8,128)(2,1)} %dynamic-slice_bitcast_fusion.4), channel_id=1, source_target_pairs={{0,4},{2,6},{4,0},{6,2},{8,12},{10,14},{12,8},{14,10},{16,20},{18,... | collective-permute-start | bytes 2654216 | tf_op jit(solution)/shard_map/ppermute | solution.py:306
  475.2 89.7 %collective-permute-start.42 = (bf16[2,2,2,96,1152]{4,3,2,1,0:T(8,128)(2,1)}, bf16[2,2,2,96,1152]{4,3,2,1,0:T(8,128)(2,1)}, u32[]{:S(2)}, u32[]{:S(2)}) collective-permute-start(bf16[2,2,2,96,1152]{4,3,2,1,0:T(8,128)(2,1)} %dynamic-slice_bitcast_fusion.1), channel_id=1, source_target_pairs={{0,16},{2,18},{4,20},{6,22},{8,24},{10,26},{12,28},{14,30},{16,0},... | collective-permute-start | bytes 5308424 | tf_op jit(solution)/shard_map/ppermute | solution.py:306
  482.4 33.1 %collective-permute-start.39 = (bf16[256,1536]{1,0:T(8,128)(2,1)S(1)}, bf16[256,1536]{1,0:T(8,128)(2,1)S(1)}, u32[]{:S(2)}, u32[]{:S(2)}) collective-permute-start(bf16[256,1536]{1,0:T(8,128)(2,1)S(1)} %get-tuple-element.160), channel_id=1, source_target_pairs={{0,1},{1,0},{2,3},{3,2},{4,5},{5,4},{6,7},{7,6},{8,9},{9,8},{10,11... | collective-permute-start | bytes 2359304 | tf_op jit(solution)/shard_map/ppermute | solution.py:327
  541.5 41.6 %collective-permute-start.46 = (bf16[512,256]{1,0:T(8,128)(2,1)}, bf16[512,256]{1,0:T(8,128)(2,1)}, u32[]{:S(2)}, u32[]{:S(2)}) collective-permute-start(bf16[512,256]{1,0:T(8,128)(2,1)} %get-tuple-element.128), channel_id=1, source_target_pairs={{0,2},{2,0},{4,6},{6,4},{8,10},{10,8},{12,14},{14,12},{16,18},{18,... | collective-permute-start | bytes 786440 | tf_op jit(solution)/shard_map/ppermute | solution.py:306
  541.6 41.5 %collective-permute-start.47 = (bf16[512,256]{1,0:T(8,128)(2,1)}, bf16[512,256]{1,0:T(8,128)(2,1)}, u32[]{:S(2)}, u32[]{:S(2)}) collective-permute-start(bf16[512,256]{1,0:T(8,128)(2,1)} %get-tuple-element.130), channel_id=1, source_target_pairs={{0,4},{2,6},{4,0},{6,2},{8,12},{10,14},{12,8},{14,10},{16,20},{18,... | collective-permute-start | bytes 786440 | tf_op jit(solution)/shard_map/ppermute | solution.py:306
  541.7 41.4 %collective-permute-start.48 = (bf16[512,256]{1,0:T(8,128)(2,1)}, bf16[512,256]{1,0:T(8,128)(2,1)}, u32[]{:S(2)}, u32[]{:S(2)}) collective-permute-start(bf16[512,256]{1,0:T(8,128)(2,1)} %get-tuple-element.132), channel_id=1, source_target_pairs={{0,6},{2,4},{4,2},{6,0},{8,14},{10,12},{12,10},{14,8},{16,22},{18,... | collective-permute-start | bytes 786440 | tf_op jit(solution)/shard_map/ppermute | solution.py:306
  563.1 34.8 %collective-permute-start.51 = (bf16[192,1536]{1,0:T(8,128)(2,1)}, bf16[192,1536]{1,0:T(8,128)(2,1)}, u32[]{:S(2)}, u32[]{:S(2)}) collective-permute-start(bf16[192,1536]{1,0:T(8,128)(2,1)} %get-tuple-element.135), channel_id=1, source_target_pairs={{0,8},{2,10},{4,12},{6,14},{8,0},{10,2},{12,4},{14,6},{16,24},{18,... | collective-permute-start | bytes 1769480 | tf_op jit(solution)/shard_map/ppermute | solution.py:306
  583.1 56.3 %collective-permute-start.43 = (bf16[1024,1536]{1,0:T(8,128)(2,1)}, bf16[1024,1536]{1,0:T(8,128)(2,1)}, u32[]{:S(2)}, u32[]{:S(2)}) collective-permute-start(bf16[1024,1536]{1,0:T(8,128)(2,1)} %slice.392), channel_id=1, source_target_pairs={{0,1},{1,0},{2,3},{3,2},{4,5},{5,4},{6,7},{7,6},{8,9},{9,8},{10,11... | collective-permute-start | bytes 9437192 | tf_op jit(solution)/shard_map/ppermute | solution.py:327
  597.0 57.3 %collective-permute-start.71 = (bf16[2,2,96,1152]{3,2,1,0:T(8,128)(2,1)}, bf16[2,2,96,1152]{3,2,1,0:T(8,128)(2,1)}, u32[]{:S(2)}, u32[]{:S(2)}) collective-permute-start(bf16[2,2,96,1152]{3,2,1,0:T(8,128)(2,1)} %dynamic-slice_bitcast_fusion.2), channel_id=1, source_target_pairs={{0,4},{2,6},{4,0},{6,2},{8,12},{10,14},{12,8},{14,10},{16,20},{18,... | collective-permute-start | bytes 2654216 | tf_op jit(solution)/shard_map/ppermute | solution.py:306
  627.4 37.5 %collective-permute-start.66 = (bf16[384,1536]{1,0:T(8,128)(2,1)S(1)}, bf16[384,1536]{1,0:T(8,128)(2,1)S(1)}, u32[]{:S(2)}, u32[]{:S(2)}) collective-permute-start(bf16[384,1536]{1,0:T(8,128)(2,1)S(1)} %copy-done.54), channel_id=1, source_target_pairs={{0,16},{2,18},{4,20},{6,22},{8,24},{10,26},{12,28},{14,30},{16,0},... | collective-permute-start | bytes 3538952 | tf_op jit(solution)/shard_map/ppermute | solution.py:306
  687.9 33.4 %collective-permute-start.56 = (bf16[256,1536]{1,0:T(8,128)(2,1)S(1)}, bf16[256,1536]{1,0:T(8,128)(2,1)S(1)}, u32[]{:S(2)}, u32[]{:S(2)}) collective-permute-start(bf16[256,1536]{1,0:T(8,128)(2,1)S(1)} %fusion.11), channel_id=1, source_target_pairs={{0,1},{1,0},{2,3},{3,2},{4,5},{5,4},{6,7},{7,6},{8,9},{9,8},{10,11... | collective-permute-start | bytes 2359304 | tf_op jit(solution)/shard_map/ppermute | solution.py:327
  (148 other events, 2261.3 us)
Sparse Core Ops, SparseCore 0:
  10.8 91.8 all-gather.1

commit v3 on v2

v3 whole, which is shorter than its diff:
```python
import functools

import jax
import jax.numpy as jnp
from jax import lax
from jax.experimental import pallas as pl
from jax.experimental.pallas import tpu as pltpu
from jax.sharding import PartitionSpec as P

EPSILON = 1e-06
ROPE_BASE = 1000000.0
MASKED = -1e30
LANES = 128
BOTH = ("fsdp", "context")
KERNEL_BYTES = 56 << 20
BF = jnp.bfloat16
F32 = jnp.float32


def tables(positions, head_width):
    ladder = jnp.arange(head_width // 2, dtype=F32)
    inverse = jnp.exp(-jnp.log(ROPE_BASE) * 2.0 * ladder / head_width)
    angles = positions.astype(F32)[:, None] * inverse[None, :]
    cosine, sine = jnp.cos(angles), jnp.sin(angles)
    return (
        jnp.concatenate([cosine, cosine], axis=1),
        jnp.concatenate([-sine, sine], axis=1),
    )


def swap_halves(x):
    middle = x.shape[1] // 2
    return jnp.concatenate([x[:, middle:], x[:, :middle]], axis=1)


def locate(blocks, prompt_slots, block_rows):
    segment = jnp.where(blocks < prompt_slots, 0, blocks - prompt_slots + 1)
    anchor = jnp.where(blocks < prompt_slots, blocks * block_rows, prompt_slots * block_rows)
    return (segment, anchor)


def dot_nn(left, right):
    return lax.dot_general(left, right, (((1,), (0,)), ((), ())), preferred_element_type=F32)


def dot_tn(left, right):
    return lax.dot_general(left, right, (((0,), (0,)), ((), ())), preferred_element_type=F32)


def dot_nt(left, right):
    return lax.dot_general(left, right, (((1,), (1,)), ((), ())), preferred_element_type=F32)


def norm_back(grad_normed, rows_normed, inv_rms, gain):
    grad_rows = grad_normed * gain.astype(F32)
    return inv_rms * (
        grad_rows - rows_normed * jnp.mean(grad_rows * rows_normed, axis=-1, keepdims=True)
    )


def turn(x, cosine, sine):
    return x * cosine + pltpu.roll(x, x.shape[1] // 2, 1) * sine


def attend_kernel(count, scale, seen, lin_ref, cos_ref, sin_ref, *refs):
    pairs = refs[:count]
    q_ref, out_ref, low_ref, lse_ref, peak_ref, total_ref, sum_ref = refs[count:]
    wide = lin_ref.shape[1]
    query = turn(lin_ref[...], cos_ref[...], sin_ref[...]).astype(BF)
    q_ref[...] = query

    def piece(r):
        scores = dot_nt(pairs[r][:, :wide], query) * scale
        if r == 0:
            rows = lax.broadcasted_iota(jnp.int32, scores.shape, 0)
            columns = lax.broadcasted_iota(jnp.int32, scores.shape, 1)
            scores = jnp.where(rows <= columns, scores, MASKED)
            peak = jnp.max(scores, axis=0, keepdims=True)
        else:
            old = peak_ref[...]
            peak = jnp.maximum(old, jnp.max(scores, axis=0, keepdims=True))
        probs = jnp.exp(scores - peak)
        total = jnp.sum(probs, axis=0, keepdims=True)
        mixed = dot_tn(pairs[r][:, wide:], probs.astype(BF))
        if r:
            shrink = jnp.exp(old - peak)
            total = total + total_ref[...] * shrink
            mixed = mixed + sum_ref[...] * shrink
        peak_ref[...] = peak
        total_ref[...] = total
        sum_ref[...] = mixed

    piece(0)
    for r in range(1, count):
        pl.when(seen[r] != 0)(functools.partial(piece, r))
    total = total_ref[...]
    out = jnp.transpose(sum_ref[...] / total)
    out_ref[...] = out
    low_ref[...] = out.astype(BF)
    lse_ref[...] = (peak_ref[...] + jnp.log(total))[None]


def attend(seen, lin, cosine, sine, pairs, heads, scale):
    rows, wide = cosine.shape
    count = len(pairs)
    every = pl.BlockSpec((rows, wide), lambda h, seen: (0, 0))
    head = pl.BlockSpec((rows, wide), lambda h, seen: (0, h))
    whole = pl.BlockSpec(pairs[0].shape, lambda h, seen: (0, 0))
    return pl.pallas_call(
        functools.partial(attend_kernel, count, scale),
        grid_spec=pltpu.PrefetchScalarGridSpec(
            num_scalar_prefetch=1,
            grid=(heads,),
            in_specs=[head, every, every] + [whole] * count,
            out_specs=[head, head, head, pl.BlockSpec((1, 1, rows), lambda h, seen: (h, 0, 0))],
            scratch_shapes=[
                pltpu.VMEM((1, rows), F32),
                pltpu.VMEM((1, rows), F32),
                pltpu.VMEM((wide, rows), F32),
            ],
        ),
        out_shape=[
            jax.ShapeDtypeStruct((rows, heads * wide), BF),
            jax.ShapeDtypeStruct((rows, heads * wide), F32),
            jax.ShapeDtypeStruct((rows, heads * wide), BF),
            jax.ShapeDtypeStruct((heads, 1, rows), F32),
        ],
        compiler_params=pltpu.CompilerParams(vmem_limit_bytes=KERNEL_BYTES),
        cost_estimate=pl.CostEstimate(flops=1, bytes_accessed=1, transcendentals=0),
    )(seen, lin, cosine, sine, *pairs)


def attend_back_kernel(
    count, scale, seen, q_ref, g_ref, out_ref, lse_ref, cos_ref, sin_ref, *refs
):
    pairs = refs[:count]
    dq_ref = refs[count]
    grads = refs[count + 1 : 2 * count + 1]
    held, sum_ref = refs[2 * count + 1 :]
    wide = q_ref.shape[1]
    step = pl.program_id(0)
    query = q_ref[...]
    grad = g_ref[...]
    delta = jnp.sum(grad.astype(F32) * out_ref[...], axis=1, keepdims=True)
    delta = jnp.transpose(jnp.broadcast_to(delta, q_ref.shape))[:1]
    lse = lse_ref[0]

    @pl.when(step == 0)
    def _():
        held[...] = jnp.zeros_like(held)

    def piece(r):
        key = pairs[r][:, :wide]
        probs = jnp.exp(dot_nt(key, query) * scale - lse)
        if r == 0:
            rows = lax.broadcasted_iota(jnp.int32, probs.shape, 0)
            columns = lax.broadcasted_iota(jnp.int32, probs.shape, 1)
            probs = jnp.where(rows <= columns, probs, 0.0)
        grad_scores = (probs * (dot_nt(pairs[r][:, wide:], grad) - delta)).astype(BF)
        held[r, :, wide:] += dot_nn(probs.astype(BF), grad)
        held[r, :, :wide] += dot_nn(grad_scores, query) * scale
        term = dot_tn(key, grad_scores)
        sum_ref[...] = term if r == 0 else sum_ref[...] + term

    piece(0)
    for r in range(1, count):
        pl.when(seen[r] != 0)(functools.partial(piece, r))
    grad_query = jnp.transpose(sum_ref[...]) * scale
    dq_ref[...] = turn(grad_query, cos_ref[...], -sin_ref[...]).astype(BF)

    @pl.when(step == pl.num_programs(0) - 1)
    def _():
        for r in range(count):
            grads[r][...] = held[r].astype(grads[r].dtype)


def attend_back(seen, queries, grads, outs, lse, cosine, sine, pairs, heads, scale):
    rows = queries.shape[0]
    wide = queries.shape[1] // heads
    count = len(pairs)
    head = pl.BlockSpec((rows, wide), lambda h, seen: (0, h))
    whole = pl.BlockSpec(pairs[0].shape, lambda h, seen: (0, 0))
    results = pl.pallas_call(
        functools.partial(attend_back_kernel, count, scale),
        grid_spec=pltpu.PrefetchScalarGridSpec(
            num_scalar_prefetch=1,
            grid=(heads,),
            in_specs=[head] * 3
            + [pl.BlockSpec((1, 1, rows), lambda h, seen: (h, 0, 0))]
            + [pl.BlockSpec((rows, wide), lambda h, seen: (0, 0))] * 2
            + [whole] * count,
            out_specs=[head] + [whole] * count,
            scratch_shapes=[
                pltpu.VMEM((count,) + pairs[0].shape, F32),
                pltpu.VMEM((wide, rows), F32),
            ],
        ),
        out_shape=[jax.ShapeDtypeStruct(queries.shape, BF)]
        + [jax.ShapeDtypeStruct(pairs[0].shape, F32 if r == 0 else BF) for r in range(count)],
        compiler_params=pltpu.CompilerParams(vmem_limit_bytes=KERNEL_BYTES),
        cost_estimate=pl.CostEstimate(flops=1, bytes_accessed=1, transcendentals=0),
    )(seen, queries, grads, outs, lse, cosine, sine, *pairs)
    return results[0], results[1:]


def products_kernel(a_ref, b_ref, c_ref, d_ref, out_ref):
    wide = b_ref.shape[1]
    out_ref[:, :wide] = dot_tn(a_ref[...], b_ref[...]).astype(BF)
    out_ref[:, wide:] = dot_tn(c_ref[...], d_ref[...]).astype(BF)


def products(a, b, c, d):
    tokens, depth = a.shape
    tile = depth // 3 if depth % (3 * LANES) == 0 else depth
    left = pl.BlockSpec((tokens, tile), lambda m: (0, m))
    right = pl.BlockSpec(b.shape, lambda m: (0, 0))
    return pl.pallas_call(
        products_kernel,
        grid=(depth // tile,),
        in_specs=[left, right, left, right],
        out_specs=pl.BlockSpec((tile, 2 * b.shape[1]), lambda m: (m, 0)),
        out_shape=jax.ShapeDtypeStruct((depth, 2 * b.shape[1]), BF),
        compiler_params=pltpu.CompilerParams(vmem_limit_bytes=KERNEL_BYTES),
        cost_estimate=pl.CostEstimate(flops=1, bytes_accessed=1, transcendentals=0),
    )(a, b, c, d)


def hidden_kernel(n_ref, wg_ref, wu_ref, act_ref, by_gate_ref, by_up_ref):
    gate = dot_nn(n_ref[...], wg_ref[...])
    up = dot_nn(n_ref[...], wu_ref[...])
    sigmoid = jax.nn.sigmoid(gate)
    silu = gate * sigmoid
    act_ref[...] = (silu * up).astype(BF)
    by_gate_ref[...] = (up * (sigmoid + silu * (1.0 - sigmoid))).astype(BF)
    by_up_ref[...] = silu.astype(BF)


def hidden_units(normed, gate_w, up_w):
    tokens, depth = normed.shape
    units = gate_w.shape[1]
    tm = min(tokens, 256)
    rows = pl.BlockSpec((tm, depth), lambda m: (m, 0))
    weight = pl.BlockSpec((depth, units), lambda m: (0, 0))
    out = pl.BlockSpec((tm, units), lambda m: (m, 0))
    return pl.pallas_call(
        hidden_kernel,
        grid=(tokens // tm,),
        in_specs=[rows, weight, weight],
        out_specs=[out] * 3,
        out_shape=[jax.ShapeDtypeStruct((tokens, units), BF)] * 3,
        compiler_params=pltpu.CompilerParams(vmem_limit_bytes=KERNEL_BYTES),
        cost_estimate=pl.CostEstimate(flops=1, bytes_accessed=1, transcendentals=0),
    )(normed, gate_w, up_w)


def hidden_grad_kernel(d_ref, wd_ref, by_gate_ref, by_up_ref, dg_ref, du_ref):
    grad = dot_nn(d_ref[...], wd_ref[...])
    dg_ref[...] = (grad * by_gate_ref[...].astype(F32)).astype(BF)
    du_ref[...] = (grad * by_up_ref[...].astype(F32)).astype(BF)


def hidden_grads(grads, down_w, by_gate, by_up):
    tokens, depth = grads.shape
    units = down_w.shape[1]
    tm = min(tokens, 256)
    out = pl.BlockSpec((tm, units), lambda m: (m, 0))
    return pl.pallas_call(
        hidden_grad_kernel,
        grid=(tokens // tm,),
        in_specs=[
            pl.BlockSpec((tm, depth), lambda m: (m, 0)),
            pl.BlockSpec((depth, units), lambda m: (0, 0)),
            out,
            out,
        ],
        out_specs=[out] * 2,
        out_shape=[jax.ShapeDtypeStruct((tokens, units), BF)] * 2,
        compiler_params=pltpu.CompilerParams(vmem_limit_bytes=KERNEL_BYTES),
        cost_estimate=pl.CostEstimate(flops=1, bytes_accessed=1, transcendentals=0),
    )(grads, down_w, by_gate, by_up)


def back_kernel(count, half, *refs):
    lefts, rights = refs[:count], refs[count : 2 * count]
    first, second = refs[2 * count :]
    total = dot_nt(lefts[0][...], rights[0][...])
    for left, right in zip(lefts[1:], rights[1:]):
        total = total + dot_nt(left[...], right[...])
    step = pl.program_id(0)

    @pl.when(step < half)
    def _():
        first[...] = total.astype(BF)

    @pl.when(step >= half)
    def _():
        second[...] = total.astype(BF)


def hidden_back(lefts, rights):
    tokens, units = lefts[0].shape
    depth = rights[0].shape[0]
    count = len(lefts)
    tm = min(tokens // 2, 512)
    half = tokens // 2 // tm
    rows = pl.BlockSpec((tm, units), lambda m: (m, 0))
    weight = pl.BlockSpec((depth, units), lambda m: (0, 0))
    return pl.pallas_call(
        functools.partial(back_kernel, count, half),
        grid=(tokens // tm,),
        in_specs=[rows] * count + [weight] * count,
        out_specs=[
            pl.BlockSpec((tm, depth), lambda m: (jnp.minimum(m, half - 1), 0)),
            pl.BlockSpec((tm, depth), lambda m: (jnp.maximum(m - half, 0), 0)),
        ],
        out_shape=[jax.ShapeDtypeStruct((tokens // 2, depth), BF)] * 2,
        compiler_params=pltpu.CompilerParams(vmem_limit_bytes=KERNEL_BYTES),
        cost_estimate=pl.CostEstimate(flops=1, bytes_accessed=1, transcendentals=0),
    )(*lefts, *rights)


def after(x, *earlier):
    return lax.optimization_barrier((x,) + earlier)[0]


class Pending:
    def __init__(self, got, finish):
        self.got = got
        self.finish = finish


class Grid:
    def __init__(self):
        self.nf = lax.axis_size("fsdp")
        self.nc = lax.axis_size("context")
        self.n = self.nf * self.nc
        self.cbits = self.nc.bit_length() - 1
        self.fbits = self.nf.bit_length() - 1
        self.me = lax.axis_index("fsdp") * self.nc + lax.axis_index("context")
        self.my_slot = lax.axis_index("context")
        self.core = lax.axis_index("tensor")
        self.done = ()
        self.zm = 1
        self.xm = self.nc
        self.deep = list(range(1, self.cbits)) + list(range(self.cbits + 1, self.cbits + self.fbits))

    def bit(self, b):
        return (self.me >> b) & 1

    def fence(self, *xs):
        return lax.optimization_barrier(xs + self.done)[: len(xs)]

    def close(self, *xs):
        raw = lax.optimization_barrier(
            tuple(x.got if isinstance(x, Pending) else x for x in xs)
        )
        self.done = raw
        outs = [x.finish(r) if isinstance(x, Pending) else r for x, r in zip(xs, raw)]
        return outs[0] if len(outs) == 1 else outs

    def one(self, x, mask, pin=()):
        if pin:
            x = after(x, *pin)
        return lax.ppermute(x, BOTH, [(i, i ^ mask) for i in range(self.n)])

    def swap(self, x):
        return lax.ppermute(x, "tensor", [(0, 1), (1, 0)])

    def pair(self, b, mine, theirs, axis):
        low = self.bit(b) == 0
        return jnp.stack([jnp.where(low, mine, theirs), jnp.where(low, theirs, mine)], axis)

    def ordered(self, pieces, bits):
        if len(bits) == 0:
            return pieces[0]
        half = len(pieces) // 2
        low = self.ordered(pieces[:half], bits[:-1])
        high = self.ordered(pieces[half:], bits[:-1])
        return self.pair(bits[-1], low, high, 0)

    def fsdp_take(self, x, r):
        x = x.reshape(self.nf, -1, x.shape[1])
        return lax.dynamic_index_in_dim(x, lax.axis_index("fsdp") ^ r, 0, keepdims=False)

    def fsdp_far(self, x):
        far = self.fsdp_take(x, 3)
        cut = far.shape[0] // 2
        return far[:cut], far[cut:]

    def fsdp_near(self, x, by_y, by_x):
        px, py = self.fsdp_take(x, 1), self.fsdp_take(x, 2)
        cut = px.shape[0] // 2
        px = jnp.concatenate([px[:cut].astype(F32) + by_y.astype(F32), px[cut:].astype(F32)], 0)
        py = jnp.concatenate([py[:cut].astype(F32), py[cut:].astype(F32) + by_x.astype(F32)], 0)
        return px.astype(BF), py.astype(BF)

    def fsdp_end(self, x, rx, ry):
        return (self.fsdp_take(x, 0).astype(F32) + rx.astype(F32) + ry.astype(F32)).astype(BF)

    def over_x(self, x):
        return self.one(x, self.xm)

    def over_y(self, x):
        return self.one(x, 2 * self.xm)

    def over_z(self, x):
        return self.one(x, self.zm)

    def context_pick(self, x, r):
        x = x.reshape(self.nc, -1, x.shape[1])
        return lax.dynamic_index_in_dim(x, self.my_slot ^ r, 0, keepdims=False)

    def scatter_context(self, x):
        gives = self.fence(*[self.context_pick(x, r) for r in range(1, self.nc)])
        total = self.context_pick(x, 0).astype(F32)
        for r in range(1, self.nc):
            total = total + self.one(gives[r - 1], r).astype(F32)
        return total

    def tokens_near(self, x, pin_x=(), pin_z=()):
        return self.one(x, self.xm, pin_x), self.one(x, self.zm, pin_z)

    def tokens_far(self, nears):
        cut = nears[0][0].shape[0] // 2
        by_z = self.one(jnp.concatenate([px[:cut] for px, _ in nears], 0), self.zm)
        by_x = self.one(jnp.concatenate([pz[cut:] for _, pz in nears], 0), self.xm)
        parts = []
        for k, (px, pz) in enumerate(nears):
            here = slice(k * cut, (k + 1) * cut)
            parts.append(jnp.concatenate([px, pz, by_z[here], by_x[here]], 0))
        return parts

    def tokens_split(self, part, other):
        rows = part.shape[0] // 4
        cut = rows // 2
        here = [slice(k * rows, (k + 1) * rows) for k in range(4)]
        own, px, pz, far = [part[k].astype(F32) + other[k].astype(F32) for k in here]
        return own, px, pz, far[:cut].astype(BF), far[cut:].astype(BF)

    def tokens_add(self, px, pz, by_z, by_x):
        cut = by_z.shape[0]
        px = jnp.concatenate([px[:cut] + by_z.astype(F32), px[cut:]], 0).astype(BF)
        pz = jnp.concatenate([pz[:cut], pz[cut:] + by_x.astype(F32)], 0).astype(BF)
        return px, pz

    def quarter_masks(self):
        return (0, self.zm, self.xm, self.xm + self.zm)

    def my_quarter(self):
        return 2 * self.bit(self.cbits) + self.bit(0)

    def quarter_groups(self):
        masks = (0, self.zm, self.xm, self.xm + self.zm)
        return [[i | m for m in masks] for i in range(self.n) if i & masks[3] == 0]

    def quarters_in(self, w):
        return lax.all_to_all(w, BOTH, 0, 0, axis_index_groups=self.quarter_groups())

    def quarters_out(self, g):
        return lax.all_to_all(g, BOTH, 0, 0, axis_index_groups=self.quarter_groups())

    def deepen(self, w, held, bits):
        for b in bits[:-1]:
            w = self.pair(b, w, self.one(w, 1 << b), sum(1 for h in held if h > b))
            held.append(b)
        b = bits[-1]
        axis = sum(1 for h in held if h > b)
        held.append(b)
        return Pending(self.one(w, 1 << b), lambda got: self.pair(b, w, got, axis))

    def fold(self, g, held, bits):
        def step(g, b):
            axis = held.index(b)
            held.remove(b)
            give = lax.dynamic_index_in_dim(g, 1 - self.bit(b), axis, keepdims=False)
            keep = lax.dynamic_index_in_dim(g, self.bit(b), axis, keepdims=False)
            finish = lambda got: (keep.astype(F32) + got.astype(F32)).astype(BF)
            return Pending(self.one(give, 1 << b), finish)

        for b in bits[:-1]:
            pending = step(g, b)
            g = pending.finish(pending.got)
        return step(g, bits[-1])


def on_device(
    tokens,
    block_order,
    norm_one,
    w_query,
    b_query,
    w_key,
    b_key,
    w_value,
    b_value,
    w_out,
    norm_two,
    w_gate,
    w_up,
    w_down,
    cotangent,
):
    grid = Grid()
    block_rows, width = tokens.shape
    shard = norm_one.shape[0]
    slot_count = grid.nc
    prompt_slots = slot_count // 2
    head_width = w_key.shape[1]
    query_width = w_query.shape[1]
    head_group = query_width // head_width
    score_scale = head_width ** (-0.5)
    cores = lax.axis_size("tensor")
    own_rows = block_rows // cores
    owners = block_order[0]
    my_block = lax.dynamic_index_in_dim(owners, grid.my_slot, 0, keepdims=False)
    query_anchor = locate(my_block, prompt_slots, block_rows)[1]
    query_pos = query_anchor + jnp.arange(block_rows)

    def own(x):
        return lax.dynamic_slice(x, (grid.core * own_rows, 0), (own_rows, x.shape[1]))

    def others(x):
        return lax.dynamic_slice(x, ((1 - grid.core) * own_rows, 0), (own_rows, x.shape[1]))

    def both(x):
        other = grid.swap(x)
        first = grid.core == 0
        return jnp.concatenate([jnp.where(first, x, other), jnp.where(first, other, x)], 0)

    def summed(part):
        give = lax.dynamic_slice(part, ((1 - grid.core) * own_rows, 0), (own_rows, width))
        return own(part) + grid.swap(give.astype(BF)).astype(F32)

    bias_shard = b_query.shape[1]
    small_bias = b_key.shape[1]
    vector = jnp.concatenate([norm_one[None], norm_two[None], b_query, b_key, b_value], axis=1)
    columns = query_width + 2 * head_width
    vector = jnp.pad(vector, ((0, 7), (0, columns - vector.shape[1])))
    packed = jnp.concatenate(
        [jnp.concatenate([w_query, w_key, w_value], axis=1), vector], axis=0
    )
    hidden = w_gate.shape[1]
    quarter = -(-hidden // (4 * LANES)) * LANES
    pad = ((0, 0), (0, 4 * quarter - hidden))
    w_out_t = lax.all_gather(w_out.T, BOTH, axis=0, tiled=True)

    context_deep = [b for b in grid.deep if b < grid.cbits]
    fsdp_deep = [b for b in grid.deep if b > grid.cbits]

    def quarters(w):
        return w.reshape(shard, 4, quarter).transpose(1, 0, 2)

    def deep_z(w):
        return grid.deepen(w, [0], context_deep)

    def deep_y(w):
        return grid.deepen(w, [0] + context_deep, fsdp_deep)

    def whole(halves):
        return jnp.stack(halves, len(fsdp_deep)).reshape(grid.n * shard, quarter)

    held = []
    gate_near = grid.quarters_in(quarters(jnp.pad(w_gate, pad)))
    packed = grid.deepen(packed, held, context_deep[::-1])
    gate_near, packed = grid.close(gate_near, packed)

    gate_near = gate_near.reshape(2, 2, shard, quarter)
    packed = grid.close(grid.deepen(packed, held, [0]))

    packed = packed.reshape(grid.nc * (shard + 8), columns)
    (gate_0,) = grid.fence(gate_near[0])
    gx, gy, gate_0 = grid.close(grid.over_x(packed), grid.over_y(packed), deep_z(gate_0))

    cut = gx.shape[0] // 2
    gate_1, up_in = grid.fence(gate_near[1], quarters(jnp.pad(w_up, pad)))
    by_y, by_x = grid.over_y(gx[:cut]), grid.over_x(gy[cut:])
    by_y, by_x, gate_1, up_near = grid.close(
        by_y, by_x, deep_z(gate_1), grid.quarters_in(up_in)
    )

    up_near = up_near.reshape(2, 2, shard, quarter)
    pieces = [packed, gx, gy, jnp.concatenate([by_y, by_x], 0)]
    pieces = [x.reshape(grid.nc, shard + 8, columns) for x in pieces]
    sources = [grid.cbits, grid.cbits + 1]
    w_qkv = grid.ordered([x[:, :shard] for x in pieces], sources)
    w_qkv = w_qkv.reshape(grid.n * shard, columns)
    vectors = grid.ordered([x[:, shard] for x in pieces], sources).reshape(grid.n, columns)
    gain_one = vectors[:, :shard].reshape(-1)
    gain_two = vectors[:, shard : 2 * shard].reshape(-1)
    start = 2 * shard
    bias = jnp.concatenate(
        [
            vectors[:, start : start + bias_shard].reshape(-1),
            vectors[:, start + bias_shard : start + bias_shard + small_bias].reshape(-1),
            vectors[
                :, start + bias_shard + small_bias : start + bias_shard + 2 * small_bias
            ].reshape(-1),
        ]
    ).astype(F32)

    inputs = tokens.astype(F32)
    inv_one = lax.rsqrt(jnp.mean(inputs * inputs, axis=-1, keepdims=True) + EPSILON)
    rows_one = inputs * inv_one
    normed_one = (rows_one * gain_one.astype(F32)).astype(BF)
    cosine, sine = tables(query_pos, head_width)
    grads_own, grads_other = own(cotangent), others(cotangent)
    gate_0, grads_pz = grid.fence(gate_0, grads_own)
    gate_0, grads_pz = deep_y(gate_0), grid.over_z(grads_pz)
    qkv = dot_nn(normed_one, w_qkv) + bias
    keys = qkv[:, query_width : query_width + head_width]
    keys = keys * cosine + swap_halves(keys) * sine
    pair = jnp.concatenate([keys, qkv[:, query_width + head_width :]], axis=1).astype(BF)
    pair, qkv, gate_0, grads_pz = grid.close(pair, qkv, gate_0, grads_pz)

    gate_1, grads_px = grid.fence(gate_1, grads_own)
    met = [grid.one(pair, r) for r in range(1, slot_count)]
    gate_1, grads_px, *met = grid.close(deep_y(gate_1), grid.over_x(grads_px), *met)
    pairs = [pair] + met

    piece_block = owners[grid.my_slot ^ jnp.arange(slot_count)]
    seen = ((piece_block < prompt_slots) & (piece_block < my_block)).astype(jnp.int32)
    up_0, down_in = grid.fence(up_near[0], quarters(jnp.pad(w_down.T, pad)))
    up_0, down_near = deep_z(up_0), grid.quarters_in(down_in)
    queries, attn_heads, out_low, log_total = attend(
        seen, qkv, cosine, sine, pairs, head_group, score_scale
    )
    out_low, up_0, down_near = grid.close(out_low, up_0, down_near)

    down_near = down_near.reshape(2, 2, shard, quarter)
    hidden_one = own(tokens).astype(F32) + summed(dot_nt(out_low, w_out_t))

    inv_two = lax.rsqrt(jnp.mean(hidden_one * hidden_one, axis=-1, keepdims=True) + EPSILON)
    rows_two = hidden_one * inv_two
    normed_two = (rows_two * gain_two.astype(F32)).astype(BF)
    normed_two = grid.close(normed_two)

    up_0, up_1 = grid.fence(up_0, up_near[1])
    px, pz, normed_other, up_1, up_0 = grid.close(
        grid.over_x(normed_two),
        grid.over_z(normed_two),
        grid.swap(normed_two),
        deep_z(up_1),
        deep_y(up_0),
    )

    cut = px.shape[0] // 2
    (down_0,) = grid.fence(down_near[0])
    by_z, by_x, up_1, down_0 = grid.close(
        grid.over_z(px[:cut]), grid.over_x(pz[cut:]), deep_y(up_1), deep_z(down_0)
    )

    normed_got = jnp.concatenate([px, pz, by_z, by_x], 0)
    gate_0, gate_1, up_0 = grid.fence(gate_0, gate_1, up_0)
    gate_full, up_full = whole([gate_0, gate_1]), whole([up_0, up_1])
    normed_far, gate_full, up_full = grid.close(grid.swap(normed_got), gate_full, up_full)

    normed_in = jnp.concatenate([normed_two, normed_got, normed_other, normed_far], 0)
    far_z, far_x, down_0, down_1 = grid.fence(
        grads_px[:cut], grads_pz[cut:], down_0, down_near[1]
    )
    by_z, by_x = grid.over_z(far_z), grid.over_x(far_x)
    down_0, down_1 = deep_y(down_0), deep_z(down_1)
    act, by_gate, by_up = hidden_units(normed_in, gate_full, up_full)
    act, by_z, by_x, down_0, down_1 = grid.close(act, by_z, by_x, down_0, down_1)

    grads_got = jnp.concatenate([grads_px, grads_pz, by_z, by_x], 0)
    down_1 = deep_y(down_1)
    grads_in = jnp.concatenate(
        [grads_own, grads_got, grads_other, grid.swap(grads_got)], 0
    )
    grad_wdown = dot_tn(grads_in, act).astype(BF)
    grad_wdown, down_1 = grid.close(grad_wdown, down_1)

    top = sorted(range(grid.cbits + grid.fbits), reverse=True)
    shape = (2,) * len(top) + (shard, quarter)
    y_back, z_back = fsdp_deep[::-1], context_deep[::-1]

    def half(grad, h):
        return lax.index_in_dim(grad.reshape(shape), h, top.index(grid.cbits), keepdims=False)

    def fold_y(grad):
        return grid.fold(grad, [b for b in top if b != grid.cbits], y_back)

    def fold_z(grad):
        return grid.fold(grad, [b for b in top if b not in fsdp_deep and b != grid.cbits], z_back)

    def joined(first, second):
        return jnp.stack([first, second], 0).reshape(4, shard, quarter)

    down_full = whole([down_0, down_1])
    down_0 = fold_y(half(grad_wdown, 0))
    grad_gate, grad_up = hidden_grads(grads_in, down_full, by_gate, by_up)
    down_0, grad_gate, grad_up = grid.close(down_0, grad_gate, grad_up)

    (down_1,) = grid.fence(half(grad_wdown, 1))
    down_0, down_1 = fold_z(down_0), fold_y(down_1)
    part, give = hidden_back((grad_gate, grad_up), (gate_full, up_full))
    down_0, down_1, part, give = grid.close(down_0, down_1, part, give)

    other = grid.swap(give)
    (up_in,) = grid.fence(grad_up)
    grad_wup = dot_tn(normed_in, up_in).astype(BF)
    other, grad_wup = grid.close(other, grad_wup)

    part_own, px, pz, far_z, far_x = grid.tokens_split(part, other)
    down_1, gate_in = grid.fence(down_1, grad_gate)
    by_z, by_x = grid.over_z(far_z), grid.over_x(far_x)
    down_1, up_0 = fold_z(down_1), fold_y(half(grad_wup, 0))
    grad_wgate = dot_tn(normed_in, gate_in).astype(BF)
    by_z, by_x, down_1, up_0, grad_wgate = grid.close(by_z, by_x, down_1, up_0, grad_wgate)

    px, pz = grid.tokens_add(px, pz, by_z, by_x)
    up_1, act_in = grid.fence(half(grad_wup, 1), act)
    px, pz = grid.over_x(px), grid.over_z(pz)
    up_0, up_1 = fold_z(up_0), fold_y(up_1)
    mlp_part, mlp_give = hidden_back((act_in,), (down_full,))
    px, pz, up_0, up_1, mlp_part, mlp_give = grid.close(
        px, pz, up_0, up_1, mlp_part, mlp_give
    )

    (down_in,) = grid.fence(joined(down_0, down_1))
    grad_wdown = grid.quarters_out(down_in)
    mlp_other = grid.swap(mlp_give)
    grad_normed_two = part_own + px.astype(F32) + pz.astype(F32)
    grad_gain_two = jnp.sum(grad_normed_two * rows_two, axis=0)
    grad_hidden_one = own(cotangent).astype(F32) + norm_back(
        grad_normed_two, rows_two, inv_two, gain_two
    )
    grad_low = both(grad_hidden_one.astype(BF))
    grad_heads = dot_nn(grad_low, w_out_t).astype(BF)
    grad_heads, mlp_other, grad_wdown = grid.close(grad_heads, mlp_other, grad_wdown)

    mlp_own, mx, mz, far_z, far_x = grid.tokens_split(mlp_part, mlp_other)
    gate_0, up_1 = grid.fence(half(grad_wgate, 0), up_1)
    by_z, by_x = grid.over_z(far_z), grid.over_x(far_x)
    gate_0, up_1 = fold_y(gate_0), fold_z(up_1)
    grad_query, grad_pairs = attend_back(
        seen,
        queries,
        grad_heads,
        attn_heads,
        log_total,
        cosine,
        sine,
        pairs,
        head_group,
        score_scale,
    )
    by_z, by_x, gate_0, up_1, grad_query, *grad_pairs = grid.close(
        by_z, by_x, gate_0, up_1, grad_query, *grad_pairs
    )

    grad_got = [grid.one(x, r + 1) for r, x in enumerate(grad_pairs[1:])]
    mx, mz = grid.tokens_add(mx, mz, by_z, by_x)
    (gate_1,) = grid.fence(half(grad_wgate, 1))
    mx, gate_1 = grid.over_x(mx), fold_y(gate_1)
    grad_attn = products(normed_one, grad_query, grad_low, out_low)
    mx, gate_1, grad_attn, *grad_got = grid.close(mx, gate_1, grad_attn, *grad_got)

    far_y, far_x = grid.fsdp_far(grad_attn)
    mz, grad_query = grid.fence(mz, grad_query)
    by_y, by_x = grid.over_y(far_y), grid.over_x(far_x)
    gate_0, mz = fold_z(gate_0), grid.over_z(mz)
    grad_pair = grad_pairs[0]
    for x in grad_got:
        grad_pair = grad_pair + x.astype(F32)
    grad_keys = grad_pair[:, :head_width]
    grad_keys = grad_keys * cosine - swap_halves(grad_keys) * sine
    grad_kv = jnp.concatenate([grad_keys, grad_pair[:, head_width:]], axis=1).astype(BF)
    grad_qkv = jnp.concatenate([grad_query, grad_kv], axis=1)
    grad_bias = jnp.sum(grad_qkv.astype(F32), axis=0)
    grad_normed_one = summed(dot_nt(grad_qkv, w_qkv))
    rows_own = own(rows_one)
    inv_own = own(inv_one)
    grad_gain_one = jnp.sum(grad_normed_one * rows_own, axis=0)
    gains = jnp.concatenate(
        [grad_gain_one.reshape(-1, shard), grad_gain_two.reshape(-1, shard)], axis=1
    )
    gains = gains + grid.swap(gains)
    small = jnp.concatenate(
        [
            gains,
            grad_bias[:query_width].reshape(-1, bias_shard),
            grad_bias[query_width : query_width + head_width].reshape(-1, small_bias),
            grad_bias[query_width + head_width :].reshape(-1, small_bias),
        ],
        axis=1,
    )
    wide = 2 * head_width
    small = jnp.pad(small[:, None], ((0, 0), (0, 7), (0, max(wide - small.shape[1], 0))))
    grad_wkv = dot_tn(normed_one, grad_kv).reshape(grid.n, shard, wide)
    grad_wkv = jnp.concatenate([grad_wkv, small], axis=1).astype(BF)
    grad_wkv = grad_wkv.reshape(grid.n * (shard + 8), wide)
    by_y, by_x, gate_0, mz, grad_wkv, grad_normed_one = grid.close(
        by_y, by_x, gate_0, mz, grad_wkv, grad_normed_one
    )

    ax, ay = grid.fsdp_near(grad_attn, by_y, by_x)
    far_y, far_x = grid.fsdp_far(grad_wkv)
    (gate_1,) = grid.fence(gate_1)
    ax, ay = grid.over_x(ax), grid.over_y(ay)
    by_y, by_x, gate_1 = grid.over_y(far_y), grid.over_x(far_x), fold_z(gate_1)
    grad_inputs = grad_hidden_one + norm_back(grad_normed_one, rows_own, inv_own, gain_one)
    result = (hidden_one + mlp_own + mx.astype(F32) + mz.astype(F32)).astype(BF)
    ax, ay, by_y, by_x, gate_1, grad_tokens, result = grid.close(
        ax, ay, by_y, by_x, gate_1, grad_inputs.astype(BF), result
    )

    kx, ky = grid.fsdp_near(grad_wkv, by_y, by_x)
    (up_in,) = grid.fence(joined(up_0, up_1))
    kx, ky = grid.over_x(kx), grid.over_y(ky)
    grad_wup = grid.quarters_out(up_in)
    grad_tokens = both(grad_tokens)
    kx, ky, grad_wup = grid.close(kx, ky, grad_wup)

    (gate_in,) = grid.fence(joined(gate_0, gate_1))
    grad_wgate = grid.quarters_out(gate_in)
    grad_attn = grid.fsdp_end(grad_attn, ax, ay)
    grad_wkv = grid.fsdp_end(grad_wkv, kx, ky)
    grad_attn = jnp.pad(
        grad_attn.reshape(-1, shard, 2 * query_width), ((0, 0), (0, 8), (0, 0))
    )
    grad_attn = jnp.concatenate([grad_attn, grad_wkv.reshape(-1, shard + 8, wide)], axis=2)
    grad_attn = grid.scatter_context(grad_attn.reshape(-1, 2 * query_width + wide))
    result = both(result)
    small = grad_attn[shard : shard + 1, 2 * query_width :]
    grad_attn = grad_attn[:shard]
    grad_wdown, grad_wup, grad_wgate = [
        g.transpose(1, 0, 2).reshape(shard, 4 * quarter).astype(F32)
        for g in (grad_wdown, grad_wup, grad_wgate)
    ]
    grad_wkv = grad_attn[:, 2 * query_width :]
    return (
        result,
        grad_tokens,
        small[0, :shard],
        grad_attn[:, :query_width],
        small[:, start : start + bias_shard],
        grad_wkv[:, :head_width],
        small[:, start + bias_shard : start + bias_shard + small_bias],
        grad_wkv[:, head_width:],
        small[:, start + bias_shard + small_bias : start + bias_shard + 2 * small_bias],
        grad_attn[:, query_width : 2 * query_width].T,
        small[0, shard : 2 * shard],
        grad_wgate[:, :hidden],
        grad_wup[:, :hidden],
        grad_wdown[:, :hidden].T,
    )


def solution(mesh):
    rows = P(("fsdp", "context"), None)
    split = P(("fsdp", "context"))
    into = P(("fsdp", "context"), "tensor")
    back = P("tensor", ("fsdp", "context"))
    return jax.shard_map(
        on_device,
        mesh=mesh,
        in_specs=(
            rows,
            P("fsdp", None),
            split,
            into,
            back,
            into,
            back,
            into,
            back,
            back,
            split,
            into,
            into,
            back,
            rows,
        ),
        out_specs=(
            rows,
            rows,
            split,
            into,
            back,
            into,
            back,
            into,
            back,
            back,
            split,
            into,
            into,
            back,
        ),
        check_vma=False,
    )
```

time: 763 us -> 684 us (0.90)
  waiting for transfers between devices: 313 us -> 229 us
  matrix products: 64.9 us -> 44.6 us
  local copies, waits for them, and re-layouts: 81.7 us -> 61.7 us
  Pallas kernels: 92.1 us -> 112 us
  other arithmetic: 82.5 us -> 92.5 us
  starting transfers between devices: 108 us -> 118 us
    ppermute x70 -> x63, waiting for transfers between devices: 312 us -> 220 us  [one(): return lax.ppermute(x, BOTH, [(i, i ^ mask) for i in range(self.n)])]
    pallas_call x2 -> x5, Pallas kernels: 56.5 us -> 83.9 us  [the longest x2 37.2 us: hidden_back(): pl.pallas_call(functools.partial(back_kernel, count, half), grid=(tokens...]
    all_to_all x0 -> x6, starting transfers between devices: none -> 26.3 us  [the longest x3 14.3 us: quarters_in(): lax.all_to_all(w, BOTH, 0, 0, axis_index_groups=self.quarter_groups())]
    ppermute x70 -> x63, starting transfers between devices: 107 us -> 90.8 us  [one(): return lax.ppermute(x, BOTH, [(i, i ^ mask) for i in range(self.n)])]
    dot_general x3 -> x2, matrix products: 20 us -> 5.46 us  [dot_nt(): lax.dot_general(left, right, (((1,), (1,)), ((), ())), preferred_element_...]
    dot_general x6 -> x4, matrix products: 38.9 us -> 35 us  [dot_tn(): lax.dot_general(left, right, (((0,), (0,)), ((), ())), preferred_element_...]
    another operation x35 -> x29, other arithmetic: 19.8 us -> 18.6 us  [pair(): jnp.stack([jnp.where(low, mine, theirs), jnp.where(low, theirs, mine)], a...]
    unnamed x194 -> x185, local copies, waits for them, and re-layouts: 19.3 us -> 20.4 us
  transfers between devices with their start and end apart: 82 -> 81, of which waited for: 31 -> 36; matrix products, arithmetic and copies ran while one was open for 26% -> 24% of each run, Pallas kernels for 5% -> 17%
where the time goes in v3:
time: 684 us; the launch traced here: 676 us
  waiting for transfers between devices  229 us (33%)
  starting transfers between devices  118 us (17%)
  Pallas kernels  112 us (16%)
  other arithmetic  92.5 us (14%)
  local copies, waits for them, and re-layouts  61.7 us (9%)
  matrix products  44.6 us (7%)
  between operations  17.5 us (3%)
    ppermute x63, waiting for transfers between devices, one(): return lax.ppermute(x, BOTH, [(i, i ^ mask) for i in range(self.n)])  220 us
    ppermute x63, starting transfers between devices, one(): return lax.ppermute(x, BOTH, [(i, i ^ mask) for i in range(self.n)])  90.8 us
    pallas_call x2, Pallas kernels, hidden_back(): pl.pallas_call(functools.partial(back_kernel, count, half), grid=(tokens...  37.2 us
    dot_general x4, matrix products, dot_tn(): lax.dot_general(left, right, (((0,), (0,)), ((), ())), preferred_element_...  35 us
    pallas_call x1, Pallas kernels, hidden_units(): pl.pallas_call(hidden_kernel, grid=(tokens // tm,), in_specs=[rows, weigh...  23.6 us
    unnamed x185, local copies, waits for them, and re-layouts  20.4 us
    another operation x29, other arithmetic, pair(): jnp.stack([jnp.where(low, mine, theirs), jnp.where(low, theirs, mine)], a...  18.6 us
    pallas_call x1, Pallas kernels, hidden_grads(): pl.pallas_call(hidden_grad_kernel, grid=(tokens // tm,), in_specs=[pl.Blo...  16.1 us
  transfers between devices with their start and end apart: 81, of which 36 were waited for; matrix products, arithmetic and copies ran while one was open for 24% of the time, Pallas kernels for 17%

profile of v3, /device:TPU:0, one launch (start us, length us, event | category | flops | bytes accessed | tf_op | source)
XLA Modules:
  0.0 675.8 jit_solution(14046300899055704901)
XLA Ops:
  20.6 8.3 %collective-permute-done = bf16[104,1024]{1,0:T(8,128)(2,1)} collective-permute-done((bf16[104,1024]{1,0:T(8,128)(2,1)S(1)}, bf16[104,1024]{1,0:T(8,128)(2,1)}, u32[]{:S(2)}, u32[]{:S(2)}) %collective-permute-start) | collective-permute-done | bytes 213024 | tf_op jit(solution)/shard_map/ppermute | solution.py:364
  37.3 8.5 %collective-permute-done.1 = bf16[2,104,1024]{2,1,0:T(8,128)(2,1)S(1)} collective-permute-done((bf16[2,104,1024]{2,1,0:T(8,128)(2,1)S(1)}, bf16[2,104,1024]{2,1,0:T(8,128)(2,1)S(1)}, u32[]{:S(2)}, u32[]{:S(2)}) %collective-permute-start.1) | collective-permute-done | bytes 426016 | tf_op jit(solution)/shard_map/ppermute | solution.py:364
  50.7 24.1 %collective-permute-done.4 = bf16[2,96,1152]{2,1,0:T(8,128)(2,1)S(1)} collective-permute-done((bf16[2,96,1152]{2,1,0:T(8,128)(2,1)S(1)}, bf16[2,96,1152]{2,1,0:T(8,128)(2,1)S(1)}, u32[]{:S(2)}, u32[]{:S(2)}) %collective-permute-start.4) | collective-permute-done | bytes 442400 | tf_op jit(solution)/shard_map/ppermute | solution.py:364
  93.0 9.5 %collective-permute-done.6 = bf16[208,1024]{1,0:T(8,128)(2,1)} collective-permute-done((bf16[208,1024]{1,0:T(8,128)(2,1)}, bf16[208,1024]{1,0:T(8,128)(2,1)}, u32[]{:S(2)}, u32[]{:S(2)}) %collective-permute-start.6) | collective-permute-done | bytes 426016 | tf_op jit(solution)/shard_map/ppermute | solution.py:364
  127.1 7.8 %collective-permute-done.9 = bf16[256,1536]{1,0:T(8,128)(2,1)} collective-permute-done((bf16[256,1536]{1,0:T(8,128)(2,1)S(1)}, bf16[256,1536]{1,0:T(8,128)(2,1)}, u32[]{:S(2)}, u32[]{:S(2)}) %collective-permute-start.9) | collective-permute-done | bytes 786464 | tf_op jit(solution)/shard_map/ppermute | solution.py:364
  153.1 11.2 %collective-permute-done.13.refs_2_ = bf16[512,256]{1,0:T(8,128)(2,1)S(1)} collective-permute-done((bf16[512,256]{1,0:T(8,128)(2,1)S(1)}, bf16[512,256]{1,0:T(8,128)(2,1)S(1)}, u32[]{:S(2)}, u32[]{:S(2)}) %collective-permute-start.13) | collective-permute-done | bytes 262176 | tf_op jit(solution)/shard_map/ppermute | solution.py:364
  179.6 12.4 %shard_map.254 = (bf16[512,768]{1,0:T(8,128)(2,1)}, f32[512,768]{1,0:T(8,128)}, bf16[512,768]{1,0:T(8,128)(2,1)}, f32[6,1,512]{2,1,0:T(1,128)}) custom-call(s32[4]{0:T(128)} %and_convert_fusion.seen, f32[512,1024]{1,0:T(8,128)} %copy-done.18, f32[512,128]{1,0:T(8,128)} %get-tuple-element.420.cos_ref, f32[512,128]{1,0:T(8,128)} %get-tuple-element.320.sin_ref, ...), custom_call_target="tpu_custom_call" | custom-call | flops 1 | bytes 1 | tf_op jit(solution)/shard_map/pallas_call | solution.py:109
  214.2 18.9 %collective-permute-done.20 = bf16[2,96,1152]{2,1,0:T(8,128)(2,1)S(1)} collective-permute-done((bf16[2,96,1152]{2,1,0:T(8,128)(2,1)S(1)}, bf16[2,96,1152]{2,1,0:T(8,128)(2,1)S(1)}, u32[]{:S(2)}, u32[]{:S(2)}) %collective-permute-start.20) | collective-permute-done | bytes 442400 | tf_op jit(solution)/shard_map/ppermute | solution.py:364
  241.3 14.3 %collective-permute-done.22 = bf16[128,1536]{1,0:T(8,128)(2,1)S(1)} collective-permute-done((bf16[128,1536]{1,0:T(8,128)(2,1)S(1)}, bf16[128,1536]{1,0:T(8,128)(2,1)S(1)}, u32[]{:S(2)}, u32[]{:S(2)}) %collective-permute-start.22) | collective-permute-done | bytes 393248 | tf_op jit(solution)/shard_map/ppermute | solution.py:364
  275.1 23.6 %shard_map.255 = (bf16[2048,1152]{1,0:T(8,128)(2,1)}, bf16[2048,1152]{1,0:T(8,128)(2,1)}, bf16[2048,1152]{1,0:T(8,128)(2,1)}) custom-call(bf16[2048,1536]{1,0:T(8,128)(2,1)} %constant_dynamic-update-slice_fusion.n_ref, bf16[1536,1152]{1,0:T(8,128)(2,1)} %bitcast.306, bf16[1536,1152]{1,0:T(8,128)(2,1)} %bitcast.304), custom_call_target="tpu_custom_call" | custom-call | flops 1 | bytes 1 | tf_op jit(solution)/shard_map/pallas_call | solution.py:245
  306.5 10.6 %convolution_convert_fusion.2 = bf16[1536,1152]{1,0:T(8,128)(2,1)S(1)} fusion(bf16[2048,1536]{1,0:T(8,128)(2,1)} %constant_dynamic-update-slice_fusion.7.d_ref, bf16[2048,1152]{1,0:T(8,128)(2,1)S(1)} %bitcast.318), kind=kOutput, calls=%fused_computation.3 | convolution fusion | flops 7249526784 | bytes 14548992 | tf_op jit(solution)/shard_map/dot_general | solution.py:47
  327.2 16.1 %shard_map.256 = (bf16[2048,1152]{1,0:T(8,128)(2,1)}, bf16[2048,1152]{1,0:T(8,128)(2,1)}) custom-call(bf16[2048,1536]{1,0:T(8,128)(2,1)} %constant_dynamic-update-slice_fusion.7.d_ref, bf16[1536,1152]{1,0:T(8,128)(2,1)} %bitcast.302, bf16[2048,1152]{1,0:T(8,128)(2,1)} %get-tuple-element.224.by_gate_ref, bf16[2048,1152]{1,0:T(8,128)(2,1)} %get-tuple-element.225.by_up_ref), custom_call_target="tpu_custom_call" | custom-call | flops 1 | bytes 1 | tf_op jit(solution)/shard_map/pallas_call | solution.py:267
  348.9 23.2 %shard_map.257 = (bf16[1024,1536]{1,0:T(8,128)(2,1)}, bf16[1024,1536]{1,0:T(8,128)(2,1)}) custom-call(bf16[2048,1152]{1,0:T(8,128)(2,1)} %get-tuple-element.242.refs_0_, bf16[2048,1152]{1,0:T(8,128)(2,1)} %get-tuple-element.238.refs_1_, bf16[1536,1152]{1,0:T(8,128)(2,1)} %bitcast.307, bf16[1536,1152]{1,0:T(8,128)(2,1)} %bitcast.305), custom_call_target="tpu_custom_call" | custom-call | flops 1 | bytes 1 | tf_op jit(solution)/shard_map/pallas_call | solution.py:308
  374.1 12.2 %convolution_convert_fusion.1 = bf16[1536,1152]{1,0:T(8,128)(2,1)S(1)} fusion(bf16[2048,1536]{1,0:T(8,128)(2,1)} %constant_dynamic-update-slice_fusion.n_ref, bf16[2048,1152]{1,0:T(8,128)(2,1)} %get-tuple-element.238.refs_1_), kind=kOutput, calls=%fused_computation.2 | convolution fusion | flops 7249526784 | bytes 14548992 | tf_op jit(solution)/shard_map/dot_general | solution.py:47
  393.8 10.6 %convolution_convert_fusion = bf16[1536,1152]{1,0:T(8,128)(2,1)S(1)} fusion(bf16[2048,1536]{1,0:T(8,128)(2,1)} %constant_dynamic-update-slice_fusion.n_ref, bf16[2048,1152]{1,0:T(8,128)(2,1)S(1)} %bitcast.320), kind=kOutput, calls=%fused_computation.1 | convolution fusion | flops 7249526784 | bytes 14548992 | tf_op jit(solution)/shard_map/dot_general | solution.py:47
  424.5 14.0 %shard_map.258 = (bf16[1024,1536]{1,0:T(8,128)(2,1)}, bf16[1024,1536]{1,0:T(8,128)(2,1)}) custom-call(bf16[2048,1152]{1,0:T(8,128)(2,1)} %get-tuple-element.249.refs_0_, bf16[1536,1152]{1,0:T(8,128)(2,1)} %bitcast.303), custom_call_target="tpu_custom_call" | custom-call | flops 1 | bytes 1 | tf_op jit(solution)/shard_map/pallas_call | solution.py:308
  479.8 15.9 %shard_map.259 = (bf16[512,768]{1,0:T(8,128)(2,1)}, f32[512,256]{1,0:T(8,128)}, bf16[512,256]{1,0:T(8,128)(2,1)}, bf16[512,256]{1,0:T(8,128)(2,1)}, bf16[512,256]{1,0:T(8,128)(2,1)}) custom-call(s32[4]{0:T(128)} %and_convert_fusion.seen, bf16[512,768]{1,0:T(8,128)(2,1)} %get-tuple-element.264.q_ref, bf16[512,768]{1,0:T(8,128)(2,1)} %convolution_convert_fusion.4.g_ref, ...), custom_call_target="tpu_custom_call" | custom-call | flops 1 | bytes 1 | tf_op jit(solution)/shard_map/pallas_call | solution.py:183
  497.0 8.5 %collective-permute-start.54 = (bf16[512,256]{1,0:T(8,128)(2,1)}, bf16[512,256]{1,0:T(8,128)(2,1)}, u32[]{:S(2)}, u32[]{:S(2)}) collective-permute-start(bf16[512,256]{1,0:T(8,128)(2,1)} %get-tuple-element.279), channel_id=1, source_target_pairs={{0,4},{2,6},{4,0},{6,2},{8,12},{10,14},{12,8},{14,10},{16,20},{18,... | collective-permute-start | bytes 786440 | tf_op jit(solution)/shard_map/ppermute | solution.py:364
  513.5 6.9 %shard_map.260 = bf16[1536,1536]{1,0:T(8,128)(2,1)} custom-call(bf16[512,1536]{1,0:T(8,128)(2,1)} %copy-done.16, bf16[512,768]{1,0:T(8,128)(2,1)} %get-tuple-element.289.b_ref, bf16[512,1536]{1,0:T(8,128)(2,1)} %pad_maximum_fusion.11.c_ref, bf16[512,768]{1,0:T(8,128)(2,1)} %get-tuple-element.191.d_ref), custom_call_target="tpu_custom_call" | custom-call | flops 1 | bytes 1 | tf_op jit(solution)/shard_map/pallas_call | solution.py:217
  524.7 9.0 %collective-permute-done.54 = bf16[512,256]{1,0:T(8,128)(2,1)} collective-permute-done((bf16[512,256]{1,0:T(8,128)(2,1)}, bf16[512,256]{1,0:T(8,128)(2,1)}, u32[]{:S(2)}, u32[]{:S(2)}) %collective-permute-start.54) | collective-permute-done | bytes 262176 | tf_op jit(solution)/shard_map/ppermute | solution.py:364
  554.6 7.5 %collective-permute-done.56 = bf16[192,1536]{1,0:T(8,128)(2,1)} collective-permute-done((bf16[192,1536]{1,0:T(8,128)(2,1)}, bf16[192,1536]{1,0:T(8,128)(2,1)}, u32[]{:S(2)}, u32[]{:S(2)}) %collective-permute-start.56) | collective-permute-done | bytes 589856 | tf_op jit(solution)/shard_map/ppermute | solution.py:364
  578.2 19.7 %collective-permute-done.64 = bf16[208,256]{1,0:T(8,128)(2,1)S(1)} collective-permute-done((bf16[208,256]{1,0:T(8,128)(2,1)S(1)}, bf16[208,256]{1,0:T(8,128)(2,1)S(1)}, u32[]{:S(2)}, u32[]{:S(2)}) %collective-permute-start.64) | collective-permute-done | bytes 106528 | tf_op jit(solution)/shard_map/ppermute | solution.py:364
  632.8 22.7 %collective-permute-done.71 = bf16[104,1792]{1,0:T(8,128)(2,1)S(1)} collective-permute-done((bf16[104,1792]{1,0:T(8,128)(2,1)S(1)}, bf16[104,1792]{1,0:T(8,128)(2,1)S(1)}, u32[]{:S(2)}, u32[]{:S(2)}) %collective-permute-start.71) | collective-permute-done | bytes 372768 | tf_op jit(solution)/shard_map/ppermute | solution.py:364
  655.5 7.0 %collective-permute-done.73 = bf16[104,1792]{1,0:T(8,128)(2,1)S(1)} collective-permute-done((bf16[104,1792]{1,0:T(8,128)(2,1)S(1)}, bf16[104,1792]{1,0:T(8,128)(2,1)S(1)}, u32[]{:S(2)}, u32[]{:S(2)}) %collective-permute-start.73) | collective-permute-done | bytes 372768 | tf_op jit(solution)/shard_map/ppermute | solution.py:364
  (534 shorter events, 335.5 us)
Async XLA Ops:
  14.7 181.4 %all-gather.2.cloned.1.call-start = ((), (), s32[]{:S(2)}) async-start(), calls=%async_computation.6 | async-start | bytes 2506752 | tf_op jit(solution)/shard_map/all_gather | solution.py:545
  46.0 28.8 %collective-permute-start.2 = (bf16[416,1024]{1,0:T(8,128)(2,1)S(1)}, bf16[416,1024]{1,0:T(8,128)(2,1)S(1)}, u32[]{:S(2)}, u32[]{:S(2)}) collective-permute-start(bf16[416,1024]{1,0:T(8,128)(2,1)S(1)} %bitcast.337), channel_id=1, source_target_pairs={{0,8},{2,10},{4,12},{6,14},{8,0},{10,2},{12,4},{14,6},{16,24},{18,... | collective-permute-start | bytes 2555912 | tf_op jit(solution)/shard_map/ppermute | solution.py:364
  76.9 31.1 %collective-permute-start.7 = (bf16[2,96,1152]{2,1,0:T(8,128)(2,1)S(1)}, bf16[2,96,1152]{2,1,0:T(8,128)(2,1)}, u32[]{:S(2)}, u32[]{:S(2)}) collective-permute-start(bf16[2,96,1152]{2,1,0:T(8,128)(2,1)S(1)} %get-tuple-element.169), channel_id=1, source_target_pairs={{0,4},{2,6},{4,0},{6,2},{8,12},{10,14},{12,8},{14,10},{16,20},{18,... | collective-permute-start | bytes 1327112 | tf_op jit(solution)/shard_map/ppermute | solution.py:364
  77.0 31.7 %all-to-all-start.1 = ((bf16[4,96,1152]{2,1,0:T(8,128)(2,1)}), bf16[4,96,1152]{2,1,0:T(8,128)(2,1)}, u32[]{:S(2)}, u32[]{:S(2)}) async-start(bf16[4,96,1152]{2,1,0:T(8,128)(2,1)} %bitcast.324), calls=%async_computation.1 | async-start | bytes 1769472 | tf_op jit(solution)/shard_map/all_to_all | solution.py:457
  135.8 29.2 %collective-permute-start.10 = (bf16[2,2,96,1152]{3,2,1,0:T(8,128)(2,1)}, bf16[2,2,96,1152]{3,2,1,0:T(8,128)(2,1)}, u32[]{:S(2)}, u32[]{:S(2)}) collective-permute-start(bf16[2,2,96,1152]{3,2,1,0:T(8,128)(2,1)} %pad_maximum_fusion.17), channel_id=1, source_target_pairs={{0,16},{2,18},{4,20},{6,22},{8,24},{10,26},{12,28},{14,30},{16,0},... | collective-permute-start | bytes 2654216 | tf_op jit(solution)/shard_map/ppermute | solution.py:364
  165.1 31.0 %all-to-all-start.2 = ((bf16[4,96,1152]{2,1,0:T(8,128)(2,1)}), bf16[4,96,1152]{2,1,0:T(8,128)(2,1)S(1)}, u32[]{:S(2)}, u32[]{:S(2)}) async-start(bf16[4,96,1152]{2,1,0:T(8,128)(2,1)} %bitcast.326), calls=%async_computation.2 | async-start | bytes 1769472 | tf_op jit(solution)/shard_map/all_to_all | solution.py:457
  202.8 30.2 %collective-permute-start.17 = (bf16[256,1536]{1,0:T(8,128)(2,1)S(1)}, bf16[256,1536]{1,0:T(8,128)(2,1)S(1)}, u32[]{:S(2)}, u32[]{:S(2)}) collective-permute-start(bf16[256,1536]{1,0:T(8,128)(2,1)S(1)} %multiply_convert_fusion.1), channel_id=1, source_target_pairs={{0,8},{2,10},{4,12},{6,14},{8,0},{10,2},{12,4},{14,6},{16,24},{18,... | collective-permute-start | bytes 2359304 | tf_op jit(solution)/shard_map/ppermute | solution.py:364
  206.5 28.8 %collective-permute-start.18 = (bf16[256,1536]{1,0:T(8,128)(2,1)S(1)}, bf16[256,1536]{1,0:T(8,128)(2,1)S(1)}, u32[]{:S(2)}, u32[]{:S(2)}) collective-permute-start(bf16[256,1536]{1,0:T(8,128)(2,1)S(1)} %multiply_convert_fusion.1), channel_id=1, source_target_pairs={{0,2},{2,0},{4,6},{6,4},{8,10},{10,8},{12,14},{14,12},{16,18},{18,... | collective-permute-start | bytes 2359304 | tf_op jit(solution)/shard_map/ppermute | solution.py:364
  206.5 28.8 %collective-permute-start.19 = (bf16[256,1536]{1,0:T(8,128)(2,1)S(1)}, bf16[256,1536]{1,0:T(8,128)(2,1)S(1)}, u32[]{:S(2)}, u32[]{:S(2)}) collective-permute-start(bf16[256,1536]{1,0:T(8,128)(2,1)S(1)} %multiply_convert_fusion.1), channel_id=1, source_target_pairs={{0,1},{1,0},{2,3},{3,2},{4,5},{5,4},{6,7},{7,6},{8,9},{9,8},{10,11... | collective-permute-start | bytes 2359304 | tf_op jit(solution)/shard_map/ppermute | solution.py:367
  206.5 28.8 %collective-permute-start.21 = (bf16[2,2,96,1152]{3,2,1,0:T(8,128)(2,1)S(1)}, bf16[2,2,96,1152]{3,2,1,0:T(8,128)(2,1)S(1)}, u32[]{:S(2)}, u32[]{:S(2)}) collective-permute-start(bf16[2,2,96,1152]{3,2,1,0:T(8,128)(2,1)S(1)} %pad_maximum_fusion.19), channel_id=1, source_target_pairs={{0,16},{2,18},{4,20},{6,22},{8,24},{10,26},{12,28},{14,30},{16,0},... | collective-permute-start | bytes 2654216 | tf_op jit(solution)/shard_map/ppermute | solution.py:364
  265.5 33.2 %collective-permute-start.29 = (bf16[2,2,96,1152]{3,2,1,0:T(8,128)(2,1)S(1)}, bf16[2,2,96,1152]{3,2,1,0:T(8,128)(2,1)S(1)}, u32[]{:S(2)}, u32[]{:S(2)}) collective-permute-start(bf16[2,2,96,1152]{3,2,1,0:T(8,128)(2,1)S(1)} %pad_maximum_fusion.21), channel_id=1, source_target_pairs={{0,16},{2,18},{4,20},{6,22},{8,24},{10,26},{12,28},{14,30},{16,0},... | collective-permute-start | bytes 2654216 | tf_op jit(solution)/shard_map/ppermute | solution.py:364
  268.7 30.0 %collective-permute-start.30 = (bf16[2,96,1152]{2,1,0:T(8,128)(2,1)S(1)}, bf16[2,96,1152]{2,1,0:T(8,128)(2,1)S(1)}, u32[]{:S(2)}, u32[]{:S(2)}) collective-permute-start(bf16[2,96,1152]{2,1,0:T(8,128)(2,1)S(1)} %get-tuple-element.216), channel_id=1, source_target_pairs={{0,4},{2,6},{4,0},{6,2},{8,12},{10,14},{12,8},{14,10},{16,20},{18,... | collective-permute-start | bytes 1327112 | tf_op jit(solution)/shard_map/ppermute | solution.py:364
  268.7 29.9 %collective-permute-start.27 = (bf16[128,1536]{1,0:T(8,128)(2,1)}, bf16[128,1536]{1,0:T(8,128)(2,1)S(1)}, u32[]{:S(2)}, u32[]{:S(2)}) collective-permute-start(bf16[128,1536]{1,0:T(8,128)(2,1)} %slice.391), channel_id=1, source_target_pairs={{0,2},{2,0},{4,6},{6,4},{8,10},{10,8},{12,14},{14,12},{16,18},{18,... | collective-permute-start | bytes 1179656 | tf_op jit(solution)/shard_map/ppermute | solution.py:364
  413.9 32.2 %collective-permute-start.44 = (bf16[2,2,96,1152]{3,2,1,0:T(8,128)(2,1)}, bf16[2,2,96,1152]{3,2,1,0:T(8,128)(2,1)S(1)}, u32[]{:S(2)}, u32[]{:S(2)}) collective-permute-start(bf16[2,2,96,1152]{3,2,1,0:T(8,128)(2,1)} %dynamic-slice_bitcast_fusion.2), channel_id=1, source_target_pairs={{0,16},{2,18},{4,20},{6,22},{8,24},{10,26},{12,28},{14,30},{16,0},... | collective-permute-start | bytes 2654216 | tf_op jit(solution)/shard_map/ppermute | solution.py:364
  418.0 28.1 %collective-permute-start.42 = (bf16[256,1536]{1,0:T(8,128)(2,1)}, bf16[256,1536]{1,0:T(8,128)(2,1)}, u32[]{:S(2)}, u32[]{:S(2)}) collective-permute-start(bf16[256,1536]{1,0:T(8,128)(2,1)} %pad_maximum_fusion.29), channel_id=1, source_target_pairs={{0,2},{2,0},{4,6},{6,4},{8,10},{10,8},{12,14},{14,12},{16,18},{18,... | collective-permute-start | bytes 2359304 | tf_op jit(solution)/shard_map/ppermute | solution.py:364
  497.0 36.8 %collective-permute-start.54 = (bf16[512,256]{1,0:T(8,128)(2,1)}, bf16[512,256]{1,0:T(8,128)(2,1)}, u32[]{:S(2)}, u32[]{:S(2)}) collective-permute-start(bf16[512,256]{1,0:T(8,128)(2,1)} %get-tuple-element.279), channel_id=1, source_target_pairs={{0,4},{2,6},{4,0},{6,2},{8,12},{10,14},{12,8},{14,10},{16,20},{18,... | collective-permute-start | bytes 786440 | tf_op jit(solution)/shard_map/ppermute | solution.py:364
  505.5 28.3 %collective-permute-start.55 = (bf16[512,256]{1,0:T(8,128)(2,1)}, bf16[512,256]{1,0:T(8,128)(2,1)}, u32[]{:S(2)}, u32[]{:S(2)}) collective-permute-start(bf16[512,256]{1,0:T(8,128)(2,1)} %get-tuple-element.280), channel_id=1, source_target_pairs={{0,6},{2,4},{4,2},{6,0},{8,14},{10,12},{12,10},{14,8},{16,22},{18,... | collective-permute-start | bytes 786440 | tf_op jit(solution)/shard_map/ppermute | solution.py:364
  522.7 31.9 %collective-permute-start.58 = (bf16[2,96,1152]{2,1,0:T(8,128)(2,1)}, bf16[2,96,1152]{2,1,0:T(8,128)(2,1)}, u32[]{:S(2)}, u32[]{:S(2)}) collective-permute-start(bf16[2,96,1152]{2,1,0:T(8,128)(2,1)} %dynamic-slice_bitcast_fusion.13), channel_id=1, source_target_pairs={{0,4},{2,6},{4,0},{6,2},{8,12},{10,14},{12,8},{14,10},{16,20},{18,... | collective-permute-start | bytes 1327112 | tf_op jit(solution)/shard_map/ppermute | solution.py:364
  567.1 32.9 %collective-permute-start.66 = (bf16[2,96,1152]{2,1,0:T(8,128)(2,1)S(1)}, bf16[2,96,1152]{2,1,0:T(8,128)(2,1)S(1)}, u32[]{:S(2)}, u32[]{:S(2)}) collective-permute-start(bf16[2,96,1152]{2,1,0:T(8,128)(2,1)S(1)} %dynamic-slice_bitcast_fusion.12), channel_id=1, source_target_pairs={{0,4},{2,6},{4,0},{6,2},{8,12},{10,14},{12,8},{14,10},{16,20},{18,... | collective-permute-start | bytes 1327112 | tf_op jit(solution)/shard_map/ppermute | solution.py:364
  568.3 31.7 %collective-permute-start.63 = (bf16[384,1536]{1,0:T(8,128)(2,1)S(1)}, bf16[384,1536]{1,0:T(8,128)(2,1)S(1)}, u32[]{:S(2)}, u32[]{:S(2)}) collective-permute-start(bf16[384,1536]{1,0:T(8,128)(2,1)S(1)} %pad_maximum_fusion.15), channel_id=1, source_target_pairs={{0,16},{2,18},{4,20},{6,22},{8,24},{10,26},{12,28},{14,30},{16,0},... | collective-permute-start | bytes 3538952 | tf_op jit(solution)/shard_map/ppermute | solution.py:364
  569.6 30.4 %collective-permute-start.62 = (bf16[384,1536]{1,0:T(8,128)(2,1)S(1)}, bf16[384,1536]{1,0:T(8,128)(2,1)S(1)}, u32[]{:S(2)}, u32[]{:S(2)}) collective-permute-start(bf16[384,1536]{1,0:T(8,128)(2,1)S(1)} %pad_maximum_fusion.14), channel_id=1, source_target_pairs={{0,8},{2,10},{4,12},{6,14},{8,0},{10,2},{12,4},{14,6},{16,24},{18,... | collective-permute-start | bytes 3538952 | tf_op jit(solution)/shard_map/ppermute | solution.py:364
  622.5 43.5 %all-to-all-start.5 = ((bf16[4,96,1152]{2,1,0:T(8,128)(2,1)}), bf16[4,96,1152]{2,1,0:T(8,128)(2,1)}, u32[]{:S(2)}, u32[]{:S(2)}) async-start(bf16[4,96,1152]{2,1,0:T(8,128)(2,1)} %bitcast.126), calls=%async_computation.5 | async-start | bytes 1769472 | tf_op jit(solution)/shard_map/all_to_all | solution.py:460
  626.9 28.6 %collective-permute-start.71 = (bf16[104,1792]{1,0:T(8,128)(2,1)S(1)}, bf16[104,1792]{1,0:T(8,128)(2,1)S(1)}, u32[]{:S(2)}, u32[]{:S(2)}) collective-permute-start(bf16[104,1792]{1,0:T(8,128)(2,1)S(1)} %get-tuple-element.308), channel_id=1, source_target_pairs={{0,2},{2,0},{4,6},{6,4},{8,10},{10,8},{12,14},{14,12},{16,18},{18,... | collective-permute-start | bytes 1118216 | tf_op jit(solution)/shard_map/ppermute | solution.py:364
  630.0 32.5 %collective-permute-start.73 = (bf16[104,1792]{1,0:T(8,128)(2,1)S(1)}, bf16[104,1792]{1,0:T(8,128)(2,1)S(1)}, u32[]{:S(2)}, u32[]{:S(2)}) collective-permute-start(bf16[104,1792]{1,0:T(8,128)(2,1)S(1)} %get-tuple-element.310), channel_id=1, source_target_pairs={{0,6},{2,4},{4,2},{6,0},{8,14},{10,12},{12,10},{14,8},{16,22},{18,... | collective-permute-start | bytes 1118216 | tf_op jit(solution)/shard_map/ppermute | solution.py:364
  (142 other events, 1699.3 us)
Sparse Core Ops, SparseCore 0:
  18.3 85.2 all-gather.1

commit v4 on v3

--- a/solution.py
+++ b/solution.py
@@ -11,6 +11,7 @@
 ROPE_BASE = 1000000.0
 MASKED = -1e30
 LANES = 128
+PARTS = 4
 BOTH = ("fsdp", "context")
 KERNEL_BYTES = 56 << 20
 BF = jnp.bfloat16
@@ -225,6 +226,51 @@
     )(a, b, c, d)
 
 
+def fetch(side, parts, held, sems):
+    @pl.when(pl.program_id(0) == 0)
+    def _():
+        copies = []
+        for k, dst in enumerate(held):
+            for p in range(PARTS):
+                src = parts[PARTS * k + p]
+                rows = src.shape[0]
+                high = side[0] if p < 2 else 1 - side[0]
+                first = pl.multiple_of((2 * high + p % 2) * rows, rows)
+                copies.append(
+                    pltpu.make_async_copy(src, dst.at[pl.ds(first, rows)], sems.at[k, p])
+                )
+        for copy in copies:
+            copy.start()
+        for copy in copies:
+            copy.wait()
+
+
+def with_weights(body, grid, in_specs, weights, out_specs, out_shape):
+    rows, units = weights[0][0].shape
+    count = len(weights)
+    first = 1 + len(in_specs)
+    last = first + PARTS * count
+
+    def kernel(*refs):
+        held, sems = refs[-count - 1 : -1], refs[-1]
+        fetch(refs[0], refs[first:last], held, sems)
+        body(*refs[1:first], *held, *refs[last : -count - 1])
+
+    return pl.pallas_call(
+        kernel,
+        grid=grid,
+        in_specs=[pl.BlockSpec(memory_space=pltpu.SMEM)]
+        + in_specs
+        + [pl.BlockSpec(memory_space=pl.ANY)] * (PARTS * count),
+        out_specs=out_specs,
+        out_shape=out_shape,
+        scratch_shapes=[pltpu.VMEM((PARTS * rows, units), BF)] * count
+        + [pltpu.SemaphoreType.DMA((count, PARTS))],
+        compiler_params=pltpu.CompilerParams(vmem_limit_bytes=KERNEL_BYTES),
+        cost_estimate=pl.CostEstimate(flops=1, bytes_accessed=1, transcendentals=0),
+    )
+
+
 def hidden_kernel(n_ref, wg_ref, wu_ref, act_ref, by_gate_ref, by_up_ref):
     gate = dot_nn(n_ref[...], wg_ref[...])
     up = dot_nn(n_ref[...], wu_ref[...])
@@ -235,49 +281,36 @@
     by_up_ref[...] = silu.astype(BF)
 
 
-def hidden_units(normed, gate_w, up_w):
+def hidden_units(side, normed, gate_w, up_w):
     tokens, depth = normed.shape
-    units = gate_w.shape[1]
+    units = gate_w[0].shape[1]
     tm = min(tokens, 256)
     rows = pl.BlockSpec((tm, depth), lambda m: (m, 0))
-    weight = pl.BlockSpec((depth, units), lambda m: (0, 0))
     out = pl.BlockSpec((tm, units), lambda m: (m, 0))
-    return pl.pallas_call(
-        hidden_kernel,
-        grid=(tokens // tm,),
-        in_specs=[rows, weight, weight],
-        out_specs=[out] * 3,
-        out_shape=[jax.ShapeDtypeStruct((tokens, units), BF)] * 3,
-        compiler_params=pltpu.CompilerParams(vmem_limit_bytes=KERNEL_BYTES),
-        cost_estimate=pl.CostEstimate(flops=1, bytes_accessed=1, transcendentals=0),
-    )(normed, gate_w, up_w)
-
-
-def hidden_grad_kernel(d_ref, wd_ref, by_gate_ref, by_up_ref, dg_ref, du_ref):
+    shape = jax.ShapeDtypeStruct((tokens, units), BF)
+    call = with_weights(
+        hidden_kernel, (tokens // tm,), [rows], (gate_w, up_w), [out] * 3, [shape] * 3
+    )
+    return call(side, normed, *gate_w, *up_w)
+
+
+def hidden_grad_kernel(d_ref, by_gate_ref, by_up_ref, wd_ref, dg_ref, du_ref):
     grad = dot_nn(d_ref[...], wd_ref[...])
     dg_ref[...] = (grad * by_gate_ref[...].astype(F32)).astype(BF)
     du_ref[...] = (grad * by_up_ref[...].astype(F32)).astype(BF)
 
 
-def hidden_grads(grads, down_w, by_gate, by_up):
+def hidden_grads(side, grads, down_w, by_gate, by_up):
     tokens, depth = grads.shape
-    units = down_w.shape[1]
+    units = down_w[0].shape[1]
     tm = min(tokens, 256)
+    rows = pl.BlockSpec((tm, depth), lambda m: (m, 0))
     out = pl.BlockSpec((tm, units), lambda m: (m, 0))
-    return pl.pallas_call(
-        hidden_grad_kernel,
-        grid=(tokens // tm,),
-        in_specs=[
-            pl.BlockSpec((tm, depth), lambda m: (m, 0)),
-            pl.BlockSpec((depth, units), lambda m: (0, 0)),
-            out,
-            out,
-        ],
-        out_specs=[out] * 2,
-        out_shape=[jax.ShapeDtypeStruct((tokens, units), BF)] * 2,
-        compiler_params=pltpu.CompilerParams(vmem_limit_bytes=KERNEL_BYTES),
-        cost_estimate=pl.CostEstimate(flops=1, bytes_accessed=1, transcendentals=0),
-    )(grads, down_w, by_gate, by_up)
+    shape = jax.ShapeDtypeStruct((tokens, units), BF)
+    call = with_weights(
+        hidden_grad_kernel, (tokens // tm,), [rows, out, out], (down_w,), [out] * 2, [shape] * 2
+    )
+    return call(side, grads, by_gate, by_up, *down_w)
 
 
 def back_kernel(count, half, *refs):
@@ -297,26 +330,26 @@
         second[...] = total.astype(BF)
 
 
-def hidden_back(lefts, rights):
+def hidden_back(side, lefts, rights):
     tokens, units = lefts[0].shape
-    depth = rights[0].shape[0]
+    depth = PARTS * rights[0][0].shape[0]
     count = len(lefts)
     tm = min(tokens // 2, 512)
     half = tokens // 2 // tm
     rows = pl.BlockSpec((tm, units), lambda m: (m, 0))
-    weight = pl.BlockSpec((depth, units), lambda m: (0, 0))
-    return pl.pallas_call(
+    out_specs = [
+        pl.BlockSpec((tm, depth), lambda m: (jnp.minimum(m, half - 1), 0)),
+        pl.BlockSpec((tm, depth), lambda m: (jnp.maximum(m - half, 0), 0)),
+    ]
+    call = with_weights(
         functools.partial(back_kernel, count, half),
-        grid=(tokens // tm,),
-        in_specs=[rows] * count + [weight] * count,
-        out_specs=[
-            pl.BlockSpec((tm, depth), lambda m: (jnp.minimum(m, half - 1), 0)),
-            pl.BlockSpec((tm, depth), lambda m: (jnp.maximum(m - half, 0), 0)),
-        ],
-        out_shape=[jax.ShapeDtypeStruct((tokens // 2, depth), BF)] * 2,
-        compiler_params=pltpu.CompilerParams(vmem_limit_bytes=KERNEL_BYTES),
-        cost_estimate=pl.CostEstimate(flops=1, bytes_accessed=1, transcendentals=0),
-    )(*lefts, *rights)
+        (tokens // tm,),
+        [rows] * count,
+        rights,
+        out_specs,
+        [jax.ShapeDtypeStruct((tokens // 2, depth), BF)] * 2,
+    )
+    return call(side, *lefts, *[x for w in rights for x in w])
 
 
 def after(x, *earlier):
@@ -409,13 +442,6 @@
     def context_pick(self, x, r):
         x = x.reshape(self.nc, -1, x.shape[1])
         return lax.dynamic_index_in_dim(x, self.my_slot ^ r, 0, keepdims=False)
-
-    def scatter_context(self, x):
-        gives = self.fence(*[self.context_pick(x, r) for r in range(1, self.nc)])
-        total = self.context_pick(x, 0).astype(F32)
-        for r in range(1, self.nc):
-            total = total + self.one(gives[r - 1], r).astype(F32)
-        return total
 
     def tokens_near(self, x, pin_x=(), pin_z=()):
         return self.one(x, self.xm, pin_x), self.one(x, self.zm, pin_z)
@@ -553,12 +579,13 @@
     def deep_z(w):
         return grid.deepen(w, [0], context_deep)
 
-    def deep_y(w):
-        return grid.deepen(w, [0] + context_deep, fsdp_deep)
-
-    def whole(halves):
-        return jnp.stack(halves, len(fsdp_deep)).reshape(grid.n * shard, quarter)
-
+    def give_y(w):
+        return grid.one(w, 1 << fsdp_deep[0])
+
+    def parts_of(*pieces):
+        return tuple(x.reshape(grid.n // PARTS * shard, quarter) for x in pieces)
+
+    side = grid.bit(fsdp_deep[0]).reshape(1)
     held = []
     gate_near = grid.quarters_in(quarters(jnp.pad(w_gate, pad)))
     packed = grid.deepen(packed, held, context_deep[::-1])
@@ -605,16 +632,16 @@
     cosine, sine = tables(query_pos, head_width)
     grads_own, grads_other = own(cotangent), others(cotangent)
     gate_0, grads_pz = grid.fence(gate_0, grads_own)
-    gate_0, grads_pz = deep_y(gate_0), grid.over_z(grads_pz)
+    gate_2, grads_pz = give_y(gate_0), grid.over_z(grads_pz)
     qkv = dot_nn(normed_one, w_qkv) + bias
     keys = qkv[:, query_width : query_width + head_width]
     keys = keys * cosine + swap_halves(keys) * sine
     pair = jnp.concatenate([keys, qkv[:, query_width + head_width :]], axis=1).astype(BF)
-    pair, qkv, gate_0, grads_pz = grid.close(pair, qkv, gate_0, grads_pz)
+    pair, qkv, gate_2, grads_pz = grid.close(pair, qkv, gate_2, grads_pz)
 
     gate_1, grads_px = grid.fence(gate_1, grads_own)
     met = [grid.one(pair, r) for r in range(1, slot_count)]
-    gate_1, grads_px, *met = grid.close(deep_y(gate_1), grid.over_x(grads_px), *met)
+    gate_3, grads_px, *met = grid.close(give_y(gate_1), grid.over_x(grads_px), *met)
     pairs = [pair] + met
 
     piece_block = owners[grid.my_slot ^ jnp.arange(slot_count)]
@@ -635,41 +662,52 @@
     normed_two = grid.close(normed_two)
 
     up_0, up_1 = grid.fence(up_0, up_near[1])
-    px, pz, normed_other, up_1, up_0 = grid.close(
+    px, pz, normed_other, up_1, up_2 = grid.close(
         grid.over_x(normed_two),
         grid.over_z(normed_two),
         grid.swap(normed_two),
         deep_z(up_1),
-        deep_y(up_0),
+        give_y(up_0),
     )
 
     cut = px.shape[0] // 2
     (down_0,) = grid.fence(down_near[0])
-    by_z, by_x, up_1, down_0 = grid.close(
-        grid.over_z(px[:cut]), grid.over_x(pz[cut:]), deep_y(up_1), deep_z(down_0)
-    )
-
-    normed_got = jnp.concatenate([px, pz, by_z, by_x], 0)
-    gate_0, gate_1, up_0 = grid.fence(gate_0, gate_1, up_0)
-    gate_full, up_full = whole([gate_0, gate_1]), whole([up_0, up_1])
-    normed_far, gate_full, up_full = grid.close(grid.swap(normed_got), gate_full, up_full)
-
-    normed_in = jnp.concatenate([normed_two, normed_got, normed_other, normed_far], 0)
+    normed_near = jnp.concatenate([px, pz], 0)
+    by_z, by_x, up_3, down_0, normed_swap = grid.close(
+        grid.over_z(px[:cut]),
+        grid.over_x(pz[cut:]),
+        give_y(up_1),
+        deep_z(down_0),
+        grid.swap(normed_near),
+    )
+
+    normed_far = jnp.concatenate([by_z, by_x], 0)
+    gate_full = parts_of(gate_0, gate_1, gate_2, gate_3)
+    up_full = parts_of(up_0, up_1, up_2, up_3)
+    far_swap, grads_swap = grid.close(
+        grid.swap(normed_far), grid.swap(jnp.concatenate([grads_px, grads_pz], 0))
+    )
+
+    normed_in = jnp.concatenate(
+        [normed_two, normed_near, normed_far, normed_other, normed_swap, far_swap], 0
+    )
     far_z, far_x, down_0, down_1 = grid.fence(
         grads_px[:cut], grads_pz[cut:], down_0, down_near[1]
     )
     by_z, by_x = grid.over_z(far_z), grid.over_x(far_x)
-    down_0, down_1 = deep_y(down_0), deep_z(down_1)
-    act, by_gate, by_up = hidden_units(normed_in, gate_full, up_full)
-    act, by_z, by_x, down_0, down_1 = grid.close(act, by_z, by_x, down_0, down_1)
-
-    grads_got = jnp.concatenate([grads_px, grads_pz, by_z, by_x], 0)
-    down_1 = deep_y(down_1)
+    down_2, down_1 = give_y(down_0), deep_z(down_1)
+    act, by_gate, by_up = hidden_units(side, normed_in, gate_full, up_full)
+    act, by_z, by_x, down_2, down_1 = grid.close(act, by_z, by_x, down_2, down_1)
+
+    grads_far = jnp.concatenate([by_z, by_x], 0)
+    down_3 = give_y(down_1)
     grads_in = jnp.concatenate(
-        [grads_own, grads_got, grads_other, grid.swap(grads_got)], 0
+        [grads_own, grads_px, grads_pz, grads_far, grads_other, grads_swap, grid.swap(grads_far)],
+        0,
     )
     grad_wdown = dot_tn(grads_in, act).astype(BF)
-    grad_wdown, down_1 = grid.close(grad_wdown, down_1)
+    grad_wdown, down_3 = grid.close(grad_wdown, down_3)
+    down_full = parts_of(down_0, down_1, down_2, down_3)
 
     top = sorted(range(grid.cbits + grid.fbits), reverse=True)
     shape = (2,) * len(top) + (shard, quarter)
@@ -687,14 +725,13 @@
     def joined(first, second):
         return jnp.stack([first, second], 0).reshape(4, shard, quarter)
 
-    down_full = whole([down_0, down_1])
     down_0 = fold_y(half(grad_wdown, 0))
-    grad_gate, grad_up = hidden_grads(grads_in, down_full, by_gate, by_up)
+    grad_gate, grad_up = hidden_grads(side, grads_in, down_full, by_gate, by_up)
     down_0, grad_gate, grad_up = grid.close(down_0, grad_gate, grad_up)
 
     (down_1,) = grid.fence(half(grad_wdown, 1))
     down_0, down_1 = fold_z(down_0), fold_y(down_1)
-    part, give = hidden_back((grad_gate, grad_up), (gate_full, up_full))
+    part, give = hidden_back(side, (grad_gate, grad_up), (gate_full, up_full))
     down_0, down_1, part, give = grid.close(down_0, down_1, part, give)
 
     other = grid.swap(give)
@@ -713,7 +750,7 @@
     up_1, act_in = grid.fence(half(grad_wup, 1), act)
     px, pz = grid.over_x(px), grid.over_z(pz)
     up_0, up_1 = fold_z(up_0), fold_y(up_1)
-    mlp_part, mlp_give = hidden_back((act_in,), (down_full,))
+    mlp_part, mlp_give = hidden_back(side, (act_in,), (down_full,))
     px, pz, up_0, up_1, mlp_part, mlp_give = grid.close(
         px, pz, up_0, up_1, mlp_part, mlp_give
     )
@@ -806,30 +843,33 @@
         ax, ay, by_y, by_x, gate_1, grad_inputs.astype(BF), result
     )
 
+    grad_attn = grid.fsdp_end(grad_attn, ax, ay)
     kx, ky = grid.fsdp_near(grad_wkv, by_y, by_x)
     (up_in,) = grid.fence(joined(up_0, up_1))
     kx, ky = grid.over_x(kx), grid.over_y(ky)
+    parts = [grid.one(grid.context_pick(grad_attn, r), r) for r in range(1, grid.nc)]
     grad_wup = grid.quarters_out(up_in)
-    grad_tokens = both(grad_tokens)
-    kx, ky, grad_wup = grid.close(kx, ky, grad_wup)
+    grad_tokens, result = both(grad_tokens), both(result)
+    kx, ky, grad_wup, grad_tokens, result, *parts = grid.close(
+        kx, ky, grad_wup, grad_tokens, result, *parts
+    )
 
     (gate_in,) = grid.fence(joined(gate_0, gate_1))
     grad_wgate = grid.quarters_out(gate_in)
-    grad_attn = grid.fsdp_end(grad_attn, ax, ay)
     grad_wkv = grid.fsdp_end(grad_wkv, kx, ky)
-    grad_attn = jnp.pad(
-        grad_attn.reshape(-1, shard, 2 * query_width), ((0, 0), (0, 8), (0, 0))
-    )
-    grad_attn = jnp.concatenate([grad_attn, grad_wkv.reshape(-1, shard + 8, wide)], axis=2)
-    grad_attn = grid.scatter_context(grad_attn.reshape(-1, 2 * query_width + wide))
-    result = both(result)
-    small = grad_attn[shard : shard + 1, 2 * query_width :]
-    grad_attn = grad_attn[:shard]
+    terms = [grid.one(grid.context_pick(grad_wkv, r), r) for r in range(1, grid.nc)]
+    grad_attn = grid.context_pick(grad_attn, 0).astype(F32)
+    for x in parts:
+        grad_attn = grad_attn + x.astype(F32)
+    grad_wkv = grid.context_pick(grad_wkv, 0).astype(F32)
+    for x in terms:
+        grad_wkv = grad_wkv + x.astype(F32)
+    small = grad_wkv[shard : shard + 1]
+    grad_wkv = grad_wkv[:shard]
     grad_wdown, grad_wup, grad_wgate = [
         g.transpose(1, 0, 2).reshape(shard, 4 * quarter).astype(F32)
         for g in (grad_wdown, grad_wup, grad_wgate)
     ]
-    grad_wkv = grad_attn[:, 2 * query_width :]
     return (
         result,
         grad_tokens,

time: 684 us -> 668 us (0.977)
  waiting for transfers between devices: 229 us -> 206 us
  Pallas kernels: 112 us -> 125 us
  other arithmetic: 92.5 us -> 84.7 us
    ppermute x63 -> x66, waiting for transfers between devices: 220 us -> 194 us  [one(): return lax.ppermute(x, BOTH, [(i, i ^ mask) for i in range(self.n)])]
    another operation x29 -> x20, other arithmetic: 18.6 us -> 9.63 us  [pair(): jnp.stack([jnp.where(low, mine, theirs), jnp.where(low, theirs, mine)], a...]
    unnamed x185 -> x219, local copies, waits for them, and re-layouts: 20.4 us -> 25.6 us
    ppermute x63 -> x66, starting transfers between devices: 90.8 us -> 94.1 us  [one(): return lax.ppermute(x, BOTH, [(i, i ^ mask) for i in range(self.n)])]
  transfers between devices with their start and end apart: 81 -> 86, of which waited for: 36 -> 37; matrix products, arithmetic and copies ran while one was open for 24% -> 22% of each run, Pallas kernels for 17% -> 19%
where the time goes in v4:
time: 668 us; the launch traced here: 659 us
  waiting for transfers between devices  206 us (31%)
  Pallas kernels  125 us (19%)
  starting transfers between devices  122 us (18%)
  other arithmetic  84.7 us (13%)
  local copies, waits for them, and re-layouts  60.7 us (9%)
  matrix products  42.8 us (6%)
  between operations  17.7 us (3%)
    ppermute x66, waiting for transfers between devices, one(): return lax.ppermute(x, BOTH, [(i, i ^ mask) for i in range(self.n)])  194 us
    ppermute x66, starting transfers between devices, one(): return lax.ppermute(x, BOTH, [(i, i ^ mask) for i in range(self.n)])  94.1 us
    pallas_call x2, Pallas kernels, hidden_back(): return call(side, *lefts, *[x for w in rights for x in w])  39.3 us
    dot_general x4, matrix products, dot_tn(): lax.dot_general(left, right, (((0,), (0,)), ((), ())), preferred_element_...  33.6 us
    unnamed x219, local copies, waits for them, and re-layouts  25.6 us
    pallas_call x1, Pallas kernels, hidden_units(): return call(side, normed, *gate_w, *up_w)  24.3 us
    pallas_call x1, Pallas kernels, attend_back(): pl.pallas_call(functools.partial(attend_back_kernel, count, scale), grid_...  20.5 us
    pallas_call x1, Pallas kernels, hidden_grads(): return call(side, grads, by_gate, by_up, *down_w)  17.1 us
  transfers between devices with their start and end apart: 86, of which 37 were waited for; matrix products, arithmetic and copies ran while one was open for 22% of the time, Pallas kernels for 19%

profile of v4, /device:TPU:0, one launch (start us, length us, event | category | flops | bytes accessed | tf_op | source)
XLA Modules:
  0.0 659.3 jit_solution(1188692907254914142)
XLA Ops:
  20.6 8.3 %collective-permute-done = bf16[104,1024]{1,0:T(8,128)(2,1)} collective-permute-done((bf16[104,1024]{1,0:T(8,128)(2,1)S(1)}, bf16[104,1024]{1,0:T(8,128)(2,1)}, u32[]{:S(2)}, u32[]{:S(2)}) %collective-permute-start) | collective-permute-done | bytes 213024 | tf_op jit(solution)/shard_map/ppermute | solution.py:397
  37.3 8.5 %collective-permute-done.1 = bf16[2,104,1024]{2,1,0:T(8,128)(2,1)S(1)} collective-permute-done((bf16[2,104,1024]{2,1,0:T(8,128)(2,1)S(1)}, bf16[2,104,1024]{2,1,0:T(8,128)(2,1)S(1)}, u32[]{:S(2)}, u32[]{:S(2)}) %collective-permute-start.1) | collective-permute-done | bytes 426016 | tf_op jit(solution)/shard_map/ppermute | solution.py:397
  51.0 23.8 %collective-permute-done.4 = bf16[2,96,1152]{2,1,0:T(8,128)(2,1)S(1)} collective-permute-done((bf16[2,96,1152]{2,1,0:T(8,128)(2,1)S(1)}, bf16[2,96,1152]{2,1,0:T(8,128)(2,1)S(1)}, u32[]{:S(2)}, u32[]{:S(2)}) %collective-permute-start.4) | collective-permute-done | bytes 442400 | tf_op jit(solution)/shard_map/ppermute | solution.py:397
  93.0 9.5 %collective-permute-done.6 = bf16[208,1024]{1,0:T(8,128)(2,1)} collective-permute-done((bf16[208,1024]{1,0:T(8,128)(2,1)}, bf16[208,1024]{1,0:T(8,128)(2,1)}, u32[]{:S(2)}, u32[]{:S(2)}) %collective-permute-start.6) | collective-permute-done | bytes 426016 | tf_op jit(solution)/shard_map/ppermute | solution.py:397
  125.1 10.5 %collective-permute-done.9 = bf16[256,1536]{1,0:T(8,128)(2,1)} collective-permute-done((bf16[256,1536]{1,0:T(8,128)(2,1)}, bf16[256,1536]{1,0:T(8,128)(2,1)}, u32[]{:S(2)}, u32[]{:S(2)}) %collective-permute-start.9) | collective-permute-done | bytes 786464 | tf_op jit(solution)/shard_map/ppermute | solution.py:397
  151.9 9.5 %collective-permute-done.13.refs_2_ = bf16[512,256]{1,0:T(8,128)(2,1)S(1)} collective-permute-done((bf16[512,256]{1,0:T(8,128)(2,1)S(1)}, bf16[512,256]{1,0:T(8,128)(2,1)S(1)}, u32[]{:S(2)}, u32[]{:S(2)}) %collective-permute-start.13) | collective-permute-done | bytes 262176 | tf_op jit(solution)/shard_map/ppermute | solution.py:397
  172.9 16.7 %shard_map.254 = (bf16[512,768]{1,0:T(8,128)(2,1)}, f32[512,768]{1,0:T(8,128)}, bf16[512,768]{1,0:T(8,128)(2,1)}, f32[6,1,512]{2,1,0:T(1,128)}) custom-call(s32[4]{0:T(128)} %and_convert_fusion.seen, f32[512,1024]{1,0:T(8,128)} %copy-done.27, f32[512,128]{1,0:T(8,128)} %get-tuple-element.400.cos_ref, f32[512,128]{1,0:T(8,128)} %get-tuple-element.318.sin_ref, ...), custom_call_target="tpu_custom_call" | custom-call | flops 1 | bytes 1 | tf_op jit(solution)/shard_map/pallas_call | solution.py:110
  209.2 18.0 %collective-permute-done.20 = bf16[2,96,1152]{2,1,0:T(8,128)(2,1)S(1)} collective-permute-done((bf16[2,96,1152]{2,1,0:T(8,128)(2,1)S(1)}, bf16[2,96,1152]{2,1,0:T(8,128)(2,1)S(1)}, u32[]{:S(2)}, u32[]{:S(2)}) %collective-permute-start.20) | collective-permute-done | bytes 442400 | tf_op jit(solution)/shard_map/ppermute | solution.py:397
  237.9 10.3 %collective-permute-done.22 = bf16[128,1536]{1,0:T(8,128)(2,1)S(1)} collective-permute-done((bf16[128,1536]{1,0:T(8,128)(2,1)S(1)}, bf16[128,1536]{1,0:T(8,128)(2,1)S(1)}, u32[]{:S(2)}, u32[]{:S(2)}) %collective-permute-start.22) | collective-permute-done | bytes 393248 | tf_op jit(solution)/shard_map/ppermute | solution.py:397
  249.8 8.9 %collective-permute-done.23 = bf16[128,1536]{1,0:T(8,128)(2,1)S(1)} collective-permute-done((bf16[128,1536]{1,0:T(8,128)(2,1)S(1)}, bf16[128,1536]{1,0:T(8,128)(2,1)S(1)}, u32[]{:S(2)}, u32[]{:S(2)}) %collective-permute-start.23) | collective-permute-done | bytes 393248 | tf_op jit(solution)/shard_map/ppermute | solution.py:397
  269.3 24.3 %shard_map.255 = (bf16[2048,1152]{1,0:T(8,128)(2,1)}, bf16[2048,1152]{1,0:T(8,128)(2,1)}, bf16[2048,1152]{1,0:T(8,128)(2,1)}) custom-call(s32[1]{0:T(128)} %bitcast.24.refs_0_, bf16[2048,1536]{1,0:T(8,128)(2,1)} %copy-done.9, bf16[384,1152]{1,0:T(8,128)(2,1)} %bitcast.297, bf16[384,1152]{1,0:T(8,128)(2,1)} %bitcast.299, ...), custom_call_target="tpu_custom_call" | custom-call | flops 1 | bytes 1 | tf_op jit(solution)/shard_map/pallas_call | solution.py:294
  301.2 11.0 %convolution_convert_fusion.2 = bf16[1536,1152]{1,0:T(8,128)(2,1)S(1)} fusion(bf16[2048,1536]{1,0:T(8,128)(2,1)} %constant_dynamic-update-slice_fusion.8.refs_1_, bf16[2048,1152]{1,0:T(8,128)(2,1)S(1)} %copy-done.26), kind=kOutput, calls=%fused_computation.3 | convolution fusion | flops 7249526784 | bytes 14548992 | tf_op jit(solution)/shard_map/dot_general | solution.py:48
  320.6 17.1 %shard_map.256 = (bf16[2048,1152]{1,0:T(8,128)(2,1)}, bf16[2048,1152]{1,0:T(8,128)(2,1)}) custom-call(s32[1]{0:T(128)} %bitcast.24.refs_0_, bf16[2048,1536]{1,0:T(8,128)(2,1)} %constant_dynamic-update-slice_fusion.8.refs_1_, bf16[2048,1152]{1,0:T(8,128)(2,1)} %get-tuple-element.218.refs_2_, bf16[2048,1152]{1,0:T(8,128)(2,1)} %get-tuple-element.219.refs_3_, ...), custom_call_target="tpu_custom_call" | custom-call | flops 1 | bytes 1 | tf_op jit(solution)/shard_map/pallas_call | solution.py:313
  343.5 24.3 %shard_map.257 = (bf16[1024,1536]{1,0:T(8,128)(2,1)}, bf16[1024,1536]{1,0:T(8,128)(2,1)}) custom-call(s32[1]{0:T(128)} %bitcast.24.refs_0_, bf16[2048,1152]{1,0:T(8,128)(2,1)} %get-tuple-element.238.refs_1_, bf16[2048,1152]{1,0:T(8,128)(2,1)} %get-tuple-element.234.refs_2_, bf16[384,1152]{1,0:T(8,128)(2,1)} %bitcast.298, bf16[384,1152]{1,0:T(8,128)(2,1)} %bitcast.300, ...), custom_call_target="tpu_custom_call" | custom-call | flops 1 | bytes 1 | tf_op jit(solution)/shard_map/pallas_call | solution.py:352
  369.8 12.2 %convolution_convert_fusion.1 = bf16[1536,1152]{1,0:T(8,128)(2,1)S(1)} fusion(bf16[2048,1536]{1,0:T(8,128)(2,1)} %copy-done.9, bf16[2048,1152]{1,0:T(8,128)(2,1)} %get-tuple-element.234.refs_2_), kind=kOutput, calls=%fused_computation.2 | convolution fusion | flops 7249526784 | bytes 14548992 | tf_op jit(solution)/shard_map/dot_general | solution.py:48
  389.9 8.8 %convolution_convert_fusion = bf16[1536,1152]{1,0:T(8,128)(2,1)S(1)} fusion(bf16[2048,1536]{1,0:T(8,128)(2,1)S(1)} %bitcast.296, bf16[2048,1152]{1,0:T(8,128)(2,1)S(1)} %bitcast.304), kind=kOutput, calls=%fused_computation.1 | convolution fusion | flops 7249526784 | bytes 14548992 | tf_op jit(solution)/shard_map/dot_general | solution.py:48
  398.9 9.1 %collective-permute-done.39 = bf16[128,1536]{1,0:T(8,128)(2,1)S(1)} collective-permute-done((bf16[128,1536]{1,0:T(8,128)(2,1)S(1)}, bf16[128,1536]{1,0:T(8,128)(2,1)S(1)}, u32[]{:S(2)}, u32[]{:S(2)}) %collective-permute-start.39) | collective-permute-done | bytes 393248 | tf_op jit(solution)/shard_map/ppermute | solution.py:397
  419.2 15.0 %shard_map.258 = (bf16[1024,1536]{1,0:T(8,128)(2,1)}, bf16[1024,1536]{1,0:T(8,128)(2,1)}) custom-call(s32[1]{0:T(128)} %bitcast.24.refs_0_, bf16[2048,1152]{1,0:T(8,128)(2,1)} %get-tuple-element.245.refs_1_, bf16[384,1152]{1,0:T(8,128)(2,1)} %bitcast.292, bf16[384,1152]{1,0:T(8,128)(2,1)} %bitcast.294, bf16[384,1152]{1,0:T(8,128)(2,1)} %bitcast.311, ...), custom_call_target="tpu_custom_call" | custom-call | flops 1 | bytes 1 | tf_op jit(solution)/shard_map/pallas_call | solution.py:352
  435.2 6.1 collective-permute-done.44
  476.0 20.5 %shard_map.259 = (bf16[512,768]{1,0:T(8,128)(2,1)}, f32[512,256]{1,0:T(8,128)}, bf16[512,256]{1,0:T(8,128)(2,1)}, bf16[512,256]{1,0:T(8,128)(2,1)}, bf16[512,256]{1,0:T(8,128)(2,1)}) custom-call(s32[4]{0:T(128)} %and_convert_fusion.seen, bf16[512,768]{1,0:T(8,128)(2,1)} %get-tuple-element.260.q_ref, bf16[512,768]{1,0:T(8,128)(2,1)} %convolution_convert_fusion.4.g_ref, ...), custom_call_target="tpu_custom_call" | custom-call | flops 1 | bytes 1 | tf_op jit(solution)/shard_map/pallas_call | solution.py:184
  509.6 7.0 %shard_map.260 = bf16[1536,1536]{1,0:T(8,128)(2,1)} custom-call(bf16[512,1536]{1,0:T(8,128)(2,1)} %copy-done.22, bf16[512,768]{1,0:T(8,128)(2,1)} %get-tuple-element.285.b_ref, bf16[512,1536]{1,0:T(8,128)(2,1)} %pad_maximum_fusion.5.c_ref, bf16[512,768]{1,0:T(8,128)(2,1)} %get-tuple-element.190.d_ref), custom_call_target="tpu_custom_call" | custom-call | flops 1 | bytes 1 | tf_op jit(solution)/shard_map/pallas_call | solution.py:218
  528.7 10.0 %collective-permute-start.61 = (bf16[256,1536]{1,0:T(8,128)(2,1)}, bf16[256,1536]{1,0:T(8,128)(2,1)}, u32[]{:S(2)}, u32[]{:S(2)}) collective-permute-start(bf16[256,1536]{1,0:T(8,128)(2,1)} %pad_maximum_fusion.27), channel_id=1, source_target_pairs={{0,2},{2,0},{4,6},{6,4},{8,10},{10,8},{12,14},{14,12},{16,18},{18,... | collective-permute-start | bytes 2359304 | tf_op jit(solution)/shard_map/ppermute | solution.py:397
  549.3 7.5 %collective-permute-done.58 = bf16[192,1536]{1,0:T(8,128)(2,1)} collective-permute-done((bf16[192,1536]{1,0:T(8,128)(2,1)}, bf16[192,1536]{1,0:T(8,128)(2,1)}, u32[]{:S(2)}, u32[]{:S(2)}) %collective-permute-start.58) | collective-permute-done | bytes 589856 | tf_op jit(solution)/shard_map/ppermute | solution.py:397
  574.6 19.2 %collective-permute-done.66 = bf16[208,256]{1,0:T(8,128)(2,1)S(1)} collective-permute-done((bf16[208,256]{1,0:T(8,128)(2,1)S(1)}, bf16[208,256]{1,0:T(8,128)(2,1)S(1)}, u32[]{:S(2)}, u32[]{:S(2)}) %collective-permute-start.66) | collective-permute-done | bytes 106528 | tf_op jit(solution)/shard_map/ppermute | solution.py:397
  (564 shorter events, 325.4 us)
Async XLA Ops:
  14.7 174.9 %all-gather.2.cloned.1.call-start = ((), (), s32[]{:S(2)}) async-start(), calls=%async_computation.6 | async-start | bytes 2506752 | tf_op jit(solution)/shard_map/all_gather | solution.py:571
  46.0 28.8 %collective-permute-start.2 = (bf16[416,1024]{1,0:T(8,128)(2,1)S(1)}, bf16[416,1024]{1,0:T(8,128)(2,1)S(1)}, u32[]{:S(2)}, u32[]{:S(2)}) collective-permute-start(bf16[416,1024]{1,0:T(8,128)(2,1)S(1)} %bitcast.331), channel_id=1, source_target_pairs={{0,8},{2,10},{4,12},{6,14},{8,0},{10,2},{12,4},{14,6},{16,24},{18,... | collective-permute-start | bytes 2555912 | tf_op jit(solution)/shard_map/ppermute | solution.py:397
  76.7 31.4 %collective-permute-start.7 = (bf16[2,96,1152]{2,1,0:T(8,128)(2,1)S(1)}, bf16[2,96,1152]{2,1,0:T(8,128)(2,1)}, u32[]{:S(2)}, u32[]{:S(2)}) collective-permute-start(bf16[2,96,1152]{2,1,0:T(8,128)(2,1)S(1)} %get-tuple-element.168), channel_id=1, source_target_pairs={{0,4},{2,6},{4,0},{6,2},{8,12},{10,14},{12,8},{14,10},{16,20},{18,... | collective-permute-start | bytes 1327112 | tf_op jit(solution)/shard_map/ppermute | solution.py:397
  76.7 32.2 %all-to-all-start.1 = ((bf16[4,96,1152]{2,1,0:T(8,128)(2,1)}), bf16[4,96,1152]{2,1,0:T(8,128)(2,1)}, u32[]{:S(2)}, u32[]{:S(2)}) async-start(bf16[4,96,1152]{2,1,0:T(8,128)(2,1)} %bitcast.281), calls=%async_computation.1 | async-start | bytes 1769472 | tf_op jit(solution)/shard_map/all_to_all | solution.py:483
  197.0 31.7 %collective-permute-start.21 = (bf16[2,2,96,1152]{3,2,1,0:T(8,128)(2,1)}, bf16[2,2,96,1152]{3,2,1,0:T(8,128)(2,1)}, u32[]{:S(2)}, u32[]{:S(2)}) collective-permute-start(bf16[2,2,96,1152]{3,2,1,0:T(8,128)(2,1)} %pad_maximum_fusion.13), channel_id=1, source_target_pairs={{0,16},{2,18},{4,20},{6,22},{8,24},{10,26},{12,28},{14,30},{16,0},... | collective-permute-start | bytes 2654216 | tf_op jit(solution)/shard_map/ppermute | solution.py:397
  197.0 30.2 %collective-permute-start.17 = (bf16[256,1536]{1,0:T(8,128)(2,1)}, bf16[256,1536]{1,0:T(8,128)(2,1)S(1)}, u32[]{:S(2)}, u32[]{:S(2)}) collective-permute-start(bf16[256,1536]{1,0:T(8,128)(2,1)} %multiply_convert_fusion.1), channel_id=1, source_target_pairs={{0,8},{2,10},{4,12},{6,14},{8,0},{10,2},{12,4},{14,6},{16,24},{18,... | collective-permute-start | bytes 2359304 | tf_op jit(solution)/shard_map/ppermute | solution.py:397
  199.6 29.0 %collective-permute-start.18 = (bf16[256,1536]{1,0:T(8,128)(2,1)}, bf16[256,1536]{1,0:T(8,128)(2,1)}, u32[]{:S(2)}, u32[]{:S(2)}) collective-permute-start(bf16[256,1536]{1,0:T(8,128)(2,1)} %multiply_convert_fusion.1), channel_id=1, source_target_pairs={{0,2},{2,0},{4,6},{6,4},{8,10},{10,8},{12,14},{14,12},{16,18},{18,... | collective-permute-start | bytes 2359304 | tf_op jit(solution)/shard_map/ppermute | solution.py:397
  200.4 28.2 %collective-permute-start.19 = (bf16[256,1536]{1,0:T(8,128)(2,1)}, bf16[256,1536]{1,0:T(8,128)(2,1)}, u32[]{:S(2)}, u32[]{:S(2)}) collective-permute-start(bf16[256,1536]{1,0:T(8,128)(2,1)} %multiply_convert_fusion.1), channel_id=1, source_target_pairs={{0,1},{1,0},{2,3},{3,2},{4,5},{5,4},{6,7},{7,6},{8,9},{9,8},{10,11... | collective-permute-start | bytes 2359304 | tf_op jit(solution)/shard_map/ppermute | solution.py:400
  227.2 32.5 %collective-permute-start.28 = (bf16[512,1536]{1,0:T(8,128)(2,1)S(1)}, bf16[512,1536]{1,0:T(8,128)(2,1)S(1)}, u32[]{:S(2)}, u32[]{:S(2)}) collective-permute-start(bf16[512,1536]{1,0:T(8,128)(2,1)S(1)} %pad_maximum_fusion.4), channel_id=1, source_target_pairs={{0,1},{1,0},{2,3},{3,2},{4,5},{5,4},{6,7},{7,6},{8,9},{9,8},{10,11... | collective-permute-start | bytes 4718600 | tf_op jit(solution)/shard_map/ppermute | solution.py:400
  229.9 28.7 %collective-permute-start.26 = (bf16[512,1536]{1,0:T(8,128)(2,1)S(1)}, bf16[512,1536]{1,0:T(8,128)(2,1)S(1)}, u32[]{:S(2)}, u32[]{:S(2)}) collective-permute-start(bf16[512,1536]{1,0:T(8,128)(2,1)S(1)} %pad_maximum_fusion.3), channel_id=1, source_target_pairs={{0,1},{1,0},{2,3},{3,2},{4,5},{5,4},{6,7},{7,6},{8,9},{9,8},{10,11... | collective-permute-start | bytes 4718600 | tf_op jit(solution)/shard_map/ppermute | solution.py:400
  230.2 28.4 %collective-permute-start.24 = (bf16[2,2,96,1152]{3,2,1,0:T(8,128)(2,1)S(1)}, bf16[2,2,96,1152]{3,2,1,0:T(8,128)(2,1)S(1)}, u32[]{:S(2)}, u32[]{:S(2)}) collective-permute-start(bf16[2,2,96,1152]{3,2,1,0:T(8,128)(2,1)S(1)} %pad_maximum_fusion.14), channel_id=1, source_target_pairs={{0,16},{2,18},{4,20},{6,22},{8,24},{10,26},{12,28},{14,30},{16,0},... | collective-permute-start | bytes 2654216 | tf_op jit(solution)/shard_map/ppermute | solution.py:397
  261.1 32.6 %collective-permute-start.31 = (bf16[2,2,96,1152]{3,2,1,0:T(8,128)(2,1)S(1)}, bf16[2,2,96,1152]{3,2,1,0:T(8,128)(2,1)S(1)}, u32[]{:S(2)}, u32[]{:S(2)}) collective-permute-start(bf16[2,2,96,1152]{3,2,1,0:T(8,128)(2,1)S(1)} %pad_maximum_fusion.15), channel_id=1, source_target_pairs={{0,16},{2,18},{4,20},{6,22},{8,24},{10,26},{12,28},{14,30},{16,0},... | collective-permute-start | bytes 2654216 | tf_op jit(solution)/shard_map/ppermute | solution.py:397
  262.7 30.9 %collective-permute-start.32 = (bf16[2,96,1152]{2,1,0:T(8,128)(2,1)S(1)}, bf16[2,96,1152]{2,1,0:T(8,128)(2,1)S(1)}, u32[]{:S(2)}, u32[]{:S(2)}) collective-permute-start(bf16[2,96,1152]{2,1,0:T(8,128)(2,1)S(1)} %get-tuple-element.212), channel_id=1, source_target_pairs={{0,4},{2,6},{4,0},{6,2},{8,12},{10,14},{12,8},{14,10},{16,20},{18,... | collective-permute-start | bytes 1327112 | tf_op jit(solution)/shard_map/ppermute | solution.py:397
  262.8 30.8 %collective-permute-start.29 = (bf16[128,1536]{1,0:T(8,128)(2,1)}, bf16[128,1536]{1,0:T(8,128)(2,1)S(1)}, u32[]{:S(2)}, u32[]{:S(2)}) collective-permute-start(bf16[128,1536]{1,0:T(8,128)(2,1)} %slice.387), channel_id=1, source_target_pairs={{0,2},{2,0},{4,6},{6,4},{8,10},{10,8},{12,14},{14,12},{16,18},{18,... | collective-permute-start | bytes 1179656 | tf_op jit(solution)/shard_map/ppermute | solution.py:397
  339.7 28.2 %collective-permute-start.37 = (bf16[2,2,96,1152]{3,2,1,0:T(8,128)(2,1)S(1)}, bf16[2,2,96,1152]{3,2,1,0:T(8,128)(2,1)}, u32[]{:S(2)}, u32[]{:S(2)}) collective-permute-start(bf16[2,2,96,1152]{3,2,1,0:T(8,128)(2,1)S(1)} %dynamic-slice_bitcast_fusion.4), channel_id=1, source_target_pairs={{0,16},{2,18},{4,20},{6,22},{8,24},{10,26},{12,28},{14,30},{16,0},... | collective-permute-start | bytes 2654216 | tf_op jit(solution)/shard_map/ppermute | solution.py:397
  410.6 30.8 %collective-permute-start.46 = (bf16[2,2,96,1152]{3,2,1,0:T(8,128)(2,1)}, bf16[2,2,96,1152]{3,2,1,0:T(8,128)(2,1)S(1)}, u32[]{:S(2)}, u32[]{:S(2)}) collective-permute-start(bf16[2,2,96,1152]{3,2,1,0:T(8,128)(2,1)} %dynamic-slice_bitcast_fusion.2), channel_id=1, source_target_pairs={{0,16},{2,18},{4,20},{6,22},{8,24},{10,26},{12,28},{14,30},{16,0},... | collective-permute-start | bytes 2654216 | tf_op jit(solution)/shard_map/ppermute | solution.py:397
  413.3 28.0 %collective-permute-start.44 = (bf16[256,1536]{1,0:T(8,128)(2,1)}, bf16[256,1536]{1,0:T(8,128)(2,1)}, u32[]{:S(2)}, u32[]{:S(2)}) collective-permute-start(bf16[256,1536]{1,0:T(8,128)(2,1)} %pad_maximum_fusion.25), channel_id=1, source_target_pairs={{0,2},{2,0},{4,6},{6,4},{8,10},{10,8},{12,14},{14,12},{16,18},{18,... | collective-permute-start | bytes 2359304 | tf_op jit(solution)/shard_map/ppermute | solution.py:397
  467.4 29.3 %collective-permute-start.51 = (bf16[2,2,96,1152]{3,2,1,0:T(8,128)(2,1)}, bf16[2,2,96,1152]{3,2,1,0:T(8,128)(2,1)}, u32[]{:S(2)}, u32[]{:S(2)}) collective-permute-start(bf16[2,2,96,1152]{3,2,1,0:T(8,128)(2,1)} %dynamic-slice_bitcast_fusion.1), channel_id=1, source_target_pairs={{0,16},{2,18},{4,20},{6,22},{8,24},{10,26},{12,28},{14,30},{16,0},... | collective-permute-start | bytes 2654216 | tf_op jit(solution)/shard_map/ppermute | solution.py:397
  518.8 30.5 %collective-permute-start.60 = (bf16[2,96,1152]{2,1,0:T(8,128)(2,1)}, bf16[2,96,1152]{2,1,0:T(8,128)(2,1)}, u32[]{:S(2)}, u32[]{:S(2)}) collective-permute-start(bf16[2,96,1152]{2,1,0:T(8,128)(2,1)} %dynamic-slice_bitcast_fusion.13), channel_id=1, source_target_pairs={{0,4},{2,6},{4,0},{6,2},{8,12},{10,14},{12,8},{14,10},{16,20},{18,... | collective-permute-start | bytes 1327112 | tf_op jit(solution)/shard_map/ppermute | solution.py:397
  528.7 30.8 %collective-permute-start.61 = (bf16[256,1536]{1,0:T(8,128)(2,1)}, bf16[256,1536]{1,0:T(8,128)(2,1)}, u32[]{:S(2)}, u32[]{:S(2)}) collective-permute-start(bf16[256,1536]{1,0:T(8,128)(2,1)} %pad_maximum_fusion.27), channel_id=1, source_target_pairs={{0,2},{2,0},{4,6},{6,4},{8,10},{10,8},{12,14},{14,12},{16,18},{18,... | collective-permute-start | bytes 2359304 | tf_op jit(solution)/shard_map/ppermute | solution.py:397
  563.3 31.4 %collective-permute-start.68 = (bf16[2,96,1152]{2,1,0:T(8,128)(2,1)S(1)}, bf16[2,96,1152]{2,1,0:T(8,128)(2,1)S(1)}, u32[]{:S(2)}, u32[]{:S(2)}) collective-permute-start(bf16[2,96,1152]{2,1,0:T(8,128)(2,1)S(1)} %dynamic-slice_bitcast_fusion.12), channel_id=1, source_target_pairs={{0,4},{2,6},{4,0},{6,2},{8,12},{10,14},{12,8},{14,10},{16,20},{18,... | collective-permute-start | bytes 1327112 | tf_op jit(solution)/shard_map/ppermute | solution.py:397
  564.2 30.5 %collective-permute-start.65 = (bf16[384,1536]{1,0:T(8,128)(2,1)S(1)}, bf16[384,1536]{1,0:T(8,128)(2,1)S(1)}, u32[]{:S(2)}, u32[]{:S(2)}) collective-permute-start(bf16[384,1536]{1,0:T(8,128)(2,1)S(1)} %pad_maximum_fusion.9), channel_id=1, source_target_pairs={{0,16},{2,18},{4,20},{6,22},{8,24},{10,26},{12,28},{14,30},{16,0},... | collective-permute-start | bytes 3538952 | tf_op jit(solution)/shard_map/ppermute | solution.py:397
  565.2 29.5 %collective-permute-start.64 = (bf16[384,1536]{1,0:T(8,128)(2,1)S(1)}, bf16[384,1536]{1,0:T(8,128)(2,1)S(1)}, u32[]{:S(2)}, u32[]{:S(2)}) collective-permute-start(bf16[384,1536]{1,0:T(8,128)(2,1)S(1)} %pad_maximum_fusion.8), channel_id=1, source_target_pairs={{0,8},{2,10},{4,12},{6,14},{8,0},{10,2},{12,4},{14,6},{16,24},{18,... | collective-permute-start | bytes 3538952 | tf_op jit(solution)/shard_map/ppermute | solution.py:397
  566.9 27.8 %collective-permute-start.67 = (bf16[208,256]{1,0:T(8,128)(2,1)S(1)}, bf16[208,256]{1,0:T(8,128)(2,1)S(1)}, u32[]{:S(2)}, u32[]{:S(2)}) collective-permute-start(bf16[208,256]{1,0:T(8,128)(2,1)S(1)} %get-tuple-element.384), channel_id=1, source_target_pairs={{0,8},{2,10},{4,12},{6,14},{8,0},{10,2},{12,4},{14,6},{16,24},{18,... | collective-permute-start | bytes 319496 | tf_op jit(solution)/shard_map/ppermute | solution.py:397
  (163 other events, 1799.8 us)
Sparse Core Ops, SparseCore 0:
  18.3 85.3 all-gather.1

commit v5 on v4

--- a/solution.py
+++ b/solution.py
@@ -729,8 +729,8 @@
     grad_gate, grad_up = hidden_grads(side, grads_in, down_full, by_gate, by_up)
     down_0, grad_gate, grad_up = grid.close(down_0, grad_gate, grad_up)
 
-    (down_1,) = grid.fence(half(grad_wdown, 1))
-    down_0, down_1 = fold_z(down_0), fold_y(down_1)
+    (grad_wdown,) = grid.fence(grad_wdown)
+    down_0, down_1 = fold_z(down_0), fold_y(half(grad_wdown, 1))
     part, give = hidden_back(side, (grad_gate, grad_up), (gate_full, up_full))
     down_0, down_1, part, give = grid.close(down_0, down_1, part, give)
 
@@ -747,9 +747,9 @@
     by_z, by_x, down_1, up_0, grad_wgate = grid.close(by_z, by_x, down_1, up_0, grad_wgate)
 
     px, pz = grid.tokens_add(px, pz, by_z, by_x)
-    up_1, act_in = grid.fence(half(grad_wup, 1), act)
+    grad_wup, act_in = grid.fence(grad_wup, act)
     px, pz = grid.over_x(px), grid.over_z(pz)
-    up_0, up_1 = fold_z(up_0), fold_y(up_1)
+    up_0, up_1 = fold_z(up_0), fold_y(half(grad_wup, 1))
     mlp_part, mlp_give = hidden_back(side, (act_in,), (down_full,))
     px, pz, up_0, up_1, mlp_part, mlp_give = grid.close(
         px, pz, up_0, up_1, mlp_part, mlp_give
@@ -768,9 +768,9 @@
     grad_heads, mlp_other, grad_wdown = grid.close(grad_heads, mlp_other, grad_wdown)
 
     mlp_own, mx, mz, far_z, far_x = grid.tokens_split(mlp_part, mlp_other)
-    gate_0, up_1 = grid.fence(half(grad_wgate, 0), up_1)
+    grad_wgate, up_1 = grid.fence(grad_wgate, up_1)
     by_z, by_x = grid.over_z(far_z), grid.over_x(far_x)
-    gate_0, up_1 = fold_y(gate_0), fold_z(up_1)
+    gate_0, up_1 = fold_y(half(grad_wgate, 0)), fold_z(up_1)
     grad_query, grad_pairs = attend_back(
         seen,
         queries,
@@ -789,8 +789,8 @@
 
     grad_got = [grid.one(x, r + 1) for r, x in enumerate(grad_pairs[1:])]
     mx, mz = grid.tokens_add(mx, mz, by_z, by_x)
-    (gate_1,) = grid.fence(half(grad_wgate, 1))
-    mx, gate_1 = grid.over_x(mx), fold_y(gate_1)
+    (grad_wgate,) = grid.fence(grad_wgate)
+    mx, gate_1 = grid.over_x(mx), fold_y(half(grad_wgate, 1))
     grad_attn = products(normed_one, grad_query, grad_low, out_low)
     mx, gate_1, grad_attn, *grad_got = grid.close(mx, gate_1, grad_attn, *grad_got)
 

time: 668 us -> 672 us (level)
  waiting for transfers between devices: 206 us -> 216 us
  Pallas kernels: 125 us -> 116 us
    unnamed x219 -> x233, local copies, waits for them, and re-layouts: 25.6 us -> 27.6 us
  transfers between devices with their start and end apart: 86 -> 86, of which waited for: 37 -> 38; matrix products, arithmetic and copies ran while one was open for 22% -> 22% of each run, Pallas kernels for 19% -> 18%
where the time goes in v5:
time: 672 us; the launch traced here: 664 us
  waiting for transfers between devices  216 us (32%)
  starting transfers between devices  127 us (19%)
  Pallas kernels  116 us (17%)
  other arithmetic  81.7 us (12%)
  local copies, waits for them, and re-layouts  60.7 us (9%)
  matrix products  44.8 us (7%)
  between operations  17.8 us (3%)
    ppermute x66, waiting for transfers between devices, one(): return lax.ppermute(x, BOTH, [(i, i ^ mask) for i in range(self.n)])  200 us
    ppermute x66, starting transfers between devices, one(): return lax.ppermute(x, BOTH, [(i, i ^ mask) for i in range(self.n)])  99.3 us
    pallas_call x2, Pallas kernels, hidden_back(): return call(side, *lefts, *[x for w in rights for x in w])  39.4 us
    dot_general x4, matrix products, dot_tn(): lax.dot_general(left, right, (((0,), (0,)), ((), ())), preferred_element_...  35.6 us
    unnamed x233, local copies, waits for them, and re-layouts  27.6 us
    pallas_call x1, Pallas kernels, hidden_units(): return call(side, normed, *gate_w, *up_w)  24.3 us
    pallas_call x1, Pallas kernels, hidden_grads(): return call(side, grads, by_gate, by_up, *down_w)  17.2 us
    pallas_call x1, Pallas kernels, attend_back(): pl.pallas_call(functools.partial(attend_back_kernel, count, scale), grid_...  15.9 us
  transfers between devices with their start and end apart: 86, of which 38 were waited for; matrix products, arithmetic and copies ran while one was open for 22% of the time, Pallas kernels for 18%

profile of v5, /device:TPU:0, one launch (start us, length us, event | category | flops | bytes accessed | tf_op | source)
XLA Modules:
  0.0 663.6 jit_solution(5819168643465871148)
XLA Ops:
  20.6 8.4 %collective-permute-done = bf16[104,1024]{1,0:T(8,128)(2,1)S(1)} collective-permute-done((bf16[104,1024]{1,0:T(8,128)(2,1)S(1)}, bf16[104,1024]{1,0:T(8,128)(2,1)S(1)}, u32[]{:S(2)}, u32[]{:S(2)}) %collective-permute-start) | collective-permute-done | bytes 213024 | tf_op jit(solution)/shard_map/ppermute | solution.py:397
  36.2 8.9 %collective-permute-done.1 = bf16[2,104,1024]{2,1,0:T(8,128)(2,1)S(1)} collective-permute-done((bf16[2,104,1024]{2,1,0:T(8,128)(2,1)S(1)}, bf16[2,104,1024]{2,1,0:T(8,128)(2,1)S(1)}, u32[]{:S(2)}, u32[]{:S(2)}) %collective-permute-start.1) | collective-permute-done | bytes 426016 | tf_op jit(solution)/shard_map/ppermute | solution.py:397
  51.5 23.1 %collective-permute-done.4 = bf16[2,96,1152]{2,1,0:T(8,128)(2,1)S(1)} collective-permute-done((bf16[2,96,1152]{2,1,0:T(8,128)(2,1)S(1)}, bf16[2,96,1152]{2,1,0:T(8,128)(2,1)S(1)}, u32[]{:S(2)}, u32[]{:S(2)}) %collective-permute-start.4) | collective-permute-done | bytes 442400 | tf_op jit(solution)/shard_map/ppermute | solution.py:397
  93.1 9.5 %collective-permute-done.6 = bf16[208,1024]{1,0:T(8,128)(2,1)} collective-permute-done((bf16[208,1024]{1,0:T(8,128)(2,1)}, bf16[208,1024]{1,0:T(8,128)(2,1)}, u32[]{:S(2)}, u32[]{:S(2)}) %collective-permute-start.6) | collective-permute-done | bytes 426016 | tf_op jit(solution)/shard_map/ppermute | solution.py:397
  125.0 10.2 %collective-permute-done.9 = bf16[256,1536]{1,0:T(8,128)(2,1)} collective-permute-done((bf16[256,1536]{1,0:T(8,128)(2,1)}, bf16[256,1536]{1,0:T(8,128)(2,1)}, u32[]{:S(2)}, u32[]{:S(2)}) %collective-permute-start.9) | collective-permute-done | bytes 786464 | tf_op jit(solution)/shard_map/ppermute | solution.py:397
  150.4 10.6 %collective-permute-done.13.refs_2_ = bf16[512,256]{1,0:T(8,128)(2,1)S(1)} collective-permute-done((bf16[512,256]{1,0:T(8,128)(2,1)S(1)}, bf16[512,256]{1,0:T(8,128)(2,1)S(1)}, u32[]{:S(2)}, u32[]{:S(2)}) %collective-permute-start.13) | collective-permute-done | bytes 262176 | tf_op jit(solution)/shard_map/ppermute | solution.py:397
  172.9 12.4 %shard_map.254 = (bf16[512,768]{1,0:T(8,128)(2,1)}, f32[512,768]{1,0:T(8,128)}, bf16[512,768]{1,0:T(8,128)(2,1)}, f32[6,1,512]{2,1,0:T(1,128)}) custom-call(s32[4]{0:T(128)} %and_convert_fusion.seen, f32[512,1024]{1,0:T(8,128)} %copy-done.23, f32[512,128]{1,0:T(8,128)} %get-tuple-element.394.cos_ref, f32[512,128]{1,0:T(8,128)} %get-tuple-element.318.sin_ref, ...), custom_call_target="tpu_custom_call" | custom-call | flops 1 | bytes 1 | tf_op jit(solution)/shard_map/pallas_call | solution.py:110
  209.3 18.2 %collective-permute-done.20 = bf16[2,96,1152]{2,1,0:T(8,128)(2,1)S(1)} collective-permute-done((bf16[2,96,1152]{2,1,0:T(8,128)(2,1)S(1)}, bf16[2,96,1152]{2,1,0:T(8,128)(2,1)S(1)}, u32[]{:S(2)}, u32[]{:S(2)}) %collective-permute-start.20) | collective-permute-done | bytes 442400 | tf_op jit(solution)/shard_map/ppermute | solution.py:397
  238.1 8.1 %collective-permute-done.22 = bf16[128,1536]{1,0:T(8,128)(2,1)S(1)} collective-permute-done((bf16[128,1536]{1,0:T(8,128)(2,1)S(1)}, bf16[128,1536]{1,0:T(8,128)(2,1)S(1)}, u32[]{:S(2)}, u32[]{:S(2)}) %collective-permute-start.22) | collective-permute-done | bytes 393248 | tf_op jit(solution)/shard_map/ppermute | solution.py:397
  249.2 7.4 %collective-permute-done.23 = bf16[128,1536]{1,0:T(8,128)(2,1)S(1)} collective-permute-done((bf16[128,1536]{1,0:T(8,128)(2,1)S(1)}, bf16[128,1536]{1,0:T(8,128)(2,1)S(1)}, u32[]{:S(2)}, u32[]{:S(2)}) %collective-permute-start.23) | collective-permute-done | bytes 393248 | tf_op jit(solution)/shard_map/ppermute | solution.py:397
  269.5 24.3 %shard_map.255 = (bf16[2048,1152]{1,0:T(8,128)(2,1)}, bf16[2048,1152]{1,0:T(8,128)(2,1)}, bf16[2048,1152]{1,0:T(8,128)(2,1)}) custom-call(s32[1]{0:T(128)} %bitcast.24.refs_0_, bf16[2048,1536]{1,0:T(8,128)(2,1)} %copy-done.9, bf16[384,1152]{1,0:T(8,128)(2,1)} %bitcast.290, bf16[384,1152]{1,0:T(8,128)(2,1)} %bitcast.292, ...), custom_call_target="tpu_custom_call" | custom-call | flops 1 | bytes 1 | tf_op jit(solution)/shard_map/pallas_call | solution.py:294
  301.2 11.0 %convolution_convert_fusion.2 = bf16[1536,1152]{1,0:T(8,128)(2,1)S(1)} fusion(bf16[2048,1536]{1,0:T(8,128)(2,1)} %constant_dynamic-update-slice_fusion.8.refs_1_, bf16[2048,1152]{1,0:T(8,128)(2,1)S(1)} %copy-done.22), kind=kOutput, calls=%fused_computation.3 | convolution fusion | flops 7249526784 | bytes 14548992 | tf_op jit(solution)/shard_map/dot_general | solution.py:48
  319.3 17.2 %shard_map.256 = (bf16[2048,1152]{1,0:T(8,128)(2,1)}, bf16[2048,1152]{1,0:T(8,128)(2,1)}) custom-call(s32[1]{0:T(128)} %bitcast.24.refs_0_, bf16[2048,1536]{1,0:T(8,128)(2,1)} %constant_dynamic-update-slice_fusion.8.refs_1_, bf16[2048,1152]{1,0:T(8,128)(2,1)} %get-tuple-element.218.refs_2_, bf16[2048,1152]{1,0:T(8,128)(2,1)} %get-tuple-element.219.refs_3_, ...), custom_call_target="tpu_custom_call" | custom-call | flops 1 | bytes 1 | tf_op jit(solution)/shard_map/pallas_call | solution.py:313
  342.5 24.4 %shard_map.257 = (bf16[1024,1536]{1,0:T(8,128)(2,1)}, bf16[1024,1536]{1,0:T(8,128)(2,1)}) custom-call(s32[1]{0:T(128)} %bitcast.24.refs_0_, bf16[2048,1152]{1,0:T(8,128)(2,1)} %get-tuple-element.238.refs_1_, bf16[2048,1152]{1,0:T(8,128)(2,1)} %get-tuple-element.234.refs_2_, bf16[384,1152]{1,0:T(8,128)(2,1)} %bitcast.291, bf16[384,1152]{1,0:T(8,128)(2,1)} %bitcast.293, ...), custom_call_target="tpu_custom_call" | custom-call | flops 1 | bytes 1 | tf_op jit(solution)/shard_map/pallas_call | solution.py:352
  371.2 13.0 %convolution_convert_fusion.1 = bf16[1536,1152]{1,0:T(8,128)(2,1)S(1)} fusion(bf16[2048,1536]{1,0:T(8,128)(2,1)} %copy-done.9, bf16[2048,1152]{1,0:T(8,128)(2,1)} %get-tuple-element.234.refs_2_), kind=kOutput, calls=%fused_computation.2 | convolution fusion | flops 7249526784 | bytes 14548992 | tf_op jit(solution)/shard_map/dot_general | solution.py:48
  392.0 10.1 %convolution_convert_fusion = bf16[1536,1152]{1,0:T(8,128)(2,1)} fusion(bf16[2048,1536]{1,0:T(8,128)(2,1)S(1)} %bitcast.289, bf16[2048,1152]{1,0:T(8,128)(2,1)S(1)} %bitcast.297), kind=kOutput, calls=%fused_computation.1 | convolution fusion | flops 7249526784 | bytes 14548992 | tf_op jit(solution)/shard_map/dot_general | solution.py:48
  420.8 15.0 %shard_map.258 = (bf16[1024,1536]{1,0:T(8,128)(2,1)}, bf16[1024,1536]{1,0:T(8,128)(2,1)}) custom-call(s32[1]{0:T(128)} %bitcast.24.refs_0_, bf16[2048,1152]{1,0:T(8,128)(2,1)} %get-tuple-element.245.refs_1_, bf16[384,1152]{1,0:T(8,128)(2,1)} %bitcast.285, bf16[384,1152]{1,0:T(8,128)(2,1)} %bitcast.287, bf16[384,1152]{1,0:T(8,128)(2,1)} %bitcast.307, ...), custom_call_target="tpu_custom_call" | custom-call | flops 1 | bytes 1 | tf_op jit(solution)/shard_map/pallas_call | solution.py:352
  479.1 15.9 %shard_map.259 = (bf16[512,768]{1,0:T(8,128)(2,1)}, f32[512,256]{1,0:T(8,128)}, bf16[512,256]{1,0:T(8,128)(2,1)}, bf16[512,256]{1,0:T(8,128)(2,1)}, bf16[512,256]{1,0:T(8,128)(2,1)}) custom-call(s32[4]{0:T(128)} %and_convert_fusion.seen, bf16[512,768]{1,0:T(8,128)(2,1)} %get-tuple-element.260.q_ref, bf16[512,768]{1,0:T(8,128)(2,1)} %convolution_convert_fusion.4.g_ref, ...), custom_call_target="tpu_custom_call" | custom-call | flops 1 | bytes 1 | tf_op jit(solution)/shard_map/pallas_call | solution.py:184
  496.3 6.3 collective-permute-start.55
  512.4 7.0 %shard_map.260 = bf16[1536,1536]{1,0:T(8,128)(2,1)} custom-call(bf16[512,1536]{1,0:T(8,128)(2,1)} %copy-done.18, bf16[512,768]{1,0:T(8,128)(2,1)} %get-tuple-element.285.b_ref, bf16[512,1536]{1,0:T(8,128)(2,1)} %pad_maximum_fusion.5.c_ref, bf16[512,768]{1,0:T(8,128)(2,1)} %get-tuple-element.190.d_ref), custom_call_target="tpu_custom_call" | custom-call | flops 1 | bytes 1 | tf_op jit(solution)/shard_map/pallas_call | solution.py:218
  521.1 11.5 %collective-permute-done.56 = bf16[512,256]{1,0:T(8,128)(2,1)} collective-permute-done((bf16[512,256]{1,0:T(8,128)(2,1)}, bf16[512,256]{1,0:T(8,128)(2,1)}, u32[]{:S(2)}, u32[]{:S(2)}) %collective-permute-start.56) | collective-permute-done | bytes 262176 | tf_op jit(solution)/shard_map/ppermute | solution.py:397
  537.4 6.2 collective-permute-start.61
  552.7 8.2 %collective-permute-done.58 = bf16[192,1536]{1,0:T(8,128)(2,1)} collective-permute-done((bf16[192,1536]{1,0:T(8,128)(2,1)}, bf16[192,1536]{1,0:T(8,128)(2,1)}, u32[]{:S(2)}, u32[]{:S(2)}) %collective-permute-start.58) | collective-permute-done | bytes 589856 | tf_op jit(solution)/shard_map/ppermute | solution.py:397
  578.0 19.1 %collective-permute-done.66 = bf16[208,256]{1,0:T(8,128)(2,1)S(1)} collective-permute-done((bf16[208,256]{1,0:T(8,128)(2,1)S(1)}, bf16[208,256]{1,0:T(8,128)(2,1)S(1)}, u32[]{:S(2)}, u32[]{:S(2)}) %collective-permute-start.66) | collective-permute-done | bytes 106528 | tf_op jit(solution)/shard_map/ppermute | solution.py:397
  (581 shorter events, 340.1 us)
Async XLA Ops:
  14.7 172.3 %all-gather.2.cloned.1.call-start = ((), (), s32[]{:S(2)}) async-start(), calls=%async_computation.6 | async-start | bytes 2506752 | tf_op jit(solution)/shard_map/all_gather | solution.py:571
  45.3 29.4 %collective-permute-start.2 = (bf16[416,1024]{1,0:T(8,128)(2,1)S(1)}, bf16[416,1024]{1,0:T(8,128)(2,1)S(1)}, u32[]{:S(2)}, u32[]{:S(2)}) collective-permute-start(bf16[416,1024]{1,0:T(8,128)(2,1)S(1)} %bitcast.327), channel_id=1, source_target_pairs={{0,8},{2,10},{4,12},{6,14},{8,0},{10,2},{12,4},{14,6},{16,24},{18,... | collective-permute-start | bytes 2555912 | tf_op jit(solution)/shard_map/ppermute | solution.py:397
  46.8 27.9 %collective-permute-start.3 = (bf16[416,1024]{1,0:T(8,128)(2,1)S(1)}, bf16[416,1024]{1,0:T(8,128)(2,1)S(1)}, u32[]{:S(2)}, u32[]{:S(2)}) collective-permute-start(bf16[416,1024]{1,0:T(8,128)(2,1)S(1)} %bitcast.328), channel_id=1, source_target_pairs={{0,16},{2,18},{4,20},{6,22},{8,24},{10,26},{12,28},{14,30},{16,0},... | collective-permute-start | bytes 2555912 | tf_op jit(solution)/shard_map/ppermute | solution.py:397
  76.5 31.6 %collective-permute-start.7 = (bf16[2,96,1152]{2,1,0:T(8,128)(2,1)}, bf16[2,96,1152]{2,1,0:T(8,128)(2,1)}, u32[]{:S(2)}, u32[]{:S(2)}) collective-permute-start(bf16[2,96,1152]{2,1,0:T(8,128)(2,1)} %get-tuple-element.168), channel_id=1, source_target_pairs={{0,4},{2,6},{4,0},{6,2},{8,12},{10,14},{12,8},{14,10},{16,20},{18,... | collective-permute-start | bytes 1327112 | tf_op jit(solution)/shard_map/ppermute | solution.py:397
  76.5 32.2 %all-to-all-start.1 = ((bf16[4,96,1152]{2,1,0:T(8,128)(2,1)}), bf16[4,96,1152]{2,1,0:T(8,128)(2,1)}, u32[]{:S(2)}, u32[]{:S(2)}) async-start(bf16[4,96,1152]{2,1,0:T(8,128)(2,1)} %bitcast.274), calls=%async_computation.1 | async-start | bytes 1769472 | tf_op jit(solution)/shard_map/all_to_all | solution.py:483
  194.3 34.0 %collective-permute-start.21 = (bf16[2,2,96,1152]{3,2,1,0:T(8,128)(2,1)}, bf16[2,2,96,1152]{3,2,1,0:T(8,128)(2,1)}, u32[]{:S(2)}, u32[]{:S(2)}) collective-permute-start(bf16[2,2,96,1152]{3,2,1,0:T(8,128)(2,1)} %pad_maximum_fusion.13), channel_id=1, source_target_pairs={{0,16},{2,18},{4,20},{6,22},{8,24},{10,26},{12,28},{14,30},{16,0},... | collective-permute-start | bytes 2654216 | tf_op jit(solution)/shard_map/ppermute | solution.py:397
  197.5 29.9 %collective-permute-start.17 = (bf16[256,1536]{1,0:T(8,128)(2,1)}, bf16[256,1536]{1,0:T(8,128)(2,1)S(1)}, u32[]{:S(2)}, u32[]{:S(2)}) collective-permute-start(bf16[256,1536]{1,0:T(8,128)(2,1)} %multiply_convert_fusion.1), channel_id=1, source_target_pairs={{0,8},{2,10},{4,12},{6,14},{8,0},{10,2},{12,4},{14,6},{16,24},{18,... | collective-permute-start | bytes 2359304 | tf_op jit(solution)/shard_map/ppermute | solution.py:397
  197.5 30.8 %collective-permute-start.18 = (bf16[256,1536]{1,0:T(8,128)(2,1)}, bf16[256,1536]{1,0:T(8,128)(2,1)}, u32[]{:S(2)}, u32[]{:S(2)}) collective-permute-start(bf16[256,1536]{1,0:T(8,128)(2,1)} %multiply_convert_fusion.1), channel_id=1, source_target_pairs={{0,2},{2,0},{4,6},{6,4},{8,10},{10,8},{12,14},{14,12},{16,18},{18,... | collective-permute-start | bytes 2359304 | tf_op jit(solution)/shard_map/ppermute | solution.py:397
  227.5 32.4 %collective-permute-start.28 = (bf16[512,1536]{1,0:T(8,128)(2,1)S(1)}, bf16[512,1536]{1,0:T(8,128)(2,1)S(1)}, u32[]{:S(2)}, u32[]{:S(2)}) collective-permute-start(bf16[512,1536]{1,0:T(8,128)(2,1)S(1)} %pad_maximum_fusion.4), channel_id=1, source_target_pairs={{0,1},{1,0},{2,3},{3,2},{4,5},{5,4},{6,7},{7,6},{8,9},{9,8},{10,11... | collective-permute-start | bytes 4718600 | tf_op jit(solution)/shard_map/ppermute | solution.py:400
  229.6 29.2 %collective-permute-start.26 = (bf16[512,1536]{1,0:T(8,128)(2,1)S(1)}, bf16[512,1536]{1,0:T(8,128)(2,1)S(1)}, u32[]{:S(2)}, u32[]{:S(2)}) collective-permute-start(bf16[512,1536]{1,0:T(8,128)(2,1)S(1)} %pad_maximum_fusion.3), channel_id=1, source_target_pairs={{0,1},{1,0},{2,3},{3,2},{4,5},{5,4},{6,7},{7,6},{8,9},{9,8},{10,11... | collective-permute-start | bytes 4718600 | tf_op jit(solution)/shard_map/ppermute | solution.py:400
  229.9 28.9 %collective-permute-start.24 = (bf16[2,2,96,1152]{3,2,1,0:T(8,128)(2,1)S(1)}, bf16[2,2,96,1152]{3,2,1,0:T(8,128)(2,1)S(1)}, u32[]{:S(2)}, u32[]{:S(2)}) collective-permute-start(bf16[2,2,96,1152]{3,2,1,0:T(8,128)(2,1)S(1)} %pad_maximum_fusion.14), channel_id=1, source_target_pairs={{0,16},{2,18},{4,20},{6,22},{8,24},{10,26},{12,28},{14,30},{16,0},... | collective-permute-start | bytes 2654216 | tf_op jit(solution)/shard_map/ppermute | solution.py:397
  261.2 32.6 %collective-permute-start.31 = (bf16[2,2,96,1152]{3,2,1,0:T(8,128)(2,1)S(1)}, bf16[2,2,96,1152]{3,2,1,0:T(8,128)(2,1)S(1)}, u32[]{:S(2)}, u32[]{:S(2)}) collective-permute-start(bf16[2,2,96,1152]{3,2,1,0:T(8,128)(2,1)S(1)} %pad_maximum_fusion.15), channel_id=1, source_target_pairs={{0,16},{2,18},{4,20},{6,22},{8,24},{10,26},{12,28},{14,30},{16,0},... | collective-permute-start | bytes 2654216 | tf_op jit(solution)/shard_map/ppermute | solution.py:397
  262.9 31.0 %collective-permute-start.32 = (bf16[2,96,1152]{2,1,0:T(8,128)(2,1)S(1)}, bf16[2,96,1152]{2,1,0:T(8,128)(2,1)S(1)}, u32[]{:S(2)}, u32[]{:S(2)}) collective-permute-start(bf16[2,96,1152]{2,1,0:T(8,128)(2,1)S(1)} %get-tuple-element.212), channel_id=1, source_target_pairs={{0,4},{2,6},{4,0},{6,2},{8,12},{10,14},{12,8},{14,10},{16,20},{18,... | collective-permute-start | bytes 1327112 | tf_op jit(solution)/shard_map/ppermute | solution.py:397
  262.9 30.9 %collective-permute-start.29 = (bf16[128,1536]{1,0:T(8,128)(2,1)}, bf16[128,1536]{1,0:T(8,128)(2,1)S(1)}, u32[]{:S(2)}, u32[]{:S(2)}) collective-permute-start(bf16[128,1536]{1,0:T(8,128)(2,1)} %slice.387), channel_id=1, source_target_pairs={{0,2},{2,0},{4,6},{6,4},{8,10},{10,8},{12,14},{14,12},{16,18},{18,... | collective-permute-start | bytes 1179656 | tf_op jit(solution)/shard_map/ppermute | solution.py:397
  266.2 27.6 %collective-permute-start.30 = (bf16[128,1536]{1,0:T(8,128)(2,1)}, bf16[128,1536]{1,0:T(8,128)(2,1)S(1)}, u32[]{:S(2)}, u32[]{:S(2)}) collective-permute-start(bf16[128,1536]{1,0:T(8,128)(2,1)} %slice.388), channel_id=1, source_target_pairs={{0,8},{2,10},{4,12},{6,14},{8,0},{10,2},{12,4},{14,6},{16,24},{18,... | collective-permute-start | bytes 1179656 | tf_op jit(solution)/shard_map/ppermute | solution.py:397
  413.9 30.1 %collective-permute-start.46 = (bf16[2,2,96,1152]{3,2,1,0:T(8,128)(2,1)}, bf16[2,2,96,1152]{3,2,1,0:T(8,128)(2,1)}, u32[]{:S(2)}, u32[]{:S(2)}) collective-permute-start(bf16[2,2,96,1152]{3,2,1,0:T(8,128)(2,1)} %dynamic-slice_bitcast_fusion.2), channel_id=1, source_target_pairs={{0,16},{2,18},{4,20},{6,22},{8,24},{10,26},{12,28},{14,30},{16,0},... | collective-permute-start | bytes 2654216 | tf_op jit(solution)/shard_map/ppermute | solution.py:397
  416.0 28.1 %collective-permute-start.44 = (bf16[256,1536]{1,0:T(8,128)(2,1)}, bf16[256,1536]{1,0:T(8,128)(2,1)}, u32[]{:S(2)}, u32[]{:S(2)}) collective-permute-start(bf16[256,1536]{1,0:T(8,128)(2,1)} %pad_maximum_fusion.25), channel_id=1, source_target_pairs={{0,2},{2,0},{4,6},{6,4},{8,10},{10,8},{12,14},{14,12},{16,18},{18,... | collective-permute-start | bytes 2359304 | tf_op jit(solution)/shard_map/ppermute | solution.py:397
  502.5 30.0 %collective-permute-start.56 = (bf16[512,256]{1,0:T(8,128)(2,1)}, bf16[512,256]{1,0:T(8,128)(2,1)}, u32[]{:S(2)}, u32[]{:S(2)}) collective-permute-start(bf16[512,256]{1,0:T(8,128)(2,1)} %get-tuple-element.275), channel_id=1, source_target_pairs={{0,4},{2,6},{4,0},{6,2},{8,12},{10,14},{12,8},{14,10},{16,20},{18,... | collective-permute-start | bytes 786440 | tf_op jit(solution)/shard_map/ppermute | solution.py:397
  503.0 29.5 %collective-permute-start.57 = (bf16[512,256]{1,0:T(8,128)(2,1)}, bf16[512,256]{1,0:T(8,128)(2,1)}, u32[]{:S(2)}, u32[]{:S(2)}) collective-permute-start(bf16[512,256]{1,0:T(8,128)(2,1)} %get-tuple-element.276), channel_id=1, source_target_pairs={{0,6},{2,4},{4,2},{6,0},{8,14},{10,12},{12,10},{14,8},{16,22},{18,... | collective-permute-start | bytes 786440 | tf_op jit(solution)/shard_map/ppermute | solution.py:397
  520.6 32.1 %collective-permute-start.60 = (bf16[2,96,1152]{2,1,0:T(8,128)(2,1)}, bf16[2,96,1152]{2,1,0:T(8,128)(2,1)}, u32[]{:S(2)}, u32[]{:S(2)}) collective-permute-start(bf16[2,96,1152]{2,1,0:T(8,128)(2,1)} %dynamic-slice_bitcast_fusion.13), channel_id=1, source_target_pairs={{0,4},{2,6},{4,0},{6,2},{8,12},{10,14},{12,8},{14,10},{16,20},{18,... | collective-permute-start | bytes 1327112 | tf_op jit(solution)/shard_map/ppermute | solution.py:397
  566.4 31.8 %collective-permute-start.68 = (bf16[2,96,1152]{2,1,0:T(8,128)(2,1)S(1)}, bf16[2,96,1152]{2,1,0:T(8,128)(2,1)S(1)}, u32[]{:S(2)}, u32[]{:S(2)}) collective-permute-start(bf16[2,96,1152]{2,1,0:T(8,128)(2,1)S(1)} %dynamic-slice_bitcast_fusion.12), channel_id=1, source_target_pairs={{0,4},{2,6},{4,0},{6,2},{8,12},{10,14},{12,8},{14,10},{16,20},{18,... | collective-permute-start | bytes 1327112 | tf_op jit(solution)/shard_map/ppermute | solution.py:397
  567.5 30.7 %collective-permute-start.65 = (bf16[384,1536]{1,0:T(8,128)(2,1)S(1)}, bf16[384,1536]{1,0:T(8,128)(2,1)S(1)}, u32[]{:S(2)}, u32[]{:S(2)}) collective-permute-start(bf16[384,1536]{1,0:T(8,128)(2,1)S(1)} %pad_maximum_fusion.9), channel_id=1, source_target_pairs={{0,16},{2,18},{4,20},{6,22},{8,24},{10,26},{12,28},{14,30},{16,0},... | collective-permute-start | bytes 3538952 | tf_op jit(solution)/shard_map/ppermute | solution.py:397
  568.9 29.3 %collective-permute-start.64 = (bf16[384,1536]{1,0:T(8,128)(2,1)S(1)}, bf16[384,1536]{1,0:T(8,128)(2,1)S(1)}, u32[]{:S(2)}, u32[]{:S(2)}) collective-permute-start(bf16[384,1536]{1,0:T(8,128)(2,1)S(1)} %pad_maximum_fusion.8), channel_id=1, source_target_pairs={{0,8},{2,10},{4,12},{6,14},{8,0},{10,2},{12,4},{14,6},{16,24},{18,... | collective-permute-start | bytes 3538952 | tf_op jit(solution)/shard_map/ppermute | solution.py:397
  569.9 28.3 %collective-permute-start.67 = (bf16[208,256]{1,0:T(8,128)(2,1)S(1)}, bf16[208,256]{1,0:T(8,128)(2,1)S(1)}, u32[]{:S(2)}, u32[]{:S(2)}) collective-permute-start(bf16[208,256]{1,0:T(8,128)(2,1)S(1)} %get-tuple-element.378), channel_id=1, source_target_pairs={{0,8},{2,10},{4,12},{6,14},{8,0},{10,2},{12,4},{14,6},{16,24},{18,... | collective-permute-start | bytes 319496 | tf_op jit(solution)/shard_map/ppermute | solution.py:397
  (170 other events, 2906.8 us)
Sparse Core Ops, SparseCore 0:
  18.3 85.5 all-gather.1

commit v6 on v5

--- a/solution.py
+++ b/solution.py
@@ -795,7 +795,8 @@
     mx, gate_1, grad_attn, *grad_got = grid.close(mx, gate_1, grad_attn, *grad_got)
 
     far_y, far_x = grid.fsdp_far(grad_attn)
-    mz, grad_query = grid.fence(mz, grad_query)
+    mz, grad_query, up_in = grid.fence(mz, grad_query, joined(up_0, up_1))
+    grad_wup = grid.quarters_out(up_in)
     by_y, by_x = grid.over_y(far_y), grid.over_x(far_x)
     gate_0, mz = fold_z(gate_0), grid.over_z(mz)
     grad_pair = grad_pairs[0]
@@ -828,8 +829,8 @@
     grad_wkv = dot_tn(normed_one, grad_kv).reshape(grid.n, shard, wide)
     grad_wkv = jnp.concatenate([grad_wkv, small], axis=1).astype(BF)
     grad_wkv = grad_wkv.reshape(grid.n * (shard + 8), wide)
-    by_y, by_x, gate_0, mz, grad_wkv, grad_normed_one = grid.close(
-        by_y, by_x, gate_0, mz, grad_wkv, grad_normed_one
+    by_y, by_x, gate_0, mz, grad_wup, grad_wkv, grad_normed_one = grid.close(
+        by_y, by_x, gate_0, mz, grad_wup, grad_wkv, grad_normed_one
     )
 
     ax, ay = grid.fsdp_near(grad_attn, by_y, by_x)
@@ -845,17 +846,15 @@
 
     grad_attn = grid.fsdp_end(grad_attn, ax, ay)
     kx, ky = grid.fsdp_near(grad_wkv, by_y, by_x)
-    (up_in,) = grid.fence(joined(up_0, up_1))
+    (gate_in,) = grid.fence(joined(gate_0, gate_1))
     kx, ky = grid.over_x(kx), grid.over_y(ky)
     parts = [grid.one(grid.context_pick(grad_attn, r), r) for r in range(1, grid.nc)]
-    grad_wup = grid.quarters_out(up_in)
+    grad_wgate = grid.quarters_out(gate_in)
     grad_tokens, result = both(grad_tokens), both(result)
-    kx, ky, grad_wup, grad_tokens, result, *parts = grid.close(
-        kx, ky, grad_wup, grad_tokens, result, *parts
-    )
-
-    (gate_in,) = grid.fence(joined(gate_0, gate_1))
-    grad_wgate = grid.quarters_out(gate_in)
+    kx, ky, grad_wgate, grad_tokens, result, *parts = grid.close(
+        kx, ky, grad_wgate, grad_tokens, result, *parts
+    )
+
     grad_wkv = grid.fsdp_end(grad_wkv, kx, ky)
     terms = [grid.one(grid.context_pick(grad_wkv, r), r) for r in range(1, grid.nc)]
     grad_attn = grid.context_pick(grad_attn, 0).astype(F32)

time: 672 us -> 672 us (level)
  Pallas kernels: 116 us -> 107 us
  starting transfers between devices: 127 us -> 134 us
    unnamed x233 -> x225, local copies, waits for them, and re-layouts: 27.6 us -> 30.3 us
  transfers between devices with their start and end apart: 86 -> 86, of which waited for: 38 -> 41; matrix products, arithmetic and copies ran while one was open for 22% -> 22% of each run, Pallas kernels for 18% -> 16%
where the time goes in v6:
time: 672 us; the launch traced here: 663 us
  waiting for transfers between devices  210 us (31%)
  starting transfers between devices  134 us (20%)
  Pallas kernels  107 us (16%)
  other arithmetic  82.8 us (12%)
  local copies, waits for them, and re-layouts  66.7 us (10%)
  matrix products  44.8 us (7%)
  between operations  17.6 us (3%)
    ppermute x66, waiting for transfers between devices, one(): return lax.ppermute(x, BOTH, [(i, i ^ mask) for i in range(self.n)])  194 us
    ppermute x66, starting transfers between devices, one(): return lax.ppermute(x, BOTH, [(i, i ^ mask) for i in range(self.n)])  105 us
    pallas_call x2, Pallas kernels, hidden_back(): return call(side, *lefts, *[x for w in rights for x in w])  39.2 us
    dot_general x4, matrix products, dot_tn(): lax.dot_general(left, right, (((0,), (0,)), ((), ())), preferred_element_...  35.6 us
    unnamed x225, local copies, waits for them, and re-layouts  30.3 us
    pallas_call x1, Pallas kernels, hidden_units(): return call(side, normed, *gate_w, *up_w)  24.3 us
    pallas_call x1, Pallas kernels, hidden_grads(): return call(side, grads, by_gate, by_up, *down_w)  17.2 us
    all_to_all x3, starting transfers between devices, quarters_in(): lax.all_to_all(w, BOTH, 0, 0, axis_index_groups=self.quarter_groups())  15.4 us
  transfers between devices with their start and end apart: 86, of which 41 were waited for; matrix products, arithmetic and copies ran while one was open for 22% of the time, Pallas kernels for 16%

profile of v6, /device:TPU:0, one launch (start us, length us, event | category | flops | bytes accessed | tf_op | source)
XLA Modules:
  0.0 662.9 jit_solution(15380644100420177982)
XLA Ops:
  20.6 8.4 %collective-permute-done = bf16[104,1024]{1,0:T(8,128)(2,1)S(1)} collective-permute-done((bf16[104,1024]{1,0:T(8,128)(2,1)S(1)}, bf16[104,1024]{1,0:T(8,128)(2,1)S(1)}, u32[]{:S(2)}, u32[]{:S(2)}) %collective-permute-start) | collective-permute-done | bytes 213024 | tf_op jit(solution)/shard_map/ppermute | solution.py:397
  36.2 8.9 %collective-permute-done.1 = bf16[2,104,1024]{2,1,0:T(8,128)(2,1)S(1)} collective-permute-done((bf16[2,104,1024]{2,1,0:T(8,128)(2,1)S(1)}, bf16[2,104,1024]{2,1,0:T(8,128)(2,1)S(1)}, u32[]{:S(2)}, u32[]{:S(2)}) %collective-permute-start.1) | collective-permute-done | bytes 426016 | tf_op jit(solution)/shard_map/ppermute | solution.py:397
  51.5 23.2 %collective-permute-done.4 = bf16[2,96,1152]{2,1,0:T(8,128)(2,1)S(1)} collective-permute-done((bf16[2,96,1152]{2,1,0:T(8,128)(2,1)S(1)}, bf16[2,96,1152]{2,1,0:T(8,128)(2,1)S(1)}, u32[]{:S(2)}, u32[]{:S(2)}) %collective-permute-start.4) | collective-permute-done | bytes 442400 | tf_op jit(solution)/shard_map/ppermute | solution.py:397
  93.1 9.5 %collective-permute-done.6 = bf16[208,1024]{1,0:T(8,128)(2,1)} collective-permute-done((bf16[208,1024]{1,0:T(8,128)(2,1)}, bf16[208,1024]{1,0:T(8,128)(2,1)}, u32[]{:S(2)}, u32[]{:S(2)}) %collective-permute-start.6) | collective-permute-done | bytes 426016 | tf_op jit(solution)/shard_map/ppermute | solution.py:397
  125.0 10.1 %collective-permute-done.9 = bf16[256,1536]{1,0:T(8,128)(2,1)} collective-permute-done((bf16[256,1536]{1,0:T(8,128)(2,1)}, bf16[256,1536]{1,0:T(8,128)(2,1)}, u32[]{:S(2)}, u32[]{:S(2)}) %collective-permute-start.9) | collective-permute-done | bytes 786464 | tf_op jit(solution)/shard_map/ppermute | solution.py:397
  149.7 10.8 %collective-permute-done.13.refs_2_ = bf16[512,256]{1,0:T(8,128)(2,1)S(1)} collective-permute-done((bf16[512,256]{1,0:T(8,128)(2,1)S(1)}, bf16[512,256]{1,0:T(8,128)(2,1)S(1)}, u32[]{:S(2)}, u32[]{:S(2)}) %collective-permute-start.13) | collective-permute-done | bytes 262176 | tf_op jit(solution)/shard_map/ppermute | solution.py:397
  172.8 8.5 %shard_map.254 = (bf16[512,768]{1,0:T(8,128)(2,1)}, f32[512,768]{1,0:T(8,128)}, bf16[512,768]{1,0:T(8,128)(2,1)}, f32[6,1,512]{2,1,0:T(1,128)}) custom-call(s32[4]{0:T(128)} %and_convert_fusion.seen, f32[512,1024]{1,0:T(8,128)} %copy-done.23, f32[512,128]{1,0:T(8,128)} %get-tuple-element.396.cos_ref, f32[512,128]{1,0:T(8,128)} %get-tuple-element.320.sin_ref, ...), custom_call_target="tpu_custom_call" | custom-call | flops 1 | bytes 1 | tf_op jit(solution)/shard_map/pallas_call | solution.py:110
  209.4 18.1 %collective-permute-done.20 = bf16[2,96,1152]{2,1,0:T(8,128)(2,1)S(1)} collective-permute-done((bf16[2,96,1152]{2,1,0:T(8,128)(2,1)S(1)}, bf16[2,96,1152]{2,1,0:T(8,128)(2,1)S(1)}, u32[]{:S(2)}, u32[]{:S(2)}) %collective-permute-start.20) | collective-permute-done | bytes 442400 | tf_op jit(solution)/shard_map/ppermute | solution.py:397
  238.5 8.7 %collective-permute-done.22 = bf16[128,1536]{1,0:T(8,128)(2,1)S(1)} collective-permute-done((bf16[128,1536]{1,0:T(8,128)(2,1)S(1)}, bf16[128,1536]{1,0:T(8,128)(2,1)S(1)}, u32[]{:S(2)}, u32[]{:S(2)}) %collective-permute-start.22) | collective-permute-done | bytes 393248 | tf_op jit(solution)/shard_map/ppermute | solution.py:397
  249.0 8.6 %collective-permute-done.23 = bf16[128,1536]{1,0:T(8,128)(2,1)S(1)} collective-permute-done((bf16[128,1536]{1,0:T(8,128)(2,1)S(1)}, bf16[128,1536]{1,0:T(8,128)(2,1)S(1)}, u32[]{:S(2)}, u32[]{:S(2)}) %collective-permute-start.23) | collective-permute-done | bytes 393248 | tf_op jit(solution)/shard_map/ppermute | solution.py:397
  269.5 24.3 %shard_map.255 = (bf16[2048,1152]{1,0:T(8,128)(2,1)}, bf16[2048,1152]{1,0:T(8,128)(2,1)}, bf16[2048,1152]{1,0:T(8,128)(2,1)}) custom-call(s32[1]{0:T(128)} %bitcast.24.refs_0_, bf16[2048,1536]{1,0:T(8,128)(2,1)} %copy-done.9, bf16[384,1152]{1,0:T(8,128)(2,1)} %bitcast.288, bf16[384,1152]{1,0:T(8,128)(2,1)} %bitcast.290, ...), custom_call_target="tpu_custom_call" | custom-call | flops 1 | bytes 1 | tf_op jit(solution)/shard_map/pallas_call | solution.py:294
  301.1 11.0 %convolution_convert_fusion.2 = bf16[1536,1152]{1,0:T(8,128)(2,1)S(1)} fusion(bf16[2048,1536]{1,0:T(8,128)(2,1)} %constant_dynamic-update-slice_fusion.8.refs_1_, bf16[2048,1152]{1,0:T(8,128)(2,1)S(1)} %copy-done.22), kind=kOutput, calls=%fused_computation.3 | convolution fusion | flops 7249526784 | bytes 14548992 | tf_op jit(solution)/shard_map/dot_general | solution.py:48
  319.3 17.2 %shard_map.256 = (bf16[2048,1152]{1,0:T(8,128)(2,1)}, bf16[2048,1152]{1,0:T(8,128)(2,1)}) custom-call(s32[1]{0:T(128)} %bitcast.24.refs_0_, bf16[2048,1536]{1,0:T(8,128)(2,1)} %constant_dynamic-update-slice_fusion.8.refs_1_, bf16[2048,1152]{1,0:T(8,128)(2,1)} %get-tuple-element.219.refs_2_, bf16[2048,1152]{1,0:T(8,128)(2,1)} %get-tuple-element.220.refs_3_, ...), custom_call_target="tpu_custom_call" | custom-call | flops 1 | bytes 1 | tf_op jit(solution)/shard_map/pallas_call | solution.py:313
  342.5 24.4 %shard_map.257 = (bf16[1024,1536]{1,0:T(8,128)(2,1)}, bf16[1024,1536]{1,0:T(8,128)(2,1)}) custom-call(s32[1]{0:T(128)} %bitcast.24.refs_0_, bf16[2048,1152]{1,0:T(8,128)(2,1)} %get-tuple-element.239.refs_1_, bf16[2048,1152]{1,0:T(8,128)(2,1)} %get-tuple-element.235.refs_2_, bf16[384,1152]{1,0:T(8,128)(2,1)} %bitcast.289, bf16[384,1152]{1,0:T(8,128)(2,1)} %bitcast.291, ...), custom_call_target="tpu_custom_call" | custom-call | flops 1 | bytes 1 | tf_op jit(solution)/shard_map/pallas_call | solution.py:352
  370.6 13.0 %convolution_convert_fusion.1 = bf16[1536,1152]{1,0:T(8,128)(2,1)S(1)} fusion(bf16[2048,1536]{1,0:T(8,128)(2,1)} %copy-done.9, bf16[2048,1152]{1,0:T(8,128)(2,1)} %get-tuple-element.235.refs_2_), kind=kOutput, calls=%fused_computation.2 | convolution fusion | flops 7249526784 | bytes 14548992 | tf_op jit(solution)/shard_map/dot_general | solution.py:48
  391.9 10.1 %convolution_convert_fusion = bf16[1536,1152]{1,0:T(8,128)(2,1)} fusion(bf16[2048,1536]{1,0:T(8,128)(2,1)S(1)} %bitcast.287, bf16[2048,1152]{1,0:T(8,128)(2,1)S(1)} %bitcast.295), kind=kOutput, calls=%fused_computation.1 | convolution fusion | flops 7249526784 | bytes 14548992 | tf_op jit(solution)/shard_map/dot_general | solution.py:48
  420.3 14.8 %shard_map.258 = (bf16[1024,1536]{1,0:T(8,128)(2,1)}, bf16[1024,1536]{1,0:T(8,128)(2,1)}) custom-call(s32[1]{0:T(128)} %bitcast.24.refs_0_, bf16[2048,1152]{1,0:T(8,128)(2,1)} %get-tuple-element.246.refs_1_, bf16[384,1152]{1,0:T(8,128)(2,1)} %bitcast.283, bf16[384,1152]{1,0:T(8,128)(2,1)} %bitcast.285, bf16[384,1152]{1,0:T(8,128)(2,1)} %bitcast.305, ...), custom_call_target="tpu_custom_call" | custom-call | flops 1 | bytes 1 | tf_op jit(solution)/shard_map/pallas_call | solution.py:352
  478.3 11.3 %shard_map.259 = (bf16[512,768]{1,0:T(8,128)(2,1)}, f32[512,256]{1,0:T(8,128)}, bf16[512,256]{1,0:T(8,128)(2,1)}, bf16[512,256]{1,0:T(8,128)(2,1)}, bf16[512,256]{1,0:T(8,128)(2,1)}) custom-call(s32[4]{0:T(128)} %and_convert_fusion.seen, bf16[512,768]{1,0:T(8,128)(2,1)} %get-tuple-element.261.q_ref, bf16[512,768]{1,0:T(8,128)(2,1)} %convolution_convert_fusion.4.g_ref, ...), custom_call_target="tpu_custom_call" | custom-call | flops 1 | bytes 1 | tf_op jit(solution)/shard_map/pallas_call | solution.py:184
  493.6 8.1 %collective-permute-start.55 = (bf16[512,256]{1,0:T(8,128)(2,1)}, bf16[512,256]{1,0:T(8,128)(2,1)}, u32[]{:S(2)}, u32[]{:S(2)}) collective-permute-start(bf16[512,256]{1,0:T(8,128)(2,1)} %get-tuple-element.275), channel_id=1, source_target_pairs={{0,2},{2,0},{4,6},{6,4},{8,10},{10,8},{12,14},{14,12},{16,18},{18,... | collective-permute-start | bytes 786440 | tf_op jit(solution)/shard_map/ppermute | solution.py:397
  512.0 6.8 %shard_map.260 = bf16[1536,1536]{1,0:T(8,128)(2,1)} custom-call(bf16[512,1536]{1,0:T(8,128)(2,1)} %copy-done.18, bf16[512,768]{1,0:T(8,128)(2,1)} %get-tuple-element.287.b_ref, bf16[512,1536]{1,0:T(8,128)(2,1)} %pad_maximum_fusion.5.c_ref, bf16[512,768]{1,0:T(8,128)(2,1)} %get-tuple-element.191.d_ref), custom_call_target="tpu_custom_call" | custom-call | flops 1 | bytes 1 | tf_op jit(solution)/shard_map/pallas_call | solution.py:218
  534.5 10.8 %collective-permute-start.61 = (bf16[256,1536]{1,0:T(8,128)(2,1)}, bf16[256,1536]{1,0:T(8,128)(2,1)}, u32[]{:S(2)}, u32[]{:S(2)}) collective-permute-start(bf16[256,1536]{1,0:T(8,128)(2,1)} %pad_maximum_fusion.27), channel_id=1, source_target_pairs={{0,2},{2,0},{4,6},{6,4},{8,10},{10,8},{12,14},{14,12},{16,18},{18,... | collective-permute-start | bytes 2359304 | tf_op jit(solution)/shard_map/ppermute | solution.py:397
  568.8 6.2 collective-permute-done.59
  591.5 17.2 %collective-permute-done.66 = bf16[208,256]{1,0:T(8,128)(2,1)S(1)} collective-permute-done((bf16[208,256]{1,0:T(8,128)(2,1)S(1)}, bf16[208,256]{1,0:T(8,128)(2,1)S(1)}, u32[]{:S(2)}, u32[]{:S(2)}) %collective-permute-start.66) | collective-permute-done | bytes 106528 | tf_op jit(solution)/shard_map/ppermute | solution.py:397
  631.5 6.5 collective-permute-done.69
  (572 shorter events, 348.9 us)
Async XLA Ops:
  14.7 172.6 %all-gather.2.cloned.1.call-start = ((), (), s32[]{:S(2)}) async-start(), calls=%async_computation.6 | async-start | bytes 2506752 | tf_op jit(solution)/shard_map/all_gather | solution.py:571
  45.3 29.4 %collective-permute-start.2 = (bf16[416,1024]{1,0:T(8,128)(2,1)S(1)}, bf16[416,1024]{1,0:T(8,128)(2,1)S(1)}, u32[]{:S(2)}, u32[]{:S(2)}) collective-permute-start(bf16[416,1024]{1,0:T(8,128)(2,1)S(1)} %bitcast.325), channel_id=1, source_target_pairs={{0,8},{2,10},{4,12},{6,14},{8,0},{10,2},{12,4},{14,6},{16,24},{18,... | collective-permute-start | bytes 2555912 | tf_op jit(solution)/shard_map/ppermute | solution.py:397
  46.8 27.9 %collective-permute-start.3 = (bf16[416,1024]{1,0:T(8,128)(2,1)S(1)}, bf16[416,1024]{1,0:T(8,128)(2,1)S(1)}, u32[]{:S(2)}, u32[]{:S(2)}) collective-permute-start(bf16[416,1024]{1,0:T(8,128)(2,1)S(1)} %bitcast.326), channel_id=1, source_target_pairs={{0,16},{2,18},{4,20},{6,22},{8,24},{10,26},{12,28},{14,30},{16,0},... | collective-permute-start | bytes 2555912 | tf_op jit(solution)/shard_map/ppermute | solution.py:397
  76.5 31.6 %collective-permute-start.7 = (bf16[2,96,1152]{2,1,0:T(8,128)(2,1)}, bf16[2,96,1152]{2,1,0:T(8,128)(2,1)}, u32[]{:S(2)}, u32[]{:S(2)}) collective-permute-start(bf16[2,96,1152]{2,1,0:T(8,128)(2,1)} %get-tuple-element.169), channel_id=1, source_target_pairs={{0,4},{2,6},{4,0},{6,2},{8,12},{10,14},{12,8},{14,10},{16,20},{18,... | collective-permute-start | bytes 1327112 | tf_op jit(solution)/shard_map/ppermute | solution.py:397
  76.5 32.2 %all-to-all-start.1 = ((bf16[4,96,1152]{2,1,0:T(8,128)(2,1)}), bf16[4,96,1152]{2,1,0:T(8,128)(2,1)}, u32[]{:S(2)}, u32[]{:S(2)}) async-start(bf16[4,96,1152]{2,1,0:T(8,128)(2,1)} %bitcast.274), calls=%async_computation.1 | async-start | bytes 1769472 | tf_op jit(solution)/shard_map/all_to_all | solution.py:483
  194.6 33.8 %collective-permute-start.21 = (bf16[2,2,96,1152]{3,2,1,0:T(8,128)(2,1)}, bf16[2,2,96,1152]{3,2,1,0:T(8,128)(2,1)}, u32[]{:S(2)}, u32[]{:S(2)}) collective-permute-start(bf16[2,2,96,1152]{3,2,1,0:T(8,128)(2,1)} %pad_maximum_fusion.13), channel_id=1, source_target_pairs={{0,16},{2,18},{4,20},{6,22},{8,24},{10,26},{12,28},{14,30},{16,0},... | collective-permute-start | bytes 2654216 | tf_op jit(solution)/shard_map/ppermute | solution.py:397
  197.5 29.9 %collective-permute-start.17 = (bf16[256,1536]{1,0:T(8,128)(2,1)}, bf16[256,1536]{1,0:T(8,128)(2,1)S(1)}, u32[]{:S(2)}, u32[]{:S(2)}) collective-permute-start(bf16[256,1536]{1,0:T(8,128)(2,1)} %multiply_convert_fusion.1), channel_id=1, source_target_pairs={{0,8},{2,10},{4,12},{6,14},{8,0},{10,2},{12,4},{14,6},{16,24},{18,... | collective-permute-start | bytes 2359304 | tf_op jit(solution)/shard_map/ppermute | solution.py:397
  198.9 29.5 %collective-permute-start.18 = (bf16[256,1536]{1,0:T(8,128)(2,1)}, bf16[256,1536]{1,0:T(8,128)(2,1)}, u32[]{:S(2)}, u32[]{:S(2)}) collective-permute-start(bf16[256,1536]{1,0:T(8,128)(2,1)} %multiply_convert_fusion.1), channel_id=1, source_target_pairs={{0,2},{2,0},{4,6},{6,4},{8,10},{10,8},{12,14},{14,12},{16,18},{18,... | collective-permute-start | bytes 2359304 | tf_op jit(solution)/shard_map/ppermute | solution.py:397
  227.5 32.7 %collective-permute-start.28 = (bf16[512,1536]{1,0:T(8,128)(2,1)S(1)}, bf16[512,1536]{1,0:T(8,128)(2,1)S(1)}, u32[]{:S(2)}, u32[]{:S(2)}) collective-permute-start(bf16[512,1536]{1,0:T(8,128)(2,1)S(1)} %pad_maximum_fusion.4), channel_id=1, source_target_pairs={{0,1},{1,0},{2,3},{3,2},{4,5},{5,4},{6,7},{7,6},{8,9},{9,8},{10,11... | collective-permute-start | bytes 4718600 | tf_op jit(solution)/shard_map/ppermute | solution.py:400
  229.6 29.5 %collective-permute-start.26 = (bf16[512,1536]{1,0:T(8,128)(2,1)S(1)}, bf16[512,1536]{1,0:T(8,128)(2,1)S(1)}, u32[]{:S(2)}, u32[]{:S(2)}) collective-permute-start(bf16[512,1536]{1,0:T(8,128)(2,1)S(1)} %pad_maximum_fusion.3), channel_id=1, source_target_pairs={{0,1},{1,0},{2,3},{3,2},{4,5},{5,4},{6,7},{7,6},{8,9},{9,8},{10,11... | collective-permute-start | bytes 4718600 | tf_op jit(solution)/shard_map/ppermute | solution.py:400
  229.9 29.2 %collective-permute-start.24 = (bf16[2,2,96,1152]{3,2,1,0:T(8,128)(2,1)S(1)}, bf16[2,2,96,1152]{3,2,1,0:T(8,128)(2,1)S(1)}, u32[]{:S(2)}, u32[]{:S(2)}) collective-permute-start(bf16[2,2,96,1152]{3,2,1,0:T(8,128)(2,1)S(1)} %pad_maximum_fusion.14), channel_id=1, source_target_pairs={{0,16},{2,18},{4,20},{6,22},{8,24},{10,26},{12,28},{14,30},{16,0},... | collective-permute-start | bytes 2654216 | tf_op jit(solution)/shard_map/ppermute | solution.py:397
  261.5 32.3 %collective-permute-start.31 = (bf16[2,2,96,1152]{3,2,1,0:T(8,128)(2,1)S(1)}, bf16[2,2,96,1152]{3,2,1,0:T(8,128)(2,1)S(1)}, u32[]{:S(2)}, u32[]{:S(2)}) collective-permute-start(bf16[2,2,96,1152]{3,2,1,0:T(8,128)(2,1)S(1)} %pad_maximum_fusion.15), channel_id=1, source_target_pairs={{0,16},{2,18},{4,20},{6,22},{8,24},{10,26},{12,28},{14,30},{16,0},... | collective-permute-start | bytes 2654216 | tf_op jit(solution)/shard_map/ppermute | solution.py:397
  263.1 30.7 %collective-permute-start.32 = (bf16[2,96,1152]{2,1,0:T(8,128)(2,1)S(1)}, bf16[2,96,1152]{2,1,0:T(8,128)(2,1)S(1)}, u32[]{:S(2)}, u32[]{:S(2)}) collective-permute-start(bf16[2,96,1152]{2,1,0:T(8,128)(2,1)S(1)} %get-tuple-element.213), channel_id=1, source_target_pairs={{0,4},{2,6},{4,0},{6,2},{8,12},{10,14},{12,8},{14,10},{16,20},{18,... | collective-permute-start | bytes 1327112 | tf_op jit(solution)/shard_map/ppermute | solution.py:397
  263.2 30.6 %collective-permute-start.29 = (bf16[128,1536]{1,0:T(8,128)(2,1)}, bf16[128,1536]{1,0:T(8,128)(2,1)S(1)}, u32[]{:S(2)}, u32[]{:S(2)}) collective-permute-start(bf16[128,1536]{1,0:T(8,128)(2,1)} %slice.387), channel_id=1, source_target_pairs={{0,2},{2,0},{4,6},{6,4},{8,10},{10,8},{12,14},{14,12},{16,18},{18,... | collective-permute-start | bytes 1179656 | tf_op jit(solution)/shard_map/ppermute | solution.py:397
  266.2 27.6 %collective-permute-start.30 = (bf16[128,1536]{1,0:T(8,128)(2,1)}, bf16[128,1536]{1,0:T(8,128)(2,1)S(1)}, u32[]{:S(2)}, u32[]{:S(2)}) collective-permute-start(bf16[128,1536]{1,0:T(8,128)(2,1)} %slice.388), channel_id=1, source_target_pairs={{0,8},{2,10},{4,12},{6,14},{8,0},{10,2},{12,4},{14,6},{16,24},{18,... | collective-permute-start | bytes 1179656 | tf_op jit(solution)/shard_map/ppermute | solution.py:397
  413.6 29.6 %collective-permute-start.46 = (bf16[2,2,96,1152]{3,2,1,0:T(8,128)(2,1)}, bf16[2,2,96,1152]{3,2,1,0:T(8,128)(2,1)}, u32[]{:S(2)}, u32[]{:S(2)}) collective-permute-start(bf16[2,2,96,1152]{3,2,1,0:T(8,128)(2,1)} %dynamic-slice_bitcast_fusion.2), channel_id=1, source_target_pairs={{0,16},{2,18},{4,20},{6,22},{8,24},{10,26},{12,28},{14,30},{16,0},... | collective-permute-start | bytes 2654216 | tf_op jit(solution)/shard_map/ppermute | solution.py:397
  415.5 27.7 %collective-permute-start.44 = (bf16[256,1536]{1,0:T(8,128)(2,1)}, bf16[256,1536]{1,0:T(8,128)(2,1)}, u32[]{:S(2)}, u32[]{:S(2)}) collective-permute-start(bf16[256,1536]{1,0:T(8,128)(2,1)} %pad_maximum_fusion.25), channel_id=1, source_target_pairs={{0,2},{2,0},{4,6},{6,4},{8,10},{10,8},{12,14},{14,12},{16,18},{18,... | collective-permute-start | bytes 2359304 | tf_op jit(solution)/shard_map/ppermute | solution.py:397
  493.6 27.4 %collective-permute-start.55 = (bf16[512,256]{1,0:T(8,128)(2,1)}, bf16[512,256]{1,0:T(8,128)(2,1)}, u32[]{:S(2)}, u32[]{:S(2)}) collective-permute-start(bf16[512,256]{1,0:T(8,128)(2,1)} %get-tuple-element.275), channel_id=1, source_target_pairs={{0,2},{2,0},{4,6},{6,4},{8,10},{10,8},{12,14},{14,12},{16,18},{18,... | collective-permute-start | bytes 786440 | tf_op jit(solution)/shard_map/ppermute | solution.py:397
  521.1 42.6 %collective-permute-start.60 = (bf16[2,96,1152]{2,1,0:T(8,128)(2,1)}, bf16[2,96,1152]{2,1,0:T(8,128)(2,1)}, u32[]{:S(2)}, u32[]{:S(2)}) collective-permute-start(bf16[2,96,1152]{2,1,0:T(8,128)(2,1)} %dynamic-slice_bitcast_fusion.13), channel_id=1, source_target_pairs={{0,4},{2,6},{4,0},{6,2},{8,12},{10,14},{12,8},{14,10},{16,20},{18,... | collective-permute-start | bytes 1327112 | tf_op jit(solution)/shard_map/ppermute | solution.py:397
  534.5 40.5 %collective-permute-start.61 = (bf16[256,1536]{1,0:T(8,128)(2,1)}, bf16[256,1536]{1,0:T(8,128)(2,1)}, u32[]{:S(2)}, u32[]{:S(2)}) collective-permute-start(bf16[256,1536]{1,0:T(8,128)(2,1)} %pad_maximum_fusion.27), channel_id=1, source_target_pairs={{0,2},{2,0},{4,6},{6,4},{8,10},{10,8},{12,14},{14,12},{16,18},{18,... | collective-permute-start | bytes 2359304 | tf_op jit(solution)/shard_map/ppermute | solution.py:397
  545.3 29.7 %all-to-all-start.4 = ((bf16[4,96,1152]{2,1,0:T(8,128)(2,1)}), bf16[4,96,1152]{2,1,0:T(8,128)(2,1)}, u32[]{:S(2)}, u32[]{:S(2)}) async-start(bf16[4,96,1152]{2,1,0:T(8,128)(2,1)} %bitcast.308), calls=%async_computation.4 | async-start | bytes 1769472 | tf_op jit(solution)/shard_map/all_to_all | solution.py:486
  578.7 30.8 %collective-permute-start.68 = (bf16[2,96,1152]{2,1,0:T(8,128)(2,1)S(1)}, bf16[2,96,1152]{2,1,0:T(8,128)(2,1)S(1)}, u32[]{:S(2)}, u32[]{:S(2)}) collective-permute-start(bf16[2,96,1152]{2,1,0:T(8,128)(2,1)S(1)} %dynamic-slice_bitcast_fusion.12), channel_id=1, source_target_pairs={{0,4},{2,6},{4,0},{6,2},{8,12},{10,14},{12,8},{14,10},{16,20},{18,... | collective-permute-start | bytes 1327112 | tf_op jit(solution)/shard_map/ppermute | solution.py:397
  579.1 30.5 %collective-permute-start.65 = (bf16[384,1536]{1,0:T(8,128)(2,1)S(1)}, bf16[384,1536]{1,0:T(8,128)(2,1)S(1)}, u32[]{:S(2)}, u32[]{:S(2)}) collective-permute-start(bf16[384,1536]{1,0:T(8,128)(2,1)S(1)} %pad_maximum_fusion.9), channel_id=1, source_target_pairs={{0,16},{2,18},{4,20},{6,22},{8,24},{10,26},{12,28},{14,30},{16,0},... | collective-permute-start | bytes 3538952 | tf_op jit(solution)/shard_map/ppermute | solution.py:397
  580.4 29.2 %collective-permute-start.64 = (bf16[384,1536]{1,0:T(8,128)(2,1)S(1)}, bf16[384,1536]{1,0:T(8,128)(2,1)S(1)}, u32[]{:S(2)}, u32[]{:S(2)}) collective-permute-start(bf16[384,1536]{1,0:T(8,128)(2,1)S(1)} %pad_maximum_fusion.8), channel_id=1, source_target_pairs={{0,8},{2,10},{4,12},{6,14},{8,0},{10,2},{12,4},{14,6},{16,24},{18,... | collective-permute-start | bytes 3538952 | tf_op jit(solution)/shard_map/ppermute | solution.py:397
  (166 other events, 1837.3 us)
Sparse Core Ops, SparseCore 0:
  18.3 85.5 all-gather.1
